TPU v7x, 32 devices: a whole 2x2x4 slice. The times are simulated.
32 devices in a mesh: dp: 16 (over z, x, core), tensor: 2 (over y).
Axes of the slice: x: 2, y: 2, z: 4, core: 2. Of those that a mesh axis runs over, the one named last changes fastest.
Arguments:
- block_input: bfloat16 [131072, 1024], P(('dp', 'tensor')), may hold values from -6 to 6
- output_cot: bfloat16 [131072, 1024], P(('dp', 'tensor')), may hold values from -6 to 6
- segment_ids: int32 [32, 4096], P('dp'), may hold values from 0 to 15, never falling along the last dimension, each value on 1 to 1024 neighbouring positions
- routed_index: int32 [32, 512], P('dp'), may hold values from 0 to 4095, as said below
- w_query: bfloat16 [1024, 1024], P('dp', 'tensor'), may hold values from -0.1875 to 0.1875
- w_key: bfloat16 [1024, 1024], P('dp', 'tensor'), may hold values from -0.1875 to 0.1875
- w_value: bfloat16 [1024, 1024], P('dp', 'tensor'), may hold values from -0.1875 to 0.1875
- w_output: bfloat16 [1024, 1024], P('dp', 'tensor'), may hold values from -0.75 to 0.75
- w_up: bfloat16 [1024, 4096], P('dp', 'tensor'), may hold values from -0.1875 to 0.1875
- w_down: bfloat16 [1024, 4096], P('dp', 'tensor'), may hold values from -0.09375 to 0.09375
- attn_gain: bfloat16 [1024], P('dp'), may hold values from 0.099609375 to 1.8984375
- mlp_gain: bfloat16 [1024], P('dp'), may hold values from 0.099609375 to 1.8984375
- router_w: bfloat16 [1024], P('dp'), may hold values from -0.1875 to 0.1875
Outputs:
- block_output: bfloat16 [131072, 1024], P(('dp', 'tensor'))
- block_grad: bfloat16 [131072, 1024], P(('dp', 'tensor'))
- grad_w_query: float32 [1024, 1024], P('dp', 'tensor')
- grad_w_key: float32 [1024, 1024], P('dp', 'tensor')
- grad_w_value: float32 [1024, 1024], P('dp', 'tensor')
- grad_w_output: float32 [1024, 1024], P('dp', 'tensor')
- grad_w_up: float32 [1024, 4096], P('dp', 'tensor')
- grad_w_down: float32 [1024, 4096], P('dp', 'tensor')
- grad_attn_gain: float32 [1024], P('dp')
- grad_mlp_gain: float32 [1024], P('dp')
- grad_router_w: float32 [1024], P('dp')
Inputs may be any that keep to these rules, and one draw needn't show every extreme that they name: `routed_index`: each row lists 512 different positions of its sequence in rising order, always 0 and 4095 among them.
All inputs are finite; a program needn't handle non-finite values.
Results may differ from a plain program's by a relative error of at most 0.011.
Values may be sent and summed in bfloat16 or wider, within the bound.
No kernel may reach another device: no remote copies, remote signals or barrier semaphores. Data moves between devices by JAX's collectives and lax.ppermute only.
A program may use at most 192 MiB of HBM per device.

v0:
```python
from functools import partial

import jax
import jax.numpy as jnp
from jax import lax
from jax.sharding import PartitionSpec as P

HEAD_DIM = 64


EPSILON = 1e-05
HIGH = lax.Precision.HIGHEST


def rms_norm(values, gain):
    scale = lax.rsqrt(jnp.mean(values * values, axis=-1, keepdims=True) + EPSILON)
    return values * scale * gain


def plain_dot(left, right):
    return jnp.dot(left, right, preferred_element_type=jnp.float32)


def contract_rows(left, right):
    return lax.dot_general(
        left, right, (((0,), (0,)), ((), ())), preferred_element_type=jnp.float32
    )


def contract_last(left, right):
    return lax.dot_general(
        left, right, (((1,), (1,)), ((), ())), preferred_element_type=jnp.float32
    )


def local(
    block_input,
    output_cot,
    segment_ids,
    routed_index,
    w_query,
    w_key,
    w_value,
    w_output,
    w_up,
    w_down,
    attn_gain,
    mlp_gain,
    router_w,
):
    tensor_rank = lax.axis_index("tensor")
    tensor_count = lax.axis_size("tensor")
    routed_rows = routed_index.shape[1]
    scale = HEAD_DIM ** (-0.5)
    own_index = lax.dynamic_index_in_dim(routed_index, tensor_rank, 0, keepdims=False)
    own_input = jnp.take(block_input, own_index, axis=0)
    input_float = own_input.astype(jnp.float32)
    gathered = (
        lax.all_gather(w_query, "dp", axis=0, tiled=True),
        lax.all_gather(w_key, "dp", axis=0, tiled=True),
        lax.all_gather(w_value, "dp", axis=0, tiled=True),
        lax.all_gather(w_output, "dp", axis=0, tiled=True),
        lax.all_gather(w_up, "dp", axis=0, tiled=True),
        lax.all_gather(w_down, "dp", axis=0, tiled=True),
        lax.all_gather(attn_gain, "dp", axis=0, tiled=True),
        lax.all_gather(mlp_gain, "dp", axis=0, tiled=True),
        lax.all_gather(router_w, "dp", axis=0, tiled=True),
    )
    (
        full_query,
        full_key,
        full_value,
        full_output,
        full_up,
        full_down,
        full_attn_gain,
        full_mlp_gain,
        full_router,
    ) = gathered
    attn_gain_f = full_attn_gain.astype(jnp.float32)
    mlp_gain_f = full_mlp_gain.astype(jnp.float32)
    router_f = full_router.astype(jnp.float32)
    local_heads = full_query.shape[1] // HEAD_DIM
    seg_routed = jnp.take_along_axis(segment_ids, routed_index, axis=1)
    allowed = (seg_routed[:, :, None] == seg_routed[:, None, :]) & (
        routed_index[:, None, :] <= routed_index[:, :, None]
    )
    allowed = allowed[:, None]

    def split_heads(values):
        return values.reshape(tensor_count, routed_rows, local_heads, HEAD_DIM)

    def merge_heads(values):
        return values.reshape(tensor_count * routed_rows, local_heads * HEAD_DIM)

    normed_attn = rms_norm(input_float, attn_gain_f).astype(jnp.bfloat16)
    normed_all = lax.all_gather(normed_attn, "tensor", axis=0, tiled=True)
    query = split_heads(plain_dot(normed_all, full_query).astype(jnp.bfloat16))
    keyed = split_heads(plain_dot(normed_all, full_key).astype(jnp.bfloat16))
    valued = split_heads(plain_dot(normed_all, full_value).astype(jnp.bfloat16))

    def make_scores():
        raw = (
            jnp.einsum("sqhd,skhd->shqk", query, keyed, preferred_element_type=jnp.float32) * scale
        )
        return jnp.where(allowed, raw, -1e30)

    scores = make_scores()
    row_max = jnp.max(scores, axis=-1, keepdims=True)
    expanded = jnp.exp(scores - row_max)
    row_total = jnp.sum(expanded, axis=-1, keepdims=True)
    probs = expanded / row_total
    log_total = row_max + jnp.log(row_total)
    probs_low = probs.astype(jnp.bfloat16)
    attended = merge_heads(
        jnp.einsum("shqk,skhd->sqhd", probs_low, valued, preferred_element_type=jnp.float32).astype(
            jnp.bfloat16
        )
    )
    branch_attn = lax.psum_scatter(
        contract_last(attended, full_output), "tensor", scatter_dimension=0, tiled=True
    )
    middle = input_float + branch_attn
    normed_mlp = rms_norm(middle, mlp_gain_f).astype(jnp.bfloat16)
    mlp_all = lax.all_gather(normed_mlp, "tensor", axis=0, tiled=True)
    hidden_pre = plain_dot(mlp_all, full_up)
    hidden_act = jax.nn.gelu(hidden_pre, approximate=True).astype(jnp.bfloat16)
    branch_mlp = lax.psum_scatter(
        contract_last(hidden_act, full_down).astype(jnp.bfloat16),
        "tensor",
        scatter_dimension=0,
        tiled=True,
    ).astype(jnp.float32)
    branch_total = branch_attn + branch_mlp
    gate = jax.nn.sigmoid(plain_dot(own_input, full_router))
    updated = input_float + gate[:, None] * branch_total
    block_output = block_input.at[own_index].set(updated.astype(jnp.bfloat16))
    cot_rows = jnp.take(output_cot, own_index, axis=0).astype(jnp.float32)
    d_branch = gate[:, None] * cot_rows
    d_logit = gate * (1.0 - gate) * jnp.sum(cot_rows * branch_total, axis=-1)
    d_mlp_all = lax.all_gather(d_branch.astype(jnp.bfloat16), "tensor", axis=0, tiled=True)
    d_act = plain_dot(d_mlp_all, full_down)
    unused_act, gelu_back = jax.vjp(partial(jax.nn.gelu, approximate=True), hidden_pre)
    d_pre = gelu_back(d_act)[0].astype(jnp.bfloat16)
    grad_down = contract_rows(d_mlp_all, hidden_act)
    grad_up = contract_rows(mlp_all, d_pre)
    d_normed_mlp = lax.psum_scatter(
        contract_last(d_pre, full_up), "tensor", scatter_dimension=0, tiled=True
    )
    unused_mid, norm_back_mlp = jax.vjp(rms_norm, middle, mlp_gain_f)
    d_middle, d_mlp_gain = norm_back_mlp(d_normed_mlp)
    d_attn_all = lax.all_gather(
        (d_branch + d_middle).astype(jnp.bfloat16), "tensor", axis=0, tiled=True
    )
    d_attended_flat = plain_dot(d_attn_all, full_output).astype(jnp.bfloat16)
    grad_output = contract_rows(d_attn_all, attended)
    d_attended = split_heads(d_attended_flat)
    scores_again = make_scores()
    probs_again = jnp.exp(scores_again - log_total)
    probs_again_low = probs_again.astype(jnp.bfloat16)
    d_probs = jnp.einsum("sqhd,skhd->shqk", d_attended, valued, preferred_element_type=jnp.float32)
    row_inner = jnp.sum(probs_again * d_probs, axis=-1, keepdims=True)
    d_scores = (probs_again * (d_probs - row_inner)).astype(jnp.bfloat16)
    d_query = merge_heads(
        (
            jnp.einsum("shqk,skhd->sqhd", d_scores, keyed, preferred_element_type=jnp.float32)
            * scale
        ).astype(jnp.bfloat16)
    )
    d_key = merge_heads(
        (
            jnp.einsum("shqk,sqhd->skhd", d_scores, query, preferred_element_type=jnp.float32)
            * scale
        ).astype(jnp.bfloat16)
    )
    d_value = merge_heads(
        jnp.einsum(
            "shqk,sqhd->skhd", probs_again_low, d_attended, preferred_element_type=jnp.float32
        ).astype(jnp.bfloat16)
    )
    grad_query = contract_rows(normed_all, d_query)
    grad_key = contract_rows(normed_all, d_key)
    grad_value = contract_rows(normed_all, d_value)
    part_query = contract_last(d_query, full_query)
    part_key = contract_last(d_key, full_key)
    part_value = contract_last(d_value, full_value)
    d_normed_attn = lax.psum_scatter(
        (part_query + part_key + part_value).astype(jnp.bfloat16),
        "tensor",
        scatter_dimension=0,
        tiled=True,
    ).astype(jnp.float32)
    unused_norm, norm_back_attn = jax.vjp(rms_norm, input_float, attn_gain_f)
    d_input_norm, d_attn_gain = norm_back_attn(d_normed_attn)
    d_router = jnp.dot(d_logit, input_float, precision=HIGH, preferred_element_type=jnp.float32)
    gain_totals = lax.psum((d_attn_gain, d_mlp_gain, d_router), "tensor")
    routed_grad = cot_rows + d_logit[:, None] * router_f + d_middle + d_input_norm
    block_grad = output_cot.at[own_index].set(routed_grad.astype(jnp.bfloat16))
    sums = (
        lax.psum_scatter(grad_query, "dp", scatter_dimension=0, tiled=True),
        lax.psum_scatter(grad_key, "dp", scatter_dimension=0, tiled=True),
        lax.psum_scatter(grad_value, "dp", scatter_dimension=0, tiled=True),
        lax.psum_scatter(grad_output, "dp", scatter_dimension=0, tiled=True),
        lax.psum_scatter(grad_up, "dp", scatter_dimension=0, tiled=True),
        lax.psum_scatter(grad_down, "dp", scatter_dimension=0, tiled=True),
        lax.psum_scatter(gain_totals[0], "dp", scatter_dimension=0, tiled=True),
        lax.psum_scatter(gain_totals[1], "dp", scatter_dimension=0, tiled=True),
        lax.psum_scatter(gain_totals[2], "dp", scatter_dimension=0, tiled=True),
    )
    return (
        block_output,
        block_grad,
        sums[0],
        sums[1],
        sums[2],
        sums[3],
        sums[4],
        sums[5],
        sums[6],
        sums[7],
        sums[8],
    )


def solution(mesh):
    in_specs = (
        P(("dp", "tensor"), None),
        P(("dp", "tensor"), None),
        P("dp", None),
        P("dp", None),
        P("dp", "tensor"),
        P("dp", "tensor"),
        P("dp", "tensor"),
        P("dp", "tensor"),
        P("dp", "tensor"),
        P("dp", "tensor"),
        P("dp"),
        P("dp"),
        P("dp"),
    )
    out_specs = (
        P(("dp", "tensor"), None),
        P(("dp", "tensor"), None),
        P("dp", "tensor"),
        P("dp", "tensor"),
        P("dp", "tensor"),
        P("dp", "tensor"),
        P("dp", "tensor"),
        P("dp", "tensor"),
        P("dp"),
        P("dp"),
        P("dp"),
    )
    return jax.shard_map(local, mesh=mesh, in_specs=in_specs, out_specs=out_specs, check_vma=False)
```

profile of v0, /device:TPU:0, one launch (start us, length us, event | category | flops | bytes accessed | tf_op | source)
XLA Modules:
  0.0 1174.2 jit_solution(12379312300727711675)
XLA Ops:
  7.2 7.8 copy.100
  15.0 7.8 copy.101
  24.9 35.6 %all-reduce.8 = (bf16[1024]{0:T(1024)(128)(2,1)S(1)}, bf16[1024]{0:T(1024)(128)(2,1)S(1)}, bf16[1024]{0:T(1024)(128)(2,1)S(1)}) all-reduce(bf16[1024]{0:T(1024)(128)(2,1)S(1)} %dynamic-update-slice.1, bf16[1024]{0:T(1024)(128)(2,1)S(1)} %dynamic-update-slice.2, ...), channel_id=1, replica_groups=mesh['dp'=16,'tensor'=2] {'dp'}, use_global_device_ids=true, to_apply=%add.1 | all-reduce | flops 3072 | bytes 12288
  61.1 7.2 gather_fusion.1
  72.4 9.1 gather_fusion
  82.9 17.9 %all-gather.11.cloned.1.call-done = bf16[1024,1024]{1,0:T(8,128)(2,1)} async-done(((bf16[512,1024]{1,0:T(8,128)(2,1)}), bf16[1024,1024]{1,0:T(8,128)(2,1)}) %all-gather.11.cloned.1.call-update) | async-done | bytes 2097168 | tf_op jit(solution)/shard_map/all_gather | solution.py:97
  100.8 3.1 convolution_convert_fusion.2
  103.9 2.1 reshape.236
  105.9 2.5 copy.60
  108.5 32.3 %all-gather.15.cloned.1.call-done = bf16[1024,512]{1,0:T(8,128)(2,1)} async-done(((bf16[64,512]{1,0:T(8,128)(2,1)}), bf16[1024,512]{1,0:T(8,128)(2,1)}) %all-gather.15.cloned.1.call-update) | async-done | bytes 1048592 | tf_op jit(solution)/shard_map/all_gather | solution.py:59
  140.8 3.1 convolution_convert_fusion.3
  143.9 2.1 reshape.235
  146.0 2.5 copy.59
  148.5 31.2 %all-gather.13.cloned.1.call-done = bf16[1024,512]{1,0:T(8,128)(2,1)} async-done(((bf16[64,512]{1,0:T(8,128)(2,1)}), bf16[1024,512]{1,0:T(8,128)(2,1)}) %all-gather.13.cloned.1.call-update) | async-done | bytes 1048592 | tf_op jit(solution)/shard_map/all_gather | solution.py:61
  179.7 4.0 convolution_convert_fusion.4
  183.7 3.9 reshape.234
  187.6 3.3 copy.61
  190.9 8.4 fusion.55
  199.3 8.5 fusion
  207.8 8.0 fusion.36
  217.2 1.3 all-gather.19.cloned.1.call-done
  218.5 4.5 fusion.56
  223.9 7.9 gather_fusion.2
  232.2 44.3 %reduce-scatter.11.cloned.1.call-done = f32[512,1024]{1,0:T(8,128)} async-done(((f32[1024,1024]{1,0:T(8,128)}), f32[512,1024]{1,0:T(8,128)}) %reduce-scatter.11.cloned.1.call-update) | async-done | bytes 2097168 | tf_op jit(solution)/shard_map/reduce_scatter | solution.py:120
  276.5 3.7 fusion.15
  281.1 1.4 multiply_convert_fusion.4
  282.6 46.6 %all-gather.25.cloned.1.call-done = bf16[1024,2048]{1,0:T(8,128)(2,1)} async-done(((bf16[64,2048]{1,0:T(8,128)(2,1)}), bf16[1024,2048]{1,0:T(8,128)(2,1)}) %all-gather.25.cloned.1.call-update) | async-done | bytes 4194320 | tf_op jit(solution)/shard_map/all_gather | solution.py:64
  329.1 33.2 %all-gather.27.cloned.1.call-done = bf16[1024,1024]{1,0:T(8,128)(2,1)} async-done(((bf16[512,1024]{1,0:T(8,128)(2,1)}), bf16[1024,1024]{1,0:T(8,128)(2,1)}) %all-gather.27.cloned.1.call-update) | async-done | bytes 2097168 | tf_op jit(solution)/shard_map/all_gather | solution.py:141
  362.3 10.6 fusion.57
  372.9 42.0 %all-gather.23.cloned.1.call-done = bf16[1024,2048]{1,0:T(8,128)(2,1)} async-done(((bf16[64,2048]{1,0:T(8,128)(2,1)}), bf16[1024,2048]{1,0:T(8,128)(2,1)}) %all-gather.23.cloned.1.call-update) | async-done | bytes 4194320 | tf_op jit(solution)/shard_map/all_gather | solution.py:63
  414.9 33.1 %all-gather.21.cloned.1.call-done = bf16[1024,1024]{1,0:T(8,128)(2,1)} async-done(((bf16[512,1024]{1,0:T(8,128)(2,1)}), bf16[1024,1024]{1,0:T(8,128)(2,1)}) %all-gather.21.cloned.1.call-update) | async-done | bytes 2097168 | tf_op jit(solution)/shard_map/all_gather | solution.py:125
  448.0 14.2 %fusion.8 = (bf16[1024,2048]{1,0:T(8,128)(2,1)}, f32[1024,2048]{1,0:T(8,128)S(1)}) fusion(f32[1024,2048]{1,0:T(8,128)} %fusion.57, bf16[1024,1024]{1,0:T(8,128)(2,1)} %all-gather.21.cloned.1.call-done, bf16[1024,2048]{1,0:T(8,128)(2,1)} %all-gather.23.cloned.1.call-done), kind=kOutput, calls=%fused_computation.21 | convolution fusion | flops 4336910336 | bytes 27262976 | tf_op jit(solution)/shard_map/dot_general | solution.py:21
  462.2 3.3 copy-done.33
  465.4 6.4 convolution_convert_fusion
  471.9 10.0 fusion.58
  482.0 22.0 %reduce-scatter.13.cloned.1.call-done = bf16[512,1024]{1,0:T(8,128)(2,1)} async-done(((bf16[1024,1024]{1,0:T(8,128)(2,1)}), bf16[512,1024]{1,0:T(8,128)(2,1)}) %reduce-scatter.13.cloned.1.call-update) | async-done | bytes 1048592 | tf_op jit(solution)/shard_map/reduce_scatter | solution.py:128
  503.9 56.6 %reduce-scatter.15.cloned.1.call-done = f32[512,1024]{1,0:T(8,128)} async-done(((f32[1024,1024]{1,0:T(8,128)}), f32[512,1024]{1,0:T(8,128)}) %reduce-scatter.15.cloned.1.call-update) | async-done | bytes 2097168 | tf_op jit(solution)/shard_map/reduce_scatter | solution.py:147
  560.5 3.5 multiply_reduce_fusion.1
  564.1 2.0 fusion.18
  566.3 33.0 %all-gather.29.cloned.1.call-done = bf16[1024,1024]{1,0:T(8,128)(2,1)} async-done(((bf16[512,1024]{1,0:T(8,128)(2,1)}), bf16[1024,1024]{1,0:T(8,128)(2,1)}) %all-gather.29.cloned.1.call-update) | async-done | bytes 2097168 | tf_op jit(solution)/shard_map/all_gather | solution.py:152
  599.3 3.1 convolution_convert_fusion.1
  603.5 1.4 copy.65
  605.9 9.6 fusion.33
  615.5 13.6 %multiply_reduce_fusion = (f32[2,8,512]{2,1,0:T(8,128)S(1)}, f32[2,8,512,512]{2,3,1,0:T(8,128)}) fusion(f32[2,8,512,512]{2,3,1,0:T(8,128)} %get-tuple-element.33, f32[2,8,512]{2,1,0:T(8,128)S(1)} %log_add_fusion, bf16[2,512,8,64]{1,3,2,0:T(8,128)(2,1)} %copy-done.12, bf16[2,512,8,64]{1,3,2,0:T(8,128)(2,1)} %copy.61), kind=kOutput, calls=%fused_computation.6 | convolution fusion | flops 549445632 | bytes 35717120 | tf_op jit(solution)/shard_map/sqhd,skhd->shqk/dot_general | solution.py:161
  629.6 10.8 multiply_convert_fusion
  640.4 6.5 fusion.32
  646.9 1.5 fusion.31
  655.4 2.7 add_convert_fusion
  658.3 10.7 fusion.65
  669.1 12.0 %fusion.51 = f32[1024,2048]{1,0:T(8,128)} fusion(bf16[1024,1024]{1,0:T(8,128)(2,1)} %all-gather.27.cloned.1.call-done, f32[1024,2048]{1,0:T(8,128)} %copy-done.33), kind=kOutput, calls=%fused_computation.102 | convolution fusion | flops 4313841664 | bytes 18874368 | tf_op jit(solution)/shard_map/dot_general | solution.py:25
  682.3 4.2 fusion.64
  686.6 4.3 fusion.63
  691.2 4.2 fusion.61
  695.5 4.7 fusion.62
  700.9 13.2 %scatter_custom_fusion = bf16[4096,1024]{1,0:T(8,128)(2,1)} fusion(bf16[4096,1024]{1,0:T(8,128)(2,1)} %copy.100, s32[512]{0:T(512)} %bitcast.114, f32[512,1024]{1,0:T(8,128)S(1)} %copy-done.6, bf16[512,1024]{1,0:T(8,128)(2,1)} %reduce-scatter.13.cloned.1.call-done, f32[512]{0:T(512)S(1)} %add_divide_fusion, bf16[512,1024]{1,0:T(8,128)(2,1)S(1)} %copy-done.4, ...), kind=kCustom, calls=%fused_computation.73 | custom fusion | flops 3670016 | bytes 12585472 | tf_op jit(solution)/shard_map/scatter | solution.py:137
  714.7 2.3 fusion.19
  717.0 63.9 %all-reduce.6 = (f32[1024]{0:T(1024)S(1)}, f32[1024]{0:T(1024)S(1)}, f32[1024]{0:T(1024)S(1)}) all-reduce(f32[1024]{0:T(1024)S(1)} %get-tuple-element.15, f32[1024]{0:T(1024)S(1)} %get-tuple-element.12, f32[1024]{0:T(1024)S(1)} %bitcast.113), channel_id=12, replica_groups=mesh['dp'=16,'tensor'=2] {'dp'}, use_global_device_ids=true, to_apply=%region_22.24.clone | all-reduce | flops 3072 | bytes 24576
  781.2 13.9 %scatter_custom_fusion.1 = bf16[4096,1024]{1,0:T(8,128)(2,1)} fusion(bf16[4096,1024]{1,0:T(8,128)(2,1)} %copy.101, s32[512]{0:T(512)} %bitcast.115, bf16[512,1024]{1,0:T(8,128)(2,1)} %reduce-scatter.17.cloned.1.call-done, f32[512]{0:T(512)S(1)} %multiply_multiply_fusion.2, f32[1024]{0:T(1024)S(1)} %convert_element_type.112, f32[512]{0:T(512)S(1)} %fusion.48, ...), kind=kCustom, calls=%fused_computation.74 | custom fusion | flops 11010048 | bytes 15751680 | tf_op jit(solution)/shard_map/scatter | solution.py:198
  795.1 5.4 all-reduce.7
  800.5 105.9 %reduce-scatter.29.cloned.1.call-done = f32[64,2048]{1,0:T(8,128)} async-done(((f32[1024,2048]{1,0:T(8,128)}), f32[64,2048]{1,0:T(8,128)}) %reduce-scatter.29.cloned.1.call-update) | async-done | bytes 524304 | tf_op jit(solution)/shard_map/reduce_scatter | solution.py:205
  906.4 65.6 %reduce-scatter.25.cloned.1.call-done = f32[64,512]{1,0:T(8,128)} async-done(((f32[1024,512]{1,0:T(8,128)}), f32[64,512]{1,0:T(8,128)}) %reduce-scatter.25.cloned.1.call-update) | async-done | bytes 131088 | tf_op jit(solution)/shard_map/reduce_scatter | solution.py:203
  972.0 64.9 %reduce-scatter.23.cloned.1.call-done = f32[64,512]{1,0:T(8,128)} async-done(((f32[1024,512]{1,0:T(8,128)}), f32[64,512]{1,0:T(8,128)}) %reduce-scatter.23.cloned.1.call-update) | async-done | bytes 131088 | tf_op jit(solution)/shard_map/reduce_scatter | solution.py:202
  1036.9 65.1 %reduce-scatter.19.cloned.1.call-done = f32[64,512]{1,0:T(8,128)} async-done(((f32[1024,512]{1,0:T(8,128)}), f32[64,512]{1,0:T(8,128)}) %reduce-scatter.19.cloned.1.call-update) | async-done | bytes 131088 | tf_op jit(solution)/shard_map/reduce_scatter | solution.py:200
  1102.0 64.9 %reduce-scatter.21.cloned.1.call-done = f32[64,512]{1,0:T(8,128)} async-done(((f32[1024,512]{1,0:T(8,128)}), f32[64,512]{1,0:T(8,128)}) %reduce-scatter.21.cloned.1.call-update) | async-done | bytes 131088 | tf_op jit(solution)/shard_map/reduce_scatter | solution.py:201
  (164 shorter events, 23.3 us)
Async XLA Ops:
  7.2 65.3 %copy-start = (s32[2,4096]{1,0:T(2,128)S(1)}, s32[2,4096]{1,0:T(2,128)}, u32[]{:S(2)}) copy-start(s32[2,4096]{1,0:T(2,128)} %param.17) | copy-start | bytes 98308
  7.2 75.7 %all-gather.17.cloned.1.call-start = ((), (), s32[]{:S(2)}) async-start(), calls=%async_computation.13 | async-start | bytes 1114112 | tf_op jit(solution)/shard_map/all_gather | solution.py:60
  15.0 7.9 copy-start.26
  15.0 9.2 copy-start.30
  15.0 9.4 copy-start.31
  15.0 9.7 copy-start.32
  15.0 45.5 %copy-start.19 = (s32[2,512]{1,0:T(2,128)S(1)}, s32[2,512]{1,0:T(2,128)}, u32[]{:S(2)}) copy-start(s32[2,512]{1,0:T(2,128)} %param.18) | copy-start | bytes 12292
  22.9 77.9 %all-gather.11.cloned.1.call-start = ((), (), s32[]{:S(2)}) async-start(), calls=%async_computation.10 | async-start | bytes 3145728 | tf_op jit(solution)/shard_map/all_gather | solution.py:97
  60.5 8.4 copy-start.20
  68.4 495.6 %copy-start.3 = (bf16[512,1024]{1,0:T(8,128)(2,1)}, bf16[512,1024]{1,0:T(8,128)(2,1)S(1)}, u32[]{:S(2)}) copy-start(bf16[512,1024]{1,0:T(8,128)(2,1)S(1)} %gather_fusion.1) | copy-start | bytes 3145732
  68.9 14.0 %copy-start.24 = (f32[512]{0:T(512)}, f32[512]{0:T(512)S(1)}, u32[]{:S(2)}) copy-start(f32[512]{0:T(512)S(1)} %fusion.24) | copy-start | bytes 6148
  68.9 14.0 %copy-start.22 = (f32[512]{0:T(512)}, f32[512]{0:T(512)S(1)}, u32[]{:S(2)}) copy-start(f32[512]{0:T(512)S(1)} %fusion.49) | copy-start | bytes 6148
  70.2 70.5 %all-gather.15.cloned.1.call-start = ((), (), s32[]{:S(2)}) async-start(), calls=%async_computation.12 | async-start | bytes 1114112 | tf_op jit(solution)/shard_map/all_gather | solution.py:59
  71.0 108.7 %all-gather.13.cloned.1.call-start = ((), (), s32[]{:S(2)}) async-start(), calls=%async_computation.11 | async-start | bytes 1114112 | tf_op jit(solution)/shard_map/all_gather | solution.py:61
  71.6 146.9 %all-gather.19.cloned.1.call-start = ((), (), s32[]{:S(2)}) async-start(), calls=%async_computation.14 | async-start | bytes 1114112 | tf_op jit(solution)/shard_map/all_gather | solution.py:62
  72.1 204.4 %reduce-scatter.11.cloned.1.call-start = ((), (), s32[]{:S(2)}) async-start(), calls=%async_computation.15 | async-start | bytes 6291456 | tf_op jit(solution)/shard_map/reduce_scatter | solution.py:120
  108.5 82.5 %copy-start.9 = (bf16[2,512,8,64]{1,3,2,0:T(8,128)(2,1)}, bf16[2,512,8,64]{1,3,2,0:T(8,128)(2,1)S(1)}, u32[]{:S(2)}) copy-start(bf16[2,512,8,64]{1,3,2,0:T(8,128)(2,1)S(1)} %copy.60) | copy-start | bytes 3145732
  148.5 42.4 %copy-start.11 = (bf16[2,512,8,64]{1,3,2,0:T(8,128)(2,1)}, bf16[2,512,8,64]{1,3,2,0:T(8,128)(2,1)S(1)}, u32[]{:S(2)}) copy-start(bf16[2,512,8,64]{1,3,2,0:T(8,128)(2,1)S(1)} %copy.59) | copy-start | bytes 3145732
  199.3 8.5 copy-start.13
  217.2 5.9 copy-start.16
  223.0 106.1 %all-gather.25.cloned.1.call-start = ((), (), s32[]{:S(2)}) async-start(), calls=%async_computation.18 | async-start | bytes 4456448 | tf_op jit(solution)/shard_map/all_gather | solution.py:64
  223.8 138.5 %all-gather.27.cloned.1.call-start = ((), (), s32[]{:S(2)}) async-start(), calls=%async_computation.20 | async-start | bytes 3145728 | tf_op jit(solution)/shard_map/all_gather | solution.py:141
  276.5 4.5 copy-start.5
  280.3 134.7 %all-gather.23.cloned.1.call-start = ((), (), s32[]{:S(2)}) async-start(), calls=%async_computation.17 | async-start | bytes 4456448 | tf_op jit(solution)/shard_map/all_gather | solution.py:63
  281.0 167.0 %all-gather.21.cloned.1.call-start = ((), (), s32[]{:S(2)}) async-start(), calls=%async_computation.16 | async-start | bytes 3145728 | tf_op jit(solution)/shard_map/all_gather | solution.py:125
  282.5 221.4 %reduce-scatter.13.cloned.1.call-start = ((), (), s32[]{:S(2)}) async-start(), calls=%async_computation.19 | async-start | bytes 3145728 | tf_op jit(solution)/shard_map/reduce_scatter | solution.py:128
  448.0 17.5 %copy-start.27 = (bf16[1024,2048]{1,0:T(8,128)(2,1)S(1)}, bf16[1024,2048]{1,0:T(8,128)(2,1)}, u32[]{:S(2)}) copy-start(bf16[1024,2048]{1,0:T(8,128)(2,1)} %all-gather.25.cloned.1.call-done) | copy-start | bytes 12582916
  462.2 3.3 copy-start.33
  471.9 88.6 %reduce-scatter.15.cloned.1.call-start = ((), (), s32[]{:S(2)}) async-start(), calls=%async_computation.21 | async-start | bytes 6291456 | tf_op jit(solution)/shard_map/reduce_scatter | solution.py:147
  481.9 117.4 %all-gather.29.cloned.1.call-start = ((), (), s32[]{:S(2)}) async-start(), calls=%async_computation.22 | async-start | bytes 3145728 | tf_op jit(solution)/shard_map/all_gather | solution.py:152
  560.5 3.5 copy-start.7
  560.5 3.6 copy-start.8
  566.0 148.7 %reduce-scatter.17.cloned.1.call-start = ((), (), s32[]{:S(2)}) async-start(), calls=%async_computation.23 | async-start | bytes 3145728 | tf_op jit(solution)/shard_map/reduce_scatter | solution.py:187
  605.0 1.0 copy-start.12
  605.9 23.2 %slice-start = ((s8[16777216]{0:T(1024)(128)(4,1)}), s8[4194304]{0:T(1024)(128)(4,1)S(1)}, s32[]{:S(2)}) async-start(s8[16777216]{0:T(1024)(128)(4,1)} %bitcast.93), calls=%async_computation.30 | async-start | bytes 8388608
  605.9 23.2 %slice-start.1 = ((s8[16777216]{0:T(1024)(128)(4,1)}), s8[4194304]{0:T(1024)(128)(4,1)S(1)}, s32[]{:S(2)}) async-start(s8[16777216]{0:T(1024)(128)(4,1)} %bitcast.93), calls=%async_computation.31 | async-start | bytes 8388608
  615.5 13.6 %slice-start.2 = ((s8[16777216]{0:T(1024)(128)(4,1)}), s8[4194304]{0:T(1024)(128)(4,1)S(1)}, s32[]{:S(2)}) async-start(s8[16777216]{0:T(1024)(128)(4,1)} %bitcast.93), calls=%async_computation.32 | async-start | bytes 8388608
  615.5 14.0 %slice-start.3 = ((s8[16777216]{0:T(1024)(128)(4,1)}), s8[4194304]{0:T(1024)(128)(4,1)S(1)}, s32[]{:S(2)}) async-start(s8[16777216]{0:T(1024)(128)(4,1)} %bitcast.93), calls=%async_computation.33 | async-start | bytes 8388608
  640.4 6.5 copy-start.2
  640.4 6.5 copy-start.10
  646.9 1.5 copy-start.14
  649.7 2.7 copy-start.29
  652.4 1.3 copy-start.18
  652.4 1.6 copy-start.28
  654.0 1.3 copy-start.15
  658.1 142.4 %reduce-scatter.27.cloned.1.call-start = ((), (), s32[]{:S(2)}) async-start(), calls=%async_computation.28 | async-start | bytes 8912896 | tf_op jit(solution)/shard_map/reduce_scatter | solution.py:204
  669.0 237.4 %reduce-scatter.29.cloned.1.call-start = ((), (), s32[]{:S(2)}) async-start(), calls=%async_computation.29 | async-start | bytes 8912896 | tf_op jit(solution)/shard_map/reduce_scatter | solution.py:205
  681.1 1.2 copy-start.17
  681.1 290.9 %reduce-scatter.25.cloned.1.call-start = ((), (), s32[]{:S(2)}) async-start(), calls=%async_computation.27 | async-start | bytes 2228224 | tf_op jit(solution)/shard_map/reduce_scatter | solution.py:203
  686.5 350.4 %reduce-scatter.23.cloned.1.call-start = ((), (), s32[]{:S(2)}) async-start(), calls=%async_computation.26 | async-start | bytes 2228224 | tf_op jit(solution)/shard_map/reduce_scatter | solution.py:202
  690.9 411.1 %reduce-scatter.19.cloned.1.call-start = ((), (), s32[]{:S(2)}) async-start(), calls=%async_computation.24 | async-start | bytes 2228224 | tf_op jit(solution)/shard_map/reduce_scatter | solution.py:200
  695.4 5.4 copy-start.4
  695.4 5.4 copy-start.6
  695.4 471.4 %reduce-scatter.21.cloned.1.call-start = ((), (), s32[]{:S(2)}) async-start(), calls=%async_computation.25 | async-start | bytes 2228224 | tf_op jit(solution)/shard_map/reduce_scatter | solution.py:201
  700.9 13.9 %copy-start.21 = (f32[1024]{0:T(1024)S(1)}, f32[1024]{0:T(1024)}, u32[]{:S(2)}) copy-start(f32[1024]{0:T(1024)} %copy-done.20) | copy-start | bytes 12292
  700.9 13.9 %copy-start.23 = (f32[512]{0:T(512)S(1)}, f32[512]{0:T(512)}, u32[]{:S(2)}) copy-start(f32[512]{0:T(512)} %copy-done.22) | copy-start | bytes 6148
  700.9 80.3 %copy-start.25 = (f32[512]{0:T(512)S(1)}, f32[512]{0:T(512)}, u32[]{:S(2)}) copy-start(f32[512]{0:T(512)} %copy-done.24) | copy-start | bytes 6148
  781.1 385.7 %copy-start.1 = (s32[2,4096]{1,0:T(2,128)S(1)}, s32[2,4096]{1,0:T(2,128)}, u32[]{:S(2)}) copy-start(s32[2,4096]{1,0:T(2,128)} %param.17) | copy-start | bytes 98308
Sparse Core Ops, SparseCore 0:
  23.0 40.6 all-gather.16
  70.4 30.3 all-gather.10
  102.9 37.8 all-gather.14
  142.8 36.8 all-gather.12
  181.7 36.8 all-gather.18
  223.2 53.3 reduce-scatter.10
  278.7 50.3 all-gather.24
  330.7 31.6 all-gather.26
  364.5 50.3 all-gather.22
  416.3 31.6 all-gather.20
  472.0 31.8 reduce-scatter.12
  506.1 54.3 reduce-scatter.14
  566.2 33.0 all-gather.28
  658.2 31.8 reduce-scatter.16
  694.6 104.0 reduce-scatter.26
  803.3 103.0 reduce-scatter.28
  910.5 61.3 reduce-scatter.24
  976.1 60.7 reduce-scatter.22
  1041.2 60.7 reduce-scatter.18
  1106.2 60.6 reduce-scatter.20
where the time goes:
time: 1180 us; the launch traced here: 1170 us
  waiting for transfers between devices  763 us (65%)
  matrix products  153 us (13%)
  blocking collectives  105 us (9%)
  local copies, waits for them, and re-layouts  71.8 us (6%)
  other arithmetic  63.1 us (5%)
  between operations  16.7 us (1%)
    reduce_scatter x1, waiting for transfers between devices, local(): lax.psum_scatter(grad_down, 'dp', scatter_dimension=0, tiled=True)  106 us
    unnamed x2, blocking collectives  99.5 us
    reduce_scatter x1, waiting for transfers between devices, local(): lax.psum_scatter(grad_output, 'dp', scatter_dimension=0, tiled=True)  65.6 us
    reduce_scatter x1, waiting for transfers between devices, local(): lax.psum_scatter(grad_query, 'dp', scatter_dimension=0, tiled=True)  65.1 us
    reduce_scatter x1, waiting for transfers between devices, local(): lax.psum_scatter(grad_value, 'dp', scatter_dimension=0, tiled=True)  64.9 us
    reduce_scatter x1, waiting for transfers between devices, local(): lax.psum_scatter(grad_key, 'dp', scatter_dimension=0, tiled=True)  64.9 us
    reduce_scatter x1, waiting for transfers between devices, local(): lax.psum_scatter(contract_last(d_pre, full_up), 'tensor', scatter_dimensi...  56.6 us
    all_gather x1, waiting for transfers between devices, local(): lax.all_gather(w_down, 'dp', axis=0, tiled=True)  46.6 us
  transfers between devices with their start and end apart: 20, of which 17 were waited for; matrix products, arithmetic and copies ran while one was open for 15% of the time, Pallas kernels for 0%

commit v1 on v0

v1 whole, which is shorter than its diff:
```python
from functools import partial

import jax
import jax.numpy as jnp
from jax import lax
from jax.experimental import pallas as pl
from jax.experimental.pallas import tpu as pltpu
from jax.sharding import Mesh
from jax.sharding import PartitionSpec as P

HEAD_DIM = 64
EPSILON = 1e-05
DOCS = 16
PAIR = 2 * HEAD_DIM
DP = ("chips", "core")
ALL = ("tensor", "chips", "core")
SAME_CORE = ("tensor", "chips")


def rms_norm(values, gain):
    scale = lax.rsqrt(jnp.mean(values * values, axis=-1, keepdims=True) + EPSILON)
    return values * scale * gain


def plain_dot(left, right):
    return jnp.dot(left, right, preferred_element_type=jnp.float32)


def contract_rows(left, right):
    return lax.dot_general(
        left, right, (((0,), (0,)), ((), ())), preferred_element_type=jnp.float32
    )


def contract_last(left, right):
    return lax.dot_general(
        left, right, (((1,), (1,)), ((), ())), preferred_element_type=jnp.float32
    )


def fill_bias(seg_row_ref, seg_column_ref, bias_ref):
    rows = bias_ref.shape[0]
    key_at = lax.broadcasted_iota(jnp.int32, (rows, rows), 0)
    query_at = lax.broadcasted_iota(jnp.int32, (rows, rows), 1)
    same = seg_column_ref[...] == seg_row_ref[...]
    bias_ref[...] = jnp.where(same & (key_at <= query_at), 0.0, -1e30)


def lanes_of(head):
    lane = lax.broadcasted_iota(jnp.int32, (1, PAIR), 1)
    return (lane // HEAD_DIM == head).astype(jnp.bfloat16)


def attend(qkv, seg_row, seg_column):
    rows, width = qkv.shape[0], qkv.shape[1] // 3
    pairs = width // PAIR
    scale = HEAD_DIM ** (-0.5)

    def kernel(seg_row_ref, seg_column_ref, q_ref, k_ref, v_ref, out_ref, lse_ref, bias_ref):
        @pl.when(pl.program_id(0) == 0)
        def _():
            fill_bias(seg_row_ref, seg_column_ref, bias_ref)

        query, keyed, valued = q_ref[...], k_ref[...], v_ref[...]
        found = []
        for head in (0, 1):
            chosen = query * (lanes_of(head) * scale).astype(jnp.bfloat16)
            scores = contract_last(keyed, chosen) + bias_ref[...]
            top = jnp.max(scores, axis=0, keepdims=True)
            expanded = jnp.exp(scores - top)
            total = jnp.sum(expanded, axis=0, keepdims=True)
            lse_ref[head, :, :] = top + jnp.log(total)
            probs = (expanded * (1.0 / total)).astype(jnp.bfloat16)
            found.append(contract_rows(probs, valued))
        lane = lax.broadcasted_iota(jnp.int32, (1, PAIR), 1)
        out_ref[...] = jnp.where(lane < HEAD_DIM, found[0], found[1]).astype(jnp.bfloat16)

    return pl.pallas_call(
        kernel,
        grid=(pairs,),
        out_shape=[
            jax.ShapeDtypeStruct((rows, width), jnp.bfloat16),
            jax.ShapeDtypeStruct((2 * pairs, 1, rows), jnp.float32),
        ],
        in_specs=[
            pl.BlockSpec((1, rows), lambda j: (0, 0)),
            pl.BlockSpec((rows, 1), lambda j: (0, 0)),
            pl.BlockSpec((rows, PAIR), lambda j: (0, j)),
            pl.BlockSpec((rows, PAIR), lambda j: (0, pairs + j)),
            pl.BlockSpec((rows, PAIR), lambda j: (0, 2 * pairs + j)),
        ],
        out_specs=[
            pl.BlockSpec((rows, PAIR), lambda j: (0, j)),
            pl.BlockSpec((2, 1, rows), lambda j: (j, 0, 0)),
        ],
        scratch_shapes=[pltpu.VMEM((rows, rows), jnp.float32)],
        name="attend",
    )(seg_row, seg_column, qkv, qkv, qkv)


def attend_back(qkv, d_attended, lse, seg_row, seg_column):
    rows, width = qkv.shape[0], qkv.shape[1] // 3
    pairs = width // PAIR
    scale = HEAD_DIM ** (-0.5)

    def kernel(seg_row_ref, seg_column_ref, q_ref, k_ref, v_ref, d_ref, lse_ref, out_ref, bias_ref):
        step = pl.program_id(0)

        @pl.when(step == 0)
        def _():
            fill_bias(seg_row_ref, seg_column_ref, bias_ref)

        query, keyed, valued, d_out = q_ref[...], k_ref[...], v_ref[...], d_ref[...]
        scaled = query * jnp.bfloat16(scale)
        d_query, d_key, d_value = [], [], []
        for head in (0, 1):
            lanes = lanes_of(head)
            scores = contract_last(keyed, scaled * lanes) + bias_ref[...]
            probs = jnp.exp(scores - lse_ref[head, :, :])
            d_probs = contract_last(valued, d_out * lanes)
            inner = jnp.sum(probs * d_probs, axis=0, keepdims=True)
            d_scores = (probs * (d_probs - inner)).astype(jnp.bfloat16)
            d_value.append(plain_dot(probs.astype(jnp.bfloat16), d_out))
            d_key.append(plain_dot(d_scores, scaled))
            d_query.append(contract_rows(d_scores, keyed) * scale)
        lane = lax.broadcasted_iota(jnp.int32, (1, PAIR), 1)
        for at, pair in enumerate((d_query, d_key, d_value)):
            column = pl.multiple_of(at * width + step * PAIR, PAIR)
            out_ref[:, pl.ds(column, PAIR)] = jnp.where(lane < HEAD_DIM, pair[0], pair[1]).astype(
                jnp.bfloat16
            )

    return pl.pallas_call(
        kernel,
        grid=(pairs,),
        out_shape=jax.ShapeDtypeStruct((rows, 3 * width), jnp.bfloat16),
        in_specs=[
            pl.BlockSpec((1, rows), lambda j: (0, 0)),
            pl.BlockSpec((rows, 1), lambda j: (0, 0)),
            pl.BlockSpec((rows, PAIR), lambda j: (0, j)),
            pl.BlockSpec((rows, PAIR), lambda j: (0, pairs + j)),
            pl.BlockSpec((rows, PAIR), lambda j: (0, 2 * pairs + j)),
            pl.BlockSpec((rows, PAIR), lambda j: (0, j)),
            pl.BlockSpec((2, 1, rows), lambda j: (j, 0, 0)),
        ],
        out_specs=pl.BlockSpec((rows, 3 * width), lambda j: (0, 0)),
        scratch_shapes=[pltpu.VMEM((rows, rows), jnp.float32)],
        name="attend_back",
    )(seg_row, seg_column, qkv, qkv, qkv, d_attended, lse)


def swap_cores(values):
    return lax.ppermute(values, "core", [(0, 1), (1, 0)])


def reduce_grads(grads):
    chips, core = lax.axis_size("chips"), lax.axis_index("core")
    stacked = jnp.stack(grads)
    sides, width, columns = stacked.shape
    stacked = stacked.reshape(sides, chips, 2, width // (2 * chips), columns)
    kept = lax.dynamic_index_in_dim(stacked, core, 2, keepdims=False)
    sent = lax.dynamic_index_in_dim(stacked, 1 - core, 2, keepdims=False).astype(jnp.bfloat16)
    total = (kept.astype(jnp.float32) + swap_cores(sent).astype(jnp.float32)).astype(jnp.bfloat16)
    total = total.reshape(-1, columns)
    return lax.psum_scatter(total, SAME_CORE, scatter_dimension=0, tiled=True).astype(jnp.float32)


def sum_everywhere(values):
    values = values + swap_cores(values)
    values = values + lax.ppermute(values, "tensor", [(0, 1), (1, 0)])
    count, bit = lax.axis_size("chips"), 1
    while bit < count:
        values = values + lax.ppermute(values, "chips", [(i, i ^ bit) for i in range(count)])
        bit *= 2
    return values


def local(
    block_input,
    output_cot,
    segment_ids,
    routed_index,
    w_query,
    w_key,
    w_value,
    w_output,
    w_up,
    w_down,
    attn_gain,
    mlp_gain,
    router_w,
):
    side = lax.axis_index("tensor")
    sides = lax.axis_size("tensor")
    rank = lax.axis_index(DP)
    width = block_input.shape[1]
    share, heads = w_query.shape
    hidden = w_up.shape[1]

    vectors = jnp.stack([attn_gain, mlp_gain, router_w], axis=1)
    vectors = jnp.pad(vectors, ((0, 0), (0, 128 - 3)))
    near = jnp.concatenate([w_query, w_key, w_value, w_output, vectors], axis=1)
    near = lax.all_gather(near, ALL, axis=0, tiled=True).reshape(sides, width, -1)
    far = jnp.concatenate([w_up, w_down], axis=1)
    far = lax.all_gather(far, ALL, axis=0, tiled=True).reshape(sides, width, -1)
    full_qkv = [near[t, :, : 3 * heads] for t in range(sides)]
    full_output = [near[t, :, 3 * heads : 4 * heads] for t in range(sides)]
    full_up = [far[t, :, :hidden] for t in range(sides)]
    full_down = [far[t, :, hidden:] for t in range(sides)]
    small = near[0, :, 4 * heads : 4 * heads + 3].astype(jnp.float32).T
    attn_gain_f, mlp_gain_f, router_f = small[0], small[1], small[2]

    own_index = lax.dynamic_index_in_dim(routed_index, side, 0, keepdims=False)
    own_segments = lax.dynamic_index_in_dim(segment_ids, side, 0, keepdims=False)
    input_float = jnp.take(block_input, own_index, axis=0).astype(jnp.float32)
    cot_rows = jnp.take(output_cot, own_index, axis=0).astype(jnp.float32)
    firsts = jnp.sum(
        (own_segments[None, :] < jnp.arange(1, DOCS, dtype=jnp.int32)[:, None]).astype(jnp.int32), axis=1
    )
    seg_routed = jnp.sum((own_index[:, None] >= firsts[None, :]).astype(jnp.int32), axis=1)
    seg_row, seg_column = seg_routed[None, :], seg_routed[:, None]

    normed_attn = rms_norm(input_float, attn_gain_f).astype(jnp.bfloat16)
    gate = jax.nn.sigmoid(jnp.sum(input_float * router_f, axis=-1))
    d_branch = gate[:, None] * cot_rows
    d_mlp_low = d_branch.astype(jnp.bfloat16)

    qkv = [plain_dot(normed_attn, full_qkv[t]).astype(jnp.bfloat16) for t in range(sides)]
    attended, lse = zip(*[attend(qkv[t], seg_row, seg_column) for t in range(sides)])
    branch_attn = sum(contract_last(attended[t], full_output[t]) for t in range(sides))
    middle = input_float + branch_attn
    normed_mlp = rms_norm(middle, mlp_gain_f).astype(jnp.bfloat16)

    hidden_pre = [plain_dot(normed_mlp, full_up[t]) for t in range(sides)]
    hidden_act = [jax.nn.gelu(hidden_pre[t], approximate=True).astype(jnp.bfloat16) for t in range(sides)]
    d_pre = []
    for t in range(sides):
        unused_act, gelu_back = jax.vjp(partial(jax.nn.gelu, approximate=True), hidden_pre[t])
        d_pre.append(gelu_back(plain_dot(d_mlp_low, full_down[t]))[0].astype(jnp.bfloat16))
    grad_mlp = [
        jnp.concatenate(
            [contract_rows(normed_mlp, d_pre[t]), contract_rows(d_mlp_low, hidden_act[t])], axis=1
        ).astype(jnp.bfloat16)
        for t in range(sides)
    ]
    sum_mlp = reduce_grads(grad_mlp)

    d_normed_mlp = sum(contract_last(d_pre[t], full_up[t]) for t in range(sides))
    unused_mid, norm_back_mlp = jax.vjp(rms_norm, middle, mlp_gain_f)
    d_middle, d_mlp_gain = norm_back_mlp(d_normed_mlp)
    d_attn_low = (d_branch + d_middle).astype(jnp.bfloat16)
    d_qkv = []
    for t in range(sides):
        d_attended = plain_dot(d_attn_low, full_output[t]).astype(jnp.bfloat16)
        d_qkv.append(attend_back(qkv[t], d_attended, lse[t], seg_row, seg_column))
    grad_attn = [
        jnp.concatenate(
            [contract_rows(normed_attn, d_qkv[t]), contract_rows(d_attn_low, attended[t])], axis=1
        ).astype(jnp.bfloat16)
        for t in range(sides)
    ]
    sum_attn = reduce_grads(grad_attn)

    branch_mlp = sum(contract_last(hidden_act[t], full_down[t]) for t in range(sides))
    branch_total = branch_attn + branch_mlp
    updated = input_float + gate[:, None] * branch_total
    block_output = block_input.at[own_index].set(updated.astype(jnp.bfloat16))
    d_logit = gate * (1.0 - gate) * jnp.sum(cot_rows * branch_total, axis=-1)

    d_normed_attn = sum(contract_last(d_qkv[t], full_qkv[t]) for t in range(sides))
    unused_norm, norm_back_attn = jax.vjp(rms_norm, input_float, attn_gain_f)
    d_input_norm, d_attn_gain = norm_back_attn(d_normed_attn)
    d_router = jnp.sum(d_logit[:, None] * input_float, axis=0)
    routed_grad = cot_rows + d_logit[:, None] * router_f + d_middle + d_input_norm
    block_grad = output_cot.at[own_index].set(routed_grad.astype(jnp.bfloat16))

    totals = sum_everywhere(jnp.stack([d_attn_gain, d_mlp_gain, d_router]))
    own = lax.dynamic_slice_in_dim(totals, rank * share, share, axis=1)
    return (
        block_output,
        block_grad,
        sum_attn[:, :heads],
        sum_attn[:, heads : 2 * heads],
        sum_attn[:, 2 * heads : 3 * heads],
        sum_attn[:, 3 * heads :],
        sum_mlp[:, :hidden],
        sum_mlp[:, hidden:],
        own[0],
        own[1],
        own[2],
    )


def solution(mesh):
    fine = Mesh(mesh.devices.reshape(-1, 2, mesh.shape["tensor"]), ("chips", "core", "tensor"))
    token = P(("chips", "core", "tensor"), None)
    weight = P(DP, "tensor")
    in_specs = (token, token, P(DP, None), P(DP, None)) + (weight,) * 6 + (P(DP),) * 3
    out_specs = (token, token) + (weight,) * 6 + (P(DP),) * 3
    return jax.shard_map(local, mesh=fine, in_specs=in_specs, out_specs=out_specs, check_vma=False)
```

time: 1180 us -> 634 us (0.54)
  waiting for transfers between devices: 763 us -> 367 us
  blocking collectives: 105 us -> 0 us
  matrix products: 153 us -> 98.3 us
  Pallas kernels: 0 us -> 35.7 us
  local copies, waits for them, and re-layouts: 71.8 us -> 51.5 us
    reduce_scatter x10 -> x2, waiting for transfers between devices: 489 us -> 205 us  [reduce_grads(): lax.psum_scatter(total, SAME_CORE, scatter_dimension=0, tiled=True)]
    all_gather x10 -> x2, waiting for transfers between devices: 270 us -> 147 us  [the longest x1 83.6 us: local(): far = lax.all_gather(far, ALL, axis=0, tiled=True).reshape(sides, width, -1)]
    unnamed x2 -> x0, blocking collectives: 99.5 us -> none
    dot_general x7 -> x0, matrix products: 48.1 us -> none  [the longest x1 13.6 us: local(): jnp.einsum('sqhd,skhd->shqk', d_attended, valued, preferred_element_type=...]
    pallas_call x0 -> x4, Pallas kernels: none -> 35.7 us  [the longest x2 20.4 us: attend_back(): pl.pallas_call(kernel, grid=(pairs,), out_shape=jax.ShapeDtypeStruct((row...]
    reshape x8 -> x0, local copies, waits for them, and re-layouts: 18.9 us -> none  [split_heads(): return values.reshape(tensor_count, routed_rows, local_heads, HEAD_DIM)]
    ppermute x0 -> x7, waiting for transfers between devices: none -> 15.5 us  [the longest x3 6.69 us: sum_everywhere(): lax.ppermute(values, 'chips', [(i, i ^ bit) for i in range(count)])]
    reduce_sum x3 -> x2, other arithmetic: 14.3 us -> 0.31 us  [the longest x1 0.22 us: local(): jnp.sum((own_segments[None, :] < jnp.arange(1, DOCS, dtype=jnp.int32)[:,...]
  transfers between devices with their start and end apart: 20 -> 11, of which waited for: 17 -> 9; matrix products, arithmetic and copies ran while one was open for 15% -> 18% of each run, Pallas kernels for 0% -> 2%
where the time goes in v1:
time: 634 us; the launch traced here: 631 us
  waiting for transfers between devices  367 us (58%)
  matrix products  98.3 us (16%)
  other arithmetic  58.5 us (9%)
  local copies, waits for them, and re-layouts  51.5 us (8%)
  Pallas kernels  35.7 us (6%)
  between operations  14.6 us (2%)
    reduce_scatter x2, waiting for transfers between devices, reduce_grads(): lax.psum_scatter(total, SAME_CORE, scatter_dimension=0, tiled=True)  205 us
    all_gather x1, waiting for transfers between devices, local(): far = lax.all_gather(far, ALL, axis=0, tiled=True).reshape(sides, width, -1)  83.6 us
    all_gather x1, waiting for transfers between devices, local(): lax.all_gather(near, ALL, axis=0, tiled=True).reshape(sides, width, -1)  63.7 us
    dot_general x8, matrix products, plain_dot(): return jnp.dot(left, right, preferred_element_type=jnp.float32)  38.5 us
    dot_general x8, matrix products, contract_last(): lax.dot_general(left, right, (((1,), (1,)), ((), ())), preferred_element_...  32.5 us
    dot_general x8, matrix products, contract_rows(): lax.dot_general(left, right, (((0,), (0,)), ((), ())), preferred_element_...  27.3 us
    unnamed x80, local copies, waits for them, and re-layouts  20.6 us
    pallas_call x2, Pallas kernels, attend_back(): pl.pallas_call(kernel, grid=(pairs,), out_shape=jax.ShapeDtypeStruct((row...  20.4 us
  transfers between devices with their start and end apart: 11, of which 9 were waited for; matrix products, arithmetic and copies ran while one was open for 18% of the time, Pallas kernels for 2%

profile of v1, /device:TPU:0, one launch (start us, length us, event | category | flops | bytes accessed | tf_op | source)
XLA Modules:
  0.0 631.2 jit_solution(10483002733084236554)
XLA Ops:
  7.2 7.8 %copy.48 = bf16[4096,1024]{1,0:T(8,128)(2,1)} copy(bf16[4096,1024]{1,0:T(8,128)(2,1)} %param.15) | data formatting | bytes 16777216
  15.1 7.9 %copy.49 = bf16[4096,1024]{1,0:T(8,128)(2,1)} copy(bf16[4096,1024]{1,0:T(8,128)(2,1)} %param.16) | data formatting | bytes 16777216
  23.2 0.7 copy-done.16
  24.0 0.9 pad_maximum_fusion
  25.5 0.9 copy.33.seg_column_ref
  26.4 7.2 %gather_fusion = bf16[512,1024]{1,0:T(8,128)(2,1)S(1)} fusion(bf16[4096,1024]{1,0:T(8,128)(2,1)} %copy.48, s32[1024]{0:T(1024)S(1)} %pad_clamp_fusion), kind=kCustom, calls=%fused_computation.clone | custom fusion | bytes 2099200 | tf_op jit(solution)/shard_map/jit(_take)/gather | solution.py:215
  33.6 8.2 %gather_fusion.1 = bf16[512,1024]{1,0:T(8,128)(2,1)} fusion(bf16[4096,1024]{1,0:T(8,128)(2,1)} %copy.49, s32[1024]{0:T(1024)S(1)} %pad_clamp_fusion), kind=kCustom, calls=%fused_computation.1.clone | custom fusion | bytes 2099200 | tf_op jit(solution)/shard_map/jit(_take)/gather | solution.py:216
  41.9 0.4 fusion.38
  42.3 63.7 %all-gather.3.cloned.1.call-done = bf16[2048,2176]{1,0:T(8,128)(2,1)} async-done(((bf16[64,2176]{1,0:T(8,128)(2,1)}), bf16[2048,2176]{1,0:T(8,128)(2,1)}) %all-gather.3.cloned.1.call-update) | async-done | bytes 8912912 | tf_op jit(solution)/shard_map/all_gather | solution.py:203
  106.0 1.0 slice_convert_fusion
  107.2 5.0 convolution_convert_fusion.7.q_ref.k_ref.v_ref
  112.2 7.5 %attend.2 = (bf16[512,512]{1,0:T(8,128)(2,1)}, f32[8,1,512]{2,1,0:T(1,128)}) custom-call(s32[1,512]{1,0:T(1,128)} %bitcast.138, s32[512,1]{1,0:T(8,128)} %copy.33.seg_column_ref, bf16[512,1536]{1,0:T(8,128)(2,1)} %convolution_convert_fusion.7.q_ref.k_ref.v_ref, bf16[512,1536]{1,0:T(8,128)(2,1)} %convolution_convert_fusion.7.q_ref.k_ref.v_ref, ...), custom_call_target="tpu_custom_call" | custom-call | tf_op jit(solution)/shard_map/attend/pallas_call | solution.py:78
  119.7 5.0 convolution_convert_fusion.6.q_ref.k_ref.v_ref
  124.7 7.8 %attend.3 = (bf16[512,512]{1,0:T(8,128)(2,1)}, f32[8,1,512]{2,1,0:T(1,128)}) custom-call(s32[1,512]{1,0:T(1,128)} %bitcast.139, s32[512,1]{1,0:T(8,128)} %copy.33.seg_column_ref, bf16[512,1536]{1,0:T(8,128)(2,1)} %convolution_convert_fusion.6.q_ref.k_ref.v_ref, bf16[512,1536]{1,0:T(8,128)(2,1)} %convolution_convert_fusion.6.q_ref.k_ref.v_ref, ...), custom_call_target="tpu_custom_call" | custom-call | tf_op jit(solution)/shard_map/attend/pallas_call | solution.py:78
  132.5 2.0 fusion.54
  134.4 2.4 fusion.37
  136.9 1.4 multiply_convert_fusion.2
  138.3 83.6 %all-gather.5.cloned.1.call-done = bf16[2048,4096]{1,0:T(8,128)(2,1)} async-done(((bf16[64,4096]{1,0:T(8,128)(2,1)}), bf16[2048,4096]{1,0:T(8,128)(2,1)}) %all-gather.5.cloned.1.call-update) | async-done | bytes 16777232 | tf_op jit(solution)/shard_map/all_gather | solution.py:205
  221.9 5.0 fusion.17
  226.9 6.8 %fusion.21 = f32[512,2048]{1,0:T(8,128)S(1)} fusion(bf16[512,1024]{1,0:T(8,128)(2,1)S(1)} %copy-done.11, bf16[2,1024,4096]{2,1,0:T(8,128)(2,1)} %bitcast.173), kind=kOutput, calls=%fused_computation.55 | convolution fusion | flops 2147483648 | bytes 9437184 | tf_op jit(solution)/shard_map/dot_general | solution.py:26
  233.7 4.1 fusion.19
  237.8 4.6 fusion.8
  242.5 6.4 %fusion.15 = bf16[512,2048]{1,0:T(8,128)(2,1)} fusion(f32[512,2048]{1,0:T(8,128)S(1)} %fusion.21, bf16[2,1024,4096]{2,1,0:T(8,128)(2,1)S(1)} %bitcast.176, f32[512]{0:T(512)S(1)} %get-tuple-element.45, bf16[512,1024]{1,0:T(8,128)(2,1)S(1)} %copy-done.3, pred[512]{0:T(512)(128)(4,1)S(1)} %compare_and_fusion), kind=kOutput, calls=%fused_computation.36 | convolution fusion | flops 2170552320 | bytes 11536896 | tf_op jit(solution)/shard_map/dot_general | solution.py:26
  248.9 5.0 add_add_fusion.2
  253.9 3.8 fusion.16
  257.7 5.4 multiply_reduce_fusion
  263.2 1.4 fusion.32
  264.6 2.8 convolution_convert_fusion.11.d_ref
  267.4 2.9 convolution_convert_fusion.10.d_ref
  270.2 1.7 convolution_convert_fusion.8
  271.9 1.7 convolution_convert_fusion.9
  273.7 4.4 convolution_convert_fusion.1
  278.1 4.4 convolution_convert_fusion.3
  282.5 10.1 %attend_back.3 = bf16[512,1536]{1,0:T(8,128)(2,1)} custom-call(s32[1,512]{1,0:T(1,128)} %bitcast.140, s32[512,1]{1,0:T(8,128)} %copy.33.seg_column_ref, bf16[512,1536]{1,0:T(8,128)(2,1)} %convolution_convert_fusion.6.q_ref.k_ref.v_ref, bf16[512,1536]{1,0:T(8,128)(2,1)} %convolution_convert_fusion.6.q_ref.k_ref.v_ref, ...), custom_call_target="tpu_custom_call" | custom-call | tf_op jit(solution)/shard_map/attend_back/pallas_call | solution.py:133
  292.6 5.0 convolution_convert_fusion.4
  297.6 10.3 %attend_back.2 = bf16[512,1536]{1,0:T(8,128)(2,1)} custom-call(s32[1,512]{1,0:T(1,128)} %bitcast.141, s32[512,1]{1,0:T(8,128)} %copy.33.seg_column_ref, bf16[512,1536]{1,0:T(8,128)(2,1)} %convolution_convert_fusion.7.q_ref.k_ref.v_ref, bf16[512,1536]{1,0:T(8,128)(2,1)} %convolution_convert_fusion.7.q_ref.k_ref.v_ref, ...), custom_call_target="tpu_custom_call" | custom-call | tf_op jit(solution)/shard_map/attend_back/pallas_call | solution.py:133
  308.0 3.6 convolution_convert_fusion.5
  311.5 1.1 maximum_maximum_fusion.1
  312.6 2.4 dynamic-slice_bitcast_fusion.1
  315.1 3.5 copy-done.2
  318.9 3.2 convolution_convert_fusion
  322.2 3.3 convolution_convert_fusion.2
  325.6 6.7 %maximum_maximum_fusion = bf16[2,8,2,64,4096]{4,3,2,1,0:T(8,128)(2,1)} fusion(bf16[1,8,2,64,2048]{4,3,2,1,0:T(8,128)(2,1)S(1)} %bitcast.122, bf16[1,8,2,64,2048]{4,3,2,1,0:T(8,128)(2,1)S(1)} %bitcast.120, bf16[1,8,2,64,2048]{4,3,2,1,0:T(8,128)(2,1)S(1)} %bitcast.123, bf16[1,8,2,64,2048]{4,3,2,1,0:T(8,128)(2,1)S(1)} %bitcast.121), kind=kLoop, calls=%fused_computation.4 | loop fusion | flops 67108864 | bytes 33554432 | tf_op jit(solution)/shard_map/stack | solution.py:158
  332.4 7.8 %dynamic-slice_bitcast_fusion = bf16[2,8,64,4096]{3,2,1,0:T(8,128)(2,1)} fusion(bf16[2,8,2,64,4096]{4,3,2,1,0:T(8,128)(2,1)} %maximum_maximum_fusion, s32[]{:T(128)S(6)} %select_n.40), kind=kLoop, calls=%fused_computation.10 | loop fusion | bytes 16777220 | tf_op jit(solution)/shard_map/jit(dynamic_index_in_dim)/squeeze | solution.py:162
  340.4 7.8 %fusion.1 = bf16[2,8,64,2048]{3,2,1,0:T(8,128)(2,1)} fusion(bf16[2,8,64,2048]{3,2,1,0:T(8,128)(2,1)} %collective-permute-done, bf16[2,8,2,64,2048]{4,3,2,1,0:T(8,128)(2,1)} %copy-done.2, s32[]{:T(128)S(6)} %select_n.39), kind=kLoop, calls=%fused_computation.9 | loop fusion | flops 8388608 | bytes 12582916 | tf_op jit(solution)/shard_map/convert_element_type | solution.py:163
  348.3 5.3 collective-permute-done.1
  353.6 10.5 %fusion = bf16[2,8,64,4096]{3,2,1,0:T(8,128)(2,1)} fusion(bf16[2,8,64,4096]{3,2,1,0:T(8,128)(2,1)} %collective-permute-done.1, bf16[2,8,2,64,4096]{4,3,2,1,0:T(8,128)(2,1)} %maximum_maximum_fusion, s32[]{:T(128)S(6)} %select_n.39), kind=kLoop, calls=%fused_computation.6 | loop fusion | flops 16777216 | bytes 25165828 | tf_op jit(solution)/shard_map/convert_element_type | solution.py:163
  364.2 4.3 fusion.24
  368.5 5.5 fusion.31
  374.4 0.9 collective-permute-done.2
  375.3 1.6 collective-permute-start.3
  376.9 2.6 collective-permute-done.3
  379.5 1.0 collective-permute-start.4
  380.4 3.6 collective-permute-done.4
  384.1 0.7 collective-permute-start.5
  384.8 3.0 collective-permute-done.5
  387.8 0.9 collective-permute-start.6
  388.7 12.4 %scatter_custom_fusion = bf16[4096,1024]{1,0:T(8,128)(2,1)} fusion(bf16[4096,1024]{1,0:T(8,128)(2,1)} %copy.48, s32[512]{0:T(512)S(1)} %bitcast.167, f32[512,1024]{1,0:T(8,128)} %copy-done.9, f32[512]{0:T(512)S(1)} %get-tuple-element.45, bf16[512,1024]{1,0:T(8,128)(2,1)S(1)} %gather_fusion, pred[512]{0:T(512)(128)(4,1)S(1)} %compare_and_fusion), kind=kCustom, calls=%fused_computation.97 | custom fusion | flops 2621440 | bytes 11536896 | tf_op jit(solution)/shard_map/scatter | solution.py:267
  401.2 14.2 %scatter_custom_fusion.1 = bf16[4096,1024]{1,0:T(8,128)(2,1)} fusion(bf16[4096,1024]{1,0:T(8,128)(2,1)} %copy.49, s32[512]{0:T(512)S(1)} %bitcast.168, f32[512,1024]{1,0:T(8,128)} %get-tuple-element.44, f32[512]{0:T(512)S(1)} %multiply_multiply_fusion.4, f32[512]{0:T(512)S(1)} %fusion.55, f32[1024]{0:T(1024)S(1)} %bitcast.166, f32[512]{0:T(512)S(1)} %fusion.56, ...), kind=kCustom, calls=%fused_computation.98 | custom fusion | flops 10485760 | bytes 16800256 | tf_op jit(solution)/shard_map/scatter | solution.py:275
  415.5 0.5 slice_bitcast_fusion.34
  416.0 27.1 %reduce-scatter.3.cloned.1.call-done = bf16[64,2048]{1,0:T(8,128)(2,1)} async-done(((bf16[1024,2048]{1,0:T(8,128)(2,1)}), bf16[64,2048]{1,0:T(8,128)(2,1)}) %reduce-scatter.3.cloned.1.call-update) | async-done | bytes 262160 | tf_op jit(solution)/shard_map/reduce_scatter | solution.py:165
  443.1 1.7 fusion.68
  444.9 177.5 %reduce-scatter.5.cloned.1.call-done = bf16[64,4096]{1,0:T(8,128)(2,1)} async-done(((bf16[1024,4096]{1,0:T(8,128)(2,1)}), bf16[64,4096]{1,0:T(8,128)(2,1)}) %reduce-scatter.5.cloned.1.call-update) | async-done | bytes 524304 | tf_op jit(solution)/shard_map/reduce_scatter | solution.py:165
  622.3 2.1 fusion.67
  (112 shorter events, 2.6 us)
Async XLA Ops:
  7.2 18.0 %copy-start = (s32[2,4096]{1,0:T(2,128)S(1)}, s32[2,4096]{1,0:T(2,128)}, u32[]{:S(2)}) copy-start(s32[2,4096]{1,0:T(2,128)} %param.17) | copy-start | bytes 98308
  7.2 98.8 %all-gather.3.cloned.1.call-start = ((), (), s32[]{:S(2)}) async-start(), calls=%async_computation.2 | async-start | bytes 9191424 | tf_op jit(solution)/shard_map/all_gather | solution.py:203
  15.0 8.0 %copy-start.20 = (bf16[64,512]{1,0:T(8,128)(2,1)S(1)}, bf16[64,512]{1,0:T(8,128)(2,1)}, u32[]{:S(2)}) copy-start(bf16[64,512]{1,0:T(8,128)(2,1)} %param.19) | copy-start | bytes 196612
  15.0 8.0 %copy-start.25 = (bf16[64]{0:T(256)(128)(2,1)S(1)}, bf16[64]{0:T(256)(128)(2,1)}, u32[]{:S(2)}) copy-start(bf16[64]{0:T(256)(128)(2,1)} %param.27) | copy-start | bytes 388
  15.0 8.0 %copy-start.26 = (bf16[64]{0:T(256)(128)(2,1)S(1)}, bf16[64]{0:T(256)(128)(2,1)}, u32[]{:S(2)}) copy-start(bf16[64]{0:T(256)(128)(2,1)} %param.26) | copy-start | bytes 388
  15.0 8.0 %copy-start.27 = (bf16[64]{0:T(256)(128)(2,1)S(1)}, bf16[64]{0:T(256)(128)(2,1)}, u32[]{:S(2)}) copy-start(bf16[64]{0:T(256)(128)(2,1)} %param.25) | copy-start | bytes 388
  15.0 8.1 %copy-start.21 = (bf16[64,512]{1,0:T(8,128)(2,1)S(1)}, bf16[64,512]{1,0:T(8,128)(2,1)}, u32[]{:S(2)}) copy-start(bf16[64,512]{1,0:T(8,128)(2,1)} %param.20) | copy-start | bytes 196612
  15.0 8.1 %copy-start.22 = (bf16[64,512]{1,0:T(8,128)(2,1)S(1)}, bf16[64,512]{1,0:T(8,128)(2,1)}, u32[]{:S(2)}) copy-start(bf16[64,512]{1,0:T(8,128)(2,1)} %param.21) | copy-start | bytes 196612
  15.0 8.2 %copy-start.23 = (bf16[64,512]{1,0:T(8,128)(2,1)S(1)}, bf16[64,512]{1,0:T(8,128)(2,1)}, u32[]{:S(2)}) copy-start(bf16[64,512]{1,0:T(8,128)(2,1)} %param.22) | copy-start | bytes 196612
  15.0 9.0 %copy-start.17 = (bf16[64,2048]{1,0:T(8,128)(2,1)S(1)}, bf16[64,2048]{1,0:T(8,128)(2,1)}, u32[]{:S(2)}) copy-start(bf16[64,2048]{1,0:T(8,128)(2,1)} %param.24) | copy-start | bytes 786436
  15.1 9.0 %copy-start.18 = (bf16[64,2048]{1,0:T(8,128)(2,1)S(1)}, bf16[64,2048]{1,0:T(8,128)(2,1)}, u32[]{:S(2)}) copy-start(bf16[64,2048]{1,0:T(8,128)(2,1)} %param.23) | copy-start | bytes 786436
  15.1 10.1 %copy-start.24 = (s32[2,512]{1,0:T(2,128)S(1)}, s32[2,512]{1,0:T(2,128)}, u32[]{:S(2)}) copy-start(s32[2,512]{1,0:T(2,128)} %param.18) | copy-start | bytes 12292
  23.2 0.7 copy-start.16
  24.0 197.9 %all-gather.5.cloned.1.call-start = ((), (), s32[]{:S(2)}) async-start(), calls=%async_computation.3 | async-start | bytes 17301504 | tf_op jit(solution)/shard_map/all_gather | solution.py:205
  24.9 418.2 %reduce-scatter.3.cloned.1.call-start = ((), (), s32[]{:S(2)}) async-start(), calls=%async_computation.4 | async-start | bytes 4456448 | tf_op jit(solution)/shard_map/reduce_scatter | solution.py:165
  25.5 8.1 %copy-start.19 = (s32[512]{0:T(512)}, s32[512]{0:T(512)S(1)}, u32[]{:S(2)}) copy-start(s32[512]{0:T(512)S(1)} %convert_reduce_fusion.1) | copy-start | bytes 6148
  124.7 7.8 %copy-start.14 = (bf16[512,512]{1,0:T(8,128)(2,1)S(1)}, bf16[512,512]{1,0:T(8,128)(2,1)}, u32[]{:S(2)}) copy-start(bf16[512,512]{1,0:T(8,128)(2,1)} %get-tuple-element.16) | copy-start | bytes 1572868
  221.9 5.0 copy-start.11
  221.9 11.8 %copy-start.28 = (bf16[2048,4096]{1,0:T(8,128)(2,1)S(1)}, bf16[2048,4096]{1,0:T(8,128)(2,1)}, u32[]{:S(2)}) copy-start(bf16[2048,4096]{1,0:T(8,128)(2,1)} %all-gather.5.cloned.1.call-done) | copy-start | bytes 50331652
  226.9 10.9 %copy-start.30 = (f32[512,2048]{1,0:T(8,128)}, f32[512,2048]{1,0:T(8,128)S(1)}, u32[]{:S(2)}) copy-start(f32[512,2048]{1,0:T(8,128)S(1)} %fusion.17) | copy-start | bytes 12582916
  233.7 8.8 %copy-start.32 = (f32[512,2048]{1,0:T(8,128)}, f32[512,2048]{1,0:T(8,128)S(1)}, u32[]{:S(2)}) copy-start(f32[512,2048]{1,0:T(8,128)S(1)} %fusion.21) | copy-start | bytes 12582916
  233.7 4.1 copy-start.3
  242.5 6.4 %copy-start.35 = (f32[512,1024]{1,0:T(8,128)S(1)}, f32[512,1024]{1,0:T(8,128)}, u32[]{:S(2)}) copy-start(f32[512,1024]{1,0:T(8,128)} %fusion.19) | copy-start | bytes 6291460
  253.9 3.8 copy-start.9
  263.1 4.2 copy-start.5
  264.5 5.7 copy-start.29
  267.4 4.6 copy-start.15
  267.4 6.3 %copy-start.34 = (bf16[512,2048]{1,0:T(8,128)(2,1)S(1)}, bf16[512,2048]{1,0:T(8,128)(2,1)}, u32[]{:S(2)}) copy-start(bf16[512,2048]{1,0:T(8,128)(2,1)} %fusion.15) | copy-start | bytes 6291460
  307.9 3.6 copy-start.8
  307.9 3.6 copy-start.12
  307.9 3.6 copy-start.13
  312.6 5.9 copy-start.2
  312.6 6.2 copy-start.4
  312.6 6.3 copy-start.33
  318.5 3.6 copy-start.31
  318.6 21.8 %collective-permute-start = (bf16[2,8,64,2048]{3,2,1,0:T(8,128)(2,1)}, bf16[2,8,64,2048]{3,2,1,0:T(8,128)(2,1)}, u32[]{:S(2)}, u32[]{:S(2)}) collective-permute-start(bf16[2,8,64,2048]{3,2,1,0:T(8,128)(2,1)} %dynamic-slice_bitcast_fusion.1), channel_id=1, source_target_pairs={{0,2},{2,0},{1,3},{3,1},{4,6},{6,4},{5,7},{7,5},{8,10},{10,8},{9,1... | collective-permute-start | bytes 12582920 | tf_op jit(solution)/shard_map/ppermute | solution.py:153
  322.2 3.3 copy-start.6
  322.2 3.5 copy-start.7
  340.1 13.5 %collective-permute-start.1 = (bf16[2,8,64,4096]{3,2,1,0:T(8,128)(2,1)}, bf16[2,8,64,4096]{3,2,1,0:T(8,128)(2,1)}, u32[]{:S(2)}, u32[]{:S(2)}) collective-permute-start(bf16[2,8,64,4096]{3,2,1,0:T(8,128)(2,1)} %dynamic-slice_bitcast_fusion), channel_id=1, source_target_pairs={{0,2},{2,0},{1,3},{3,1},{4,6},{6,4},{5,7},{7,5},{8,10},{10,8},{9,1... | collective-permute-start | bytes 25165832 | tf_op jit(solution)/shard_map/ppermute | solution.py:153
  348.2 274.1 %reduce-scatter.5.cloned.1.call-start = ((), (), s32[]{:S(2)}) async-start(), calls=%async_computation.5 | async-start | bytes 8912896 | tf_op jit(solution)/shard_map/reduce_scatter | solution.py:165
  364.2 4.3 copy-start.10
  374.0 1.2 collective-permute-start.2
  375.3 4.2 collective-permute-start.3
  379.5 4.6 collective-permute-start.4
  384.1 3.7 collective-permute-start.5
  387.8 27.6 %collective-permute-start.6 = (f32[3,1024]{1,0:T(4,128)S(1)}, f32[3,1024]{1,0:T(4,128)S(1)}, u32[]{:S(2)}, u32[]{:S(2)}) collective-permute-start(f32[3,1024]{1,0:T(4,128)S(1)} %add.185), channel_id=1, source_target_pairs={{0,16},{4,20},{8,24},{12,28},{16,0},{20,4},{24,8},{28,12},{1,17},{... | collective-permute-start | bytes 36872 | tf_op jit(solution)/shard_map/ppermute | solution.py:173
  401.2 223.3 %copy-start.1 = (s32[2,4096]{1,0:T(2,128)S(1)}, s32[2,4096]{1,0:T(2,128)}, u32[]{:S(2)}) copy-start(s32[2,4096]{1,0:T(2,128)} %param.17) | copy-start | bytes 98308
Sparse Core Ops, SparseCore 0:
  24.1 81.8 all-gather.2
  108.8 113.0 all-gather.4
  348.4 94.7 reduce-scatter.2
  445.3 177.0 reduce-scatter.4

commit v2 on v1

--- a/solution.py
+++ b/solution.py
@@ -7,6 +7,7 @@
 from jax.experimental.pallas import tpu as pltpu
 from jax.sharding import Mesh
 from jax.sharding import PartitionSpec as P
+
 
 HEAD_DIM = 64
 EPSILON = 1e-05
@@ -153,29 +154,93 @@
     return lax.ppermute(values, "core", [(0, 1), (1, 0)])
 
 
-def reduce_grads(grads):
-    chips, core = lax.axis_size("chips"), lax.axis_index("core")
-    stacked = jnp.stack(grads)
-    sides, width, columns = stacked.shape
-    stacked = stacked.reshape(sides, chips, 2, width // (2 * chips), columns)
-    kept = lax.dynamic_index_in_dim(stacked, core, 2, keepdims=False)
-    sent = lax.dynamic_index_in_dim(stacked, 1 - core, 2, keepdims=False).astype(jnp.bfloat16)
-    total = (kept.astype(jnp.float32) + swap_cores(sent).astype(jnp.float32)).astype(jnp.bfloat16)
-    total = total.reshape(-1, columns)
+def reduce_near(parts):
+    kept = jnp.stack([part[0] for part in parts])
+    got = swap_cores(jnp.stack([part[1] for part in parts]))
+    total = (kept.astype(jnp.float32) + got.astype(jnp.float32)).astype(jnp.bfloat16)
+    total = total.reshape(-1, total.shape[-1])
     return lax.psum_scatter(total, SAME_CORE, scatter_dimension=0, tiled=True).astype(jnp.float32)
+
+
+def relative_order(values, near_only):
+    width = values.shape[1]
+    chips = lax.axis_size("chips")
+    chip, core = lax.axis_index("chips"), lax.axis_index("core")
+    share = width // (2 * chips)
+    column = lax.broadcasted_iota(jnp.int32, (width, width), 1)
+    row = lax.broadcasted_iota(jnp.int32, (width, width), 0)
+    core_at = (column // (width // 2)) ^ core
+    if near_only:
+        chip_at = (column // share) % chips
+    else:
+        cross_at = (column // (width // 4)) % 2
+        line_at = (column // share) % (chips // 2)
+        chip_at = (line_at * 2 + cross_at) ^ chip
+    wanted = (chip_at * 2 + core_at) * share + column % share
+    return plain_dot(values, (row == wanted).astype(jnp.bfloat16)).astype(jnp.bfloat16)
+
+
+def swap_sides(values):
+    return lax.ppermute(values, "tensor", [(0, 1), (1, 0)])
+
+
+def swap_chips(values, bit):
+    return lax.ppermute(values, "chips", [(i, i ^ bit) for i in range(lax.axis_size("chips"))])
+
+
+def add_low(left, right):
+    return (left.astype(jnp.float32) + right.astype(jnp.float32)).astype(jnp.bfloat16)
+
+
+def halve_line(values):
+    bit = lax.axis_size("chips") // 2
+    while bit > 1:
+        half = values.shape[0] // 2
+        got = swap_chips(values[half:], bit)
+        values = values[:half].astype(jnp.float32) + got.astype(jnp.float32)
+        bit //= 2
+        if bit > 1:
+            values = values.astype(jnp.bfloat16)
+    return values
+
+
+def place(whole, rows, index):
+    tokens, width = whole.shape
+    count = rows.shape[0]
+    step = 512
+
+    def kernel(index_ref, whole_ref, rows_ref, out_ref):
+        at = pl.program_id(0) * step + lax.broadcasted_iota(jnp.int32, (step, count), 0)
+        hit = (at == index_ref[...]).astype(jnp.float32)
+        routed = jnp.sum(hit, axis=1, keepdims=True) > 0.5
+        found = plain_dot(hit.astype(jnp.bfloat16), rows_ref[...])
+        out_ref[...] = jnp.where(routed, found, whole_ref[...].astype(jnp.float32)).astype(jnp.bfloat16)
+
+    return pl.pallas_call(
+        kernel,
+        grid=(tokens // step,),
+        out_shape=jax.ShapeDtypeStruct(whole.shape, whole.dtype),
+        in_specs=[
+            pl.BlockSpec((1, count), lambda i: (0, 0)),
+            pl.BlockSpec((step, width), lambda i: (i, 0)),
+            pl.BlockSpec((count, width), lambda i: (0, 0)),
+        ],
+        out_specs=pl.BlockSpec((step, width), lambda i: (i, 0)),
+        name="place_rows",
+    )(index[None, :], whole, rows)
 
 
 def sum_everywhere(values):
     values = values + swap_cores(values)
-    values = values + lax.ppermute(values, "tensor", [(0, 1), (1, 0)])
+    values = values + swap_sides(values)
     count, bit = lax.axis_size("chips"), 1
     while bit < count:
-        values = values + lax.ppermute(values, "chips", [(i, i ^ bit) for i in range(count)])
+        values = values + swap_chips(values, bit)
         bit *= 2
     return values
 
 
-def local(
+def block(
     block_input,
     output_cot,
     segment_ids,
@@ -235,44 +300,67 @@
     hidden_act = [jax.nn.gelu(hidden_pre[t], approximate=True).astype(jnp.bfloat16) for t in range(sides)]
     d_pre = []
     for t in range(sides):
-        unused_act, gelu_back = jax.vjp(partial(jax.nn.gelu, approximate=True), hidden_pre[t])
+        _, gelu_back = jax.vjp(partial(jax.nn.gelu, approximate=True), hidden_pre[t])
         d_pre.append(gelu_back(plain_dot(d_mlp_low, full_down[t]))[0].astype(jnp.bfloat16))
-    grad_mlp = [
-        jnp.concatenate(
-            [contract_rows(normed_mlp, d_pre[t]), contract_rows(d_mlp_low, hidden_act[t])], axis=1
-        ).astype(jnp.bfloat16)
-        for t in range(sides)
-    ]
-    sum_mlp = reduce_grads(grad_mlp)
+    own_pre = [jnp.where(side == 0, d_pre[t], d_pre[1 - t]) for t in range(sides)]
+    own_act = [jnp.where(side == 0, hidden_act[t], hidden_act[1 - t]) for t in range(sides)]
+    left_up = relative_order(normed_mlp, False)
+    left_down = relative_order(d_mlp_low, False)
+    half = width // 2
+    sent_up = [contract_rows(left_up[:, half:], own_pre[t]).astype(jnp.bfloat16) for t in (1, 0)][::-1]
+    sent_down = [contract_rows(left_down[:, half:], own_act[t]).astype(jnp.bfloat16) for t in (1, 0)][::-1]
+    got_up = [swap_cores(sent_up[t]) for t in (1, 0)][::-1]
+    got_down = [swap_cores(sent_down[t]) for t in (1, 0)][::-1]
+    d_pre, sent_up, sent_down = lax.optimization_barrier((d_pre, sent_up, sent_down))
+    part_up = [add_low(contract_rows(left_up[:, :half], own_pre[t]), got_up[t]) for t in (0, 1)]
+    part_down = [add_low(contract_rows(left_down[:, :half], own_act[t]), got_down[t]) for t in (0, 1)]
+    quarter = half // 2
+    got_up = swap_sides(part_up[1])
+    got_down = [swap_chips(part_down[t][quarter:], 1) for t in (0, 1)]
+    one_up = add_low(part_up[0], got_up)
+    one_down = [add_low(part_down[t][:quarter], got_down[t]) for t in (0, 1)]
+    got_up = swap_chips(one_up[quarter:], 1)
+    got_down = swap_sides(one_down[1])
+    sum_up = halve_line(add_low(one_up[:quarter], got_up))
+    sum_down = halve_line(add_low(one_down[0], got_down))
 
     d_normed_mlp = sum(contract_last(d_pre[t], full_up[t]) for t in range(sides))
-    unused_mid, norm_back_mlp = jax.vjp(rms_norm, middle, mlp_gain_f)
+    _, norm_back_mlp = jax.vjp(rms_norm, middle, mlp_gain_f)
     d_middle, d_mlp_gain = norm_back_mlp(d_normed_mlp)
     d_attn_low = (d_branch + d_middle).astype(jnp.bfloat16)
     d_qkv = []
     for t in range(sides):
         d_attended = plain_dot(d_attn_low, full_output[t]).astype(jnp.bfloat16)
         d_qkv.append(attend_back(qkv[t], d_attended, lse[t], seg_row, seg_column))
+    left_qkv = relative_order(normed_attn, True)
+    left_output = relative_order(d_attn_low, True)
     grad_attn = [
-        jnp.concatenate(
-            [contract_rows(normed_attn, d_qkv[t]), contract_rows(d_attn_low, attended[t])], axis=1
-        ).astype(jnp.bfloat16)
+        [
+            jnp.concatenate(
+                [
+                    contract_rows(left_qkv[:, rows], d_qkv[t]),
+                    contract_rows(left_output[:, rows], attended[t]),
+                ],
+                axis=1,
+            ).astype(jnp.bfloat16)
+            for rows in (slice(0, half), slice(half, width))
+        ]
         for t in range(sides)
     ]
-    sum_attn = reduce_grads(grad_attn)
+    sum_attn = reduce_near(grad_attn)
 
     branch_mlp = sum(contract_last(hidden_act[t], full_down[t]) for t in range(sides))
     branch_total = branch_attn + branch_mlp
     updated = input_float + gate[:, None] * branch_total
-    block_output = block_input.at[own_index].set(updated.astype(jnp.bfloat16))
+    block_output = place(block_input, updated.astype(jnp.bfloat16), own_index)
     d_logit = gate * (1.0 - gate) * jnp.sum(cot_rows * branch_total, axis=-1)
 
     d_normed_attn = sum(contract_last(d_qkv[t], full_qkv[t]) for t in range(sides))
-    unused_norm, norm_back_attn = jax.vjp(rms_norm, input_float, attn_gain_f)
+    _, norm_back_attn = jax.vjp(rms_norm, input_float, attn_gain_f)
     d_input_norm, d_attn_gain = norm_back_attn(d_normed_attn)
     d_router = jnp.sum(d_logit[:, None] * input_float, axis=0)
     routed_grad = cot_rows + d_logit[:, None] * router_f + d_middle + d_input_norm
-    block_grad = output_cot.at[own_index].set(routed_grad.astype(jnp.bfloat16))
+    block_grad = place(output_cot, routed_grad.astype(jnp.bfloat16), own_index)
 
     totals = sum_everywhere(jnp.stack([d_attn_gain, d_mlp_gain, d_router]))
     own = lax.dynamic_slice_in_dim(totals, rank * share, share, axis=1)
@@ -283,8 +371,8 @@
         sum_attn[:, heads : 2 * heads],
         sum_attn[:, 2 * heads : 3 * heads],
         sum_attn[:, 3 * heads :],
-        sum_mlp[:, :hidden],
-        sum_mlp[:, hidden:],
+        sum_up,
+        sum_down,
         own[0],
         own[1],
         own[2],
@@ -297,4 +385,4 @@
     weight = P(DP, "tensor")
     in_specs = (token, token, P(DP, None), P(DP, None)) + (weight,) * 6 + (P(DP),) * 3
     out_specs = (token, token) + (weight,) * 6 + (P(DP),) * 3
-    return jax.shard_map(local, mesh=fine, in_specs=in_specs, out_specs=out_specs, check_vma=False)
+    return jax.shard_map(block, mesh=fine, in_specs=in_specs, out_specs=out_specs, check_vma=False)

time: 634 us -> 525 us (0.83); the launches traced: 631 us -> 515 us
  waiting for transfers between devices: 367 us -> 268 us
  other arithmetic: 58.5 us -> 20.4 us
  Pallas kernels: 35.7 us -> 58 us
  local copies, waits for them, and re-layouts: 51.5 us -> 30.3 us
  starting transfers between devices: 5.35 us -> 15.4 us
  matrix products: 98.3 us -> 108 us
    reduce_scatter x2 -> x1, waiting for transfers between devices: 205 us -> 0.01 us  [reduce_near(): lax.psum_scatter(total, SAME_CORE, scatter_dimension=0, tiled=True)]
    ppermute x4 -> x13, waiting for transfers between devices: 9.26 us -> 128 us  [the longest x10 124 us: swap_chips(): lax.ppermute(values, 'chips', [(i, i ^ bit) for i in range(lax.axis_size(...]
    scatter x2 -> x0, other arithmetic: 26.7 us -> none  [the longest x1 14.2 us: local(): block_grad = output_cot.at[own_index].set(routed_grad.astype(jnp.bfloat16))]
    pallas_call x0 -> x2, Pallas kernels: none -> 22.5 us  [place(): pl.pallas_call(kernel, grid=(tokens // step,), out_shape=jax.ShapeDtypeSt...]
    unnamed x80 -> x98, local copies, waits for them, and re-layouts: 20.6 us -> 8.7 us
    squeeze x3 -> x1, local copies, waits for them, and re-layouts: 10.7 us -> 0.52 us  [block(): own[2]]
    ppermute x4 -> x13, starting transfers between devices: 4.15 us -> 13.9 us  [the longest x10 9.33 us: swap_chips(): lax.ppermute(values, 'chips', [(i, i ^ bit) for i in range(lax.axis_size(...]
    all_gather x2, waiting for transfers between devices: 147 us -> 139 us  [the longest x1 77.6 us: block(): far = lax.all_gather(far, ALL, axis=0, tiled=True).reshape(sides, width, -1)]
  transfers between devices with their start and end apart: 11 -> 22, of which waited for: 9 -> 12; matrix products, arithmetic and copies ran while one was open for 18% -> 17% of each run, Pallas kernels for 2% -> 7%
where the time goes in v2:
time: 525 us; the launch traced here: 515 us
  waiting for transfers between devices  268 us (51%)
  matrix products  108 us (21%)
  Pallas kernels  58 us (11%)
  local copies, waits for them, and re-layouts  30.3 us (6%)
  other arithmetic  20.4 us (4%)
  starting transfers between devices  15.4 us (3%)
  between operations  14.9 us (3%)
    ppermute x10, waiting for transfers between devices, swap_chips(): lax.ppermute(values, 'chips', [(i, i ^ bit) for i in range(lax.axis_size(...  124 us
    all_gather x1, waiting for transfers between devices, block(): far = lax.all_gather(far, ALL, axis=0, tiled=True).reshape(sides, width, -1)  77.6 us
    all_gather x1, waiting for transfers between devices, block(): lax.all_gather(near, ALL, axis=0, tiled=True).reshape(sides, width, -1)  61.6 us
    dot_general x12, matrix products, plain_dot(): return jnp.dot(left, right, preferred_element_type=jnp.float32)  46.3 us
    dot_general x16, matrix products, contract_rows(): lax.dot_general(left, right, (((0,), (0,)), ((), ())), preferred_element_...  31.6 us
    dot_general x8, matrix products, contract_last(): lax.dot_general(left, right, (((1,), (1,)), ((), ())), preferred_element_...  30.5 us
    pallas_call x2, Pallas kernels, place(): pl.pallas_call(kernel, grid=(tokens // step,), out_shape=jax.ShapeDtypeSt...  22.5 us
    pallas_call x2, Pallas kernels, attend_back(): pl.pallas_call(kernel, grid=(pairs,), out_shape=jax.ShapeDtypeStruct((row...  20.2 us
  transfers between devices with their start and end apart: 22, of which 12 were waited for; matrix products, arithmetic and copies ran while one was open for 17% of the time, Pallas kernels for 7%

profile of v2, /device:TPU:0, one launch (start us, length us, event | category | flops | bytes accessed | tf_op | source)
XLA Modules:
  0.0 515.2 jit_solution(17177517023343709294)
XLA Ops:
  12.2 1.9 pad_maximum_fusion
  16.1 7.2 %gather_fusion = bf16[512,1024]{1,0:T(8,128)(2,1)S(1)} fusion(bf16[4096,1024]{1,0:T(8,128)(2,1)} %whole_ref.2, s32[1024]{0:T(1024)S(1)} %pad_clamp_fusion), kind=kCustom, calls=%fused_computation.clone | custom fusion | bytes 2099200 | tf_op jit(solution)/shard_map/jit(_take)/gather | solution.py:280
  23.3 8.1 %gather_fusion.1 = bf16[512,1024]{1,0:T(8,128)(2,1)} fusion(bf16[4096,1024]{1,0:T(8,128)(2,1)} %whole_ref.3, s32[1024]{0:T(1024)S(1)} %pad_clamp_fusion), kind=kCustom, calls=%fused_computation.1.clone | custom fusion | bytes 2099200 | tf_op jit(solution)/shard_map/jit(_take)/gather | solution.py:281
  32.6 61.6 %all-gather.3.cloned.1.call-done = bf16[2048,2176]{1,0:T(8,128)(2,1)} async-done(((bf16[64,2176]{1,0:T(8,128)(2,1)}), bf16[2048,2176]{1,0:T(8,128)(2,1)}) %all-gather.3.cloned.1.call-update) | async-done | bytes 8912912 | tf_op jit(solution)/shard_map/all_gather | solution.py:268
  95.4 5.0 convolution_convert_fusion.9.q_ref.k_ref.v_ref
  100.4 7.5 %attend.2 = (bf16[512,512]{1,0:T(8,128)(2,1)}, f32[8,1,512]{2,1,0:T(1,128)}) custom-call(s32[1,512]{1,0:T(1,128)} %bitcast.132, s32[512,1]{1,0:T(8,128)} %copy.41.seg_column_ref, bf16[512,1536]{1,0:T(8,128)(2,1)} %convolution_convert_fusion.9.q_ref.k_ref.v_ref, bf16[512,1536]{1,0:T(8,128)(2,1)} %convolution_convert_fusion.9.q_ref.k_ref.v_ref, ...), custom_call_target="tpu_custom_call" | custom-call | tf_op jit(solution)/shard_map/attend/pallas_call | solution.py:79
  107.9 5.0 convolution_convert_fusion.8.q_ref.k_ref.v_ref
  112.9 7.7 %attend.3 = (bf16[512,512]{1,0:T(8,128)(2,1)}, f32[8,1,512]{2,1,0:T(1,128)}) custom-call(s32[1,512]{1,0:T(1,128)} %bitcast.133, s32[512,1]{1,0:T(8,128)} %copy.41.seg_column_ref, bf16[512,1536]{1,0:T(8,128)(2,1)} %convolution_convert_fusion.8.q_ref.k_ref.v_ref, bf16[512,1536]{1,0:T(8,128)(2,1)} %convolution_convert_fusion.8.q_ref.k_ref.v_ref, ...), custom_call_target="tpu_custom_call" | custom-call | tf_op jit(solution)/shard_map/attend/pallas_call | solution.py:79
  120.6 2.0 fusion.64
  122.6 2.4 fusion.53
  125.5 2.5 convolution_convert_fusion.11
  128.1 2.4 convolution_convert_fusion.13
  130.5 2.5 convolution_convert_fusion.12
  133.0 77.6 %all-gather.5.cloned.1.call-done = bf16[2048,4096]{1,0:T(8,128)(2,1)} async-done(((bf16[64,4096]{1,0:T(8,128)(2,1)}), bf16[2048,4096]{1,0:T(8,128)(2,1)}) %all-gather.5.cloned.1.call-update) | async-done | bytes 16777232 | tf_op jit(solution)/shard_map/all_gather | solution.py:270
  210.6 5.6 %multiply_convert_fusion.1 = (bf16[512,2048]{1,0:T(8,128)(2,1)S(1)}, f32[512,2048]{1,0:T(8,128)S(1)}) fusion(bf16[512,1024]{1,0:T(8,128)(2,1)} %copy-done.18, bf16[2,1024,4096]{2,1,0:T(8,128)(2,1)} %bitcast.160), kind=kOutput, calls=%fused_computation.69 | convolution fusion | flops 2156920832 | bytes 11534336 | tf_op jit(solution)/shard_map/dot_general | solution.py:27
  216.3 2.0 copy-done.34
  218.3 4.6 multiply_convert_fusion
  223.0 2.7 convolution_convert_fusion.4
  225.6 2.7 convolution_convert_fusion.5
  228.4 6.9 %fusion.13 = bf16[512,2048]{1,0:T(8,128)(2,1)S(1)} fusion(f32[512,2048]{1,0:T(8,128)} %get-tuple-element.47, bf16[2,1024,4096]{2,1,0:T(8,128)(2,1)S(1)} %bitcast.162, f32[512]{0:T(512)S(1)} %add_divide_fusion, bf16[512,1024]{1,0:T(8,128)(2,1)S(1)} %copy-done.3, pred[512]{0:T(512)(128)(4,1)S(1)} %compare_and_fusion), kind=kOutput, calls=%fused_computation.42 | convolution fusion | flops 2170552320 | bytes 11536896 | tf_op jit(solution)/shard_map/dot_general | solution.py:27
  235.3 4.6 fusion.6
  239.9 2.8 convolution_convert_fusion.6
  242.7 2.7 convolution_convert_fusion.7
  245.5 2.4 fusion.31
  247.8 3.7 fusion.28
  251.5 2.7 add_add_fusion.2
  254.2 5.7 %multiply_reduce_fusion = (f32[1024]{0:T(1024)S(1)}, f32[512]{0:T(512)S(1)}, f32[512]{0:T(512)S(1)}, bf16[512,1024]{1,0:T(8,128)(2,1)}, f32[512,1024]{1,0:T(8,128)S(1)}) fusion(f32[512]{0:T(512)S(1)} %fusion.97, f32[512,1024]{1,0:T(8,128)S(1)} %get-tuple-element.43, bf16[512,1024]{1,0:T(8,128)(2,1)S(1)} %gather_fusion, ...), kind=kOutput, calls=%fused_computation.117 | convolution fusion | flops 2156394496 | bytes 17842688 | tf_op jit(solution)/shard_map/dot_general | solution.py:37
  261.2 2.7 convolution_convert_fusion.18.d_ref
  263.9 2.8 convolution_convert_fusion.19.d_ref
  266.7 1.6 convolution_convert_fusion.10
  268.3 1.3 fusion.63
  270.9 10.1 %attend_back.3 = bf16[512,1536]{1,0:T(8,128)(2,1)} custom-call(s32[1,512]{1,0:T(1,128)} %bitcast.134, s32[512,1]{1,0:T(8,128)} %copy.41.seg_column_ref, bf16[512,1536]{1,0:T(8,128)(2,1)} %convolution_convert_fusion.8.q_ref.k_ref.v_ref, bf16[512,1536]{1,0:T(8,128)(2,1)} %convolution_convert_fusion.8.q_ref.k_ref.v_ref, ...), custom_call_target="tpu_custom_call" | custom-call | tf_op jit(solution)/shard_map/attend_back/pallas_call | solution.py:134
  281.0 10.1 %attend_back.2 = bf16[512,1536]{1,0:T(8,128)(2,1)} custom-call(s32[1,512]{1,0:T(1,128)} %bitcast.135, s32[512,1]{1,0:T(8,128)} %copy.41.seg_column_ref, bf16[512,1536]{1,0:T(8,128)(2,1)} %convolution_convert_fusion.9.q_ref.k_ref.v_ref, bf16[512,1536]{1,0:T(8,128)(2,1)} %convolution_convert_fusion.9.q_ref.k_ref.v_ref, ...), custom_call_target="tpu_custom_call" | custom-call | tf_op jit(solution)/shard_map/attend_back/pallas_call | solution.py:134
  291.1 2.7 fusion.41
  299.1 5.1 fusion.36
  304.6 2.9 add_convert_fusion
  307.6 6.5 %fusion.47 = (f32[1024]{0:T(1024)S(1)}, f32[512]{0:T(512)S(1)}, f32[1024]{0:T(1024)S(1)}, f32[512,1024]{1,0:T(8,128)}) fusion(f32[512]{0:T(512)S(1)} %fusion.96, bf16[512,1024]{1,0:T(8,128)(2,1)S(1)} %gather_fusion, pred[512]{0:T(512)(128)(4,1)S(1)} %compare_and_fusion, f32[1024]{0:T(1024)S(1)} %bitcast.155, f32[512]{0:T(512)S(1)} %get-tuple-element.50, ...), kind=kOutput, calls=%fused_computation.106 | convolution fusion | flops 1616377344 | bytes 9980416 | tf_op jit(solution)/shard_map/dot_general | solution.py:37
  315.4 1.5 collective-permute-start.15
  316.9 3.9 collective-permute-done.15
  321.0 3.8 add_convert_fusion.4
  325.5 3.3 add_convert_fusion.1
  328.9 1.9 collective-permute-start.10
  330.8 1.3 fusion.65
  332.3 3.8 collective-permute-done.17
  336.9 2.9 add_convert_fusion.2
  342.0 56.5 %collective-permute-done.10 = bf16[256,2048]{1,0:T(8,128)(2,1)S(1)} collective-permute-done((bf16[256,2048]{1,0:T(8,128)(2,1)S(1)}, bf16[256,2048]{1,0:T(8,128)(2,1)S(1)}, u32[]{:S(2)}, u32[]{:S(2)}) %collective-permute-start.10) | collective-permute-done | bytes 1048608 | tf_op jit(solution)/shard_map/ppermute | solution.py:188
  398.5 1.4 add_convert_fusion.7
  399.9 2.4 collective-permute-start.11
  403.5 1.3 copy-done.7
  405.9 1.8 collective-permute-start.4
  407.7 2.5 fusion.52.rows_ref
  410.2 11.2 %place_rows.3 = bf16[4096,1024]{1,0:T(8,128)(2,1)} custom-call(s32[1,512]{1,0:T(1,128)} %copy-done.28, bf16[4096,1024]{1,0:T(8,128)(2,1)} %whole_ref.3, bf16[512,1024]{1,0:T(8,128)(2,1)} %fusion.52.rows_ref), custom_call_target="tpu_custom_call" | custom-call | tf_op jit(solution)/shard_map/place_rows/pallas_call | solution.py:219
  421.4 11.4 %place_rows.2 = bf16[4096,1024]{1,0:T(8,128)(2,1)} custom-call(s32[1,512]{1,0:T(1,128)} %copy-done.28, bf16[4096,1024]{1,0:T(8,128)(2,1)} %whole_ref.2, bf16[512,1024]{1,0:T(8,128)(2,1)} %get-tuple-element.32.rows_ref), custom_call_target="tpu_custom_call" | custom-call | tf_op jit(solution)/shard_map/place_rows/pallas_call | solution.py:219
  432.8 11.8 %collective-permute-done.8 = bf16[256,2048]{1,0:T(8,128)(2,1)} collective-permute-done((bf16[256,2048]{1,0:T(8,128)(2,1)}, bf16[256,2048]{1,0:T(8,128)(2,1)}, u32[]{:S(2)}, u32[]{:S(2)}) %collective-permute-start.8) | collective-permute-done | bytes 1048608 | tf_op jit(solution)/shard_map/ppermute | solution.py:188
  444.7 2.1 add_convert_fusion.6
  446.8 1.9 collective-permute-start.12
  448.7 18.1 %collective-permute-done.4 = bf16[256,2048]{1,0:T(8,128)(2,1)} collective-permute-done((bf16[256,2048]{1,0:T(8,128)(2,1)}, bf16[256,2048]{1,0:T(8,128)(2,1)}, u32[]{:S(2)}, u32[]{:S(2)}) %collective-permute-start.4) | collective-permute-done | bytes 1048608 | tf_op jit(solution)/shard_map/ppermute | solution.py:188
  466.8 1.6 add_convert_fusion.9
  468.5 1.7 collective-permute-start.5
  470.7 12.7 %collective-permute-done.12 = bf16[128,2048]{1,0:T(8,128)(2,1)S(1)} collective-permute-done((bf16[128,2048]{1,0:T(8,128)(2,1)S(1)}, bf16[128,2048]{1,0:T(8,128)(2,1)S(1)}, u32[]{:S(2)}, u32[]{:S(2)}) %collective-permute-start.12) | collective-permute-done | bytes 524320 | tf_op jit(solution)/shard_map/ppermute | solution.py:188
  483.6 11.0 %collective-permute-done.5 = bf16[128,2048]{1,0:T(8,128)(2,1)S(1)} collective-permute-done((bf16[128,2048]{1,0:T(8,128)(2,1)S(1)}, bf16[128,2048]{1,0:T(8,128)(2,1)S(1)}, u32[]{:S(2)}, u32[]{:S(2)}) %collective-permute-start.5) | collective-permute-done | bytes 524320 | tf_op jit(solution)/shard_map/ppermute | solution.py:188
  494.8 5.4 %collective-permute-done.13 = bf16[64,2048]{1,0:T(8,128)(2,1)S(1)} collective-permute-done((bf16[64,2048]{1,0:T(8,128)(2,1)S(1)}, bf16[64,2048]{1,0:T(8,128)(2,1)S(1)}, u32[]{:S(2)}, u32[]{:S(2)}) %collective-permute-start.13) | collective-permute-done | bytes 262176 | tf_op jit(solution)/shard_map/ppermute | solution.py:188
  501.1 4.7 collective-permute-done.6
  506.6 1.7 fusion.109
  (186 shorter events, 28.2 us)
Async XLA Ops:
  7.2 7.7 %copy-start = (s32[2,4096]{1,0:T(2,128)S(1)}, s32[2,4096]{1,0:T(2,128)}, u32[]{:S(2)}) copy-start(s32[2,4096]{1,0:T(2,128)} %param.17) | copy-start | bytes 98308
  7.2 87.0 %all-gather.3.cloned.1.call-start = ((), (), s32[]{:S(2)}) async-start(), calls=%async_computation.1 | async-start | bytes 9191424 | tf_op jit(solution)/shard_map/all_gather | solution.py:268
  12.2 198.5 %all-gather.5.cloned.1.call-start = ((), (), s32[]{:S(2)}) async-start(), calls=%async_computation.2 | async-start | bytes 17301504 | tf_op jit(solution)/shard_map/all_gather | solution.py:270
  14.1 492.5 %reduce-scatter.2.cloned.1.call-start = ((), (), s32[]{:S(2)}) async-start(), calls=%async_computation.3 | async-start | bytes 4456448 | tf_op jit(solution)/shard_map/reduce_scatter | solution.py:162
  14.9 16.6 %copy-start.28 = (s32[1,512]{1,0:T(1,128)}, s32[1,512]{1,0:T(1,128)S(1)}, u32[]{:S(2)}) copy-start(s32[1,512]{1,0:T(1,128)S(1)} %constant_dynamic-slice_fusion.1.index_ref) | copy-start | bytes 6148
  15.2 8.1 %copy-start.29 = (s32[512]{0:T(512)}, s32[512]{0:T(512)S(1)}, u32[]{:S(2)}) copy-start(s32[512]{0:T(512)S(1)} %convert_reduce_fusion.1) | copy-start | bytes 6148
  95.4 27.2 %copy-start.32 = (f32[1,1024]{1,0:T(1,128)}, f32[1,1024]{1,0:T(1,128)S(1)}, u32[]{:S(2)}) copy-start(f32[1,1024]{1,0:T(1,128)S(1)} %get-tuple-element.37) | copy-start | bytes 12292
  112.9 7.7 %copy-start.20 = (bf16[512,512]{1,0:T(8,128)(2,1)S(1)}, bf16[512,512]{1,0:T(8,128)(2,1)}, u32[]{:S(2)}) copy-start(bf16[512,512]{1,0:T(8,128)(2,1)} %get-tuple-element.18) | copy-start | bytes 1572868
  125.5 2.5 copy-start.18
  128.1 2.4 copy-start.2
  210.6 5.7 %copy-start.19 = (bf16[512,1024]{1,0:T(8,128)(2,1)S(1)}, bf16[512,1024]{1,0:T(8,128)(2,1)}, u32[]{:S(2)}) copy-start(bf16[512,1024]{1,0:T(8,128)(2,1)} %copy-done.18) | copy-start | bytes 3145732
  210.6 7.7 %copy-start.34 = (bf16[2048,4096]{1,0:T(8,128)(2,1)S(1)}, bf16[2048,4096]{1,0:T(8,128)(2,1)}, u32[]{:S(2)}) copy-start(bf16[2048,4096]{1,0:T(8,128)(2,1)} %all-gather.5.cloned.1.call-done) | copy-start | bytes 50331652
  218.3 27.1 %copy-start.39 = (bf16[512,2048]{1,0:T(8,128)(2,1)}, bf16[512,2048]{1,0:T(8,128)(2,1)S(1)}, u32[]{:S(2)}) copy-start(bf16[512,2048]{1,0:T(8,128)(2,1)S(1)} %get-tuple-element.44) | copy-start | bytes 6291460
  218.3 4.6 copy-start.43
  223.0 28.6 %copy-start.41 = (bf16[512,2048]{1,0:T(8,128)(2,1)}, bf16[512,2048]{1,0:T(8,128)(2,1)S(1)}, u32[]{:S(2)}) copy-start(bf16[512,2048]{1,0:T(8,128)(2,1)S(1)} %get-tuple-element.46) | copy-start | bytes 6291460
  225.6 2.7 copy-start.3
  235.2 19.0 %copy-start.9 = (bf16[512,2048]{1,0:T(8,128)(2,1)}, bf16[512,2048]{1,0:T(8,128)(2,1)S(1)}, u32[]{:S(2)}) copy-start(bf16[512,2048]{1,0:T(8,128)(2,1)S(1)} %fusion.13) | copy-start | bytes 6291460
  235.3 4.7 copy-start.26
  239.9 7.9 %copy-start.11 = (bf16[512,2048]{1,0:T(8,128)(2,1)}, bf16[512,2048]{1,0:T(8,128)(2,1)S(1)}, u32[]{:S(2)}) copy-start(bf16[512,2048]{1,0:T(8,128)(2,1)S(1)} %fusion.6) | copy-start | bytes 6291460
  260.0 4.0 copy-start.5
  266.7 1.6 copy-start.35
  266.7 2.9 copy-start.21
  268.3 2.6 copy-start.37
  291.1 2.7 copy-start.17
  291.1 2.7 copy-start.45
  295.1 1.5 copy-start.36
  295.1 1.5 copy-start.38
  295.1 1.9 copy-start.16
  295.7 8.9 %collective-permute-start = (bf16[2,512,2048]{2,1,0:T(8,128)(2,1)S(1)}, bf16[2,512,2048]{2,1,0:T(8,128)(2,1)S(1)}, u32[]{:S(2)}, u32[]{:S(2)}) collective-permute-start(bf16[2,512,2048]{2,1,0:T(8,128)(2,1)S(1)} %maximum_maximum_fusion), channel_id=1, source_target_pairs={{0,2},{2,0},{1,3},{3,1},{4,6},{6,4},{5,7},{7,5},{8,10},{10,8},{9,1... | collective-permute-start | bytes 12582920 | tf_op jit(solution)/shard_map/ppermute | solution.py:154
  296.0 29.5 %collective-permute-start.9 = (bf16[512,2048]{1,0:T(8,128)(2,1)}, bf16[512,2048]{1,0:T(8,128)(2,1)}, u32[]{:S(2)}, u32[]{:S(2)}) collective-permute-start(bf16[512,2048]{1,0:T(8,128)(2,1)} %convolution_convert_fusion.4), channel_id=1, source_target_pairs={{0,2},{2,0},{1,3},{3,1},{4,6},{6,4},{5,7},{7,5},{8,10},{10,8},{9,1... | collective-permute-start | bytes 6291464 | tf_op jit(solution)/shard_map/ppermute | solution.py:154
  296.3 24.7 %collective-permute-start.2 = (bf16[512,2048]{1,0:T(8,128)(2,1)}, bf16[512,2048]{1,0:T(8,128)(2,1)}, u32[]{:S(2)}, u32[]{:S(2)}) collective-permute-start(bf16[512,2048]{1,0:T(8,128)(2,1)} %convolution_convert_fusion.6), channel_id=1, source_target_pairs={{0,2},{2,0},{1,3},{3,1},{4,6},{6,4},{5,7},{7,5},{8,10},{10,8},{9,1... | collective-permute-start | bytes 6291464 | tf_op jit(solution)/shard_map/ppermute | solution.py:154
  299.0 5.1 copy-start.22
  314.1 1.2 collective-permute-start.14
  314.4 22.5 %collective-permute-start.7 = (bf16[512,2048]{1,0:T(8,128)(2,1)}, bf16[512,2048]{1,0:T(8,128)(2,1)}, u32[]{:S(2)}, u32[]{:S(2)}) collective-permute-start(bf16[512,2048]{1,0:T(8,128)(2,1)} %convolution_convert_fusion.5), channel_id=1, source_target_pairs={{0,2},{2,0},{1,3},{3,1},{4,6},{6,4},{5,7},{7,5},{8,10},{10,8},{9,1... | collective-permute-start | bytes 6291464 | tf_op jit(solution)/shard_map/ppermute | solution.py:154
  315.4 5.5 %collective-permute-start.15 = (f32[3,1024]{1,0:T(4,128)S(1)}, f32[3,1024]{1,0:T(4,128)S(1)}, u32[]{:S(2)}, u32[]{:S(2)}) collective-permute-start(f32[3,1024]{1,0:T(4,128)S(1)} %fusion.98), channel_id=1, source_target_pairs={{0,1},{1,0},{2,3},{3,2},{4,5},{5,4},{6,7},{7,6},{8,9},{9,8},{10,11... | collective-permute-start | bytes 36872 | tf_op jit(solution)/shard_map/ppermute | solution.py:184
  316.9 85.4 %collective-permute-start.1 = (bf16[512,2048]{1,0:T(8,128)(2,1)}, bf16[512,2048]{1,0:T(8,128)(2,1)S(1)}, u32[]{:S(2)}, u32[]{:S(2)}) collective-permute-start(bf16[512,2048]{1,0:T(8,128)(2,1)} %convolution_convert_fusion.7), channel_id=1, source_target_pairs={{0,2},{2,0},{1,3},{3,1},{4,6},{6,4},{5,7},{7,5},{8,10},{10,8},{9,1... | collective-permute-start | bytes 6291464 | tf_op jit(solution)/shard_map/ppermute | solution.py:154
  320.8 4.6 copy-start.40
  320.9 4.6 copy-start.42
  320.9 4.6 copy-start.44
  320.9 11.3 %collective-permute-start.16 = (f32[3,1024]{1,0:T(4,128)S(1)}, f32[3,1024]{1,0:T(4,128)S(1)}, u32[]{:S(2)}, u32[]{:S(2)}) collective-permute-start(f32[3,1024]{1,0:T(4,128)S(1)} %fusion.133), channel_id=1, source_target_pairs={{0,4},{4,0},{8,12},{12,8},{16,20},{20,16},{24,28},{28,24},{1,5},{5... | collective-permute-start | bytes 36872 | tf_op jit(solution)/shard_map/ppermute | solution.py:188
  324.8 6.0 %copy-start.10 = (bf16[512,2048]{1,0:T(8,128)(2,1)S(1)}, bf16[512,2048]{1,0:T(8,128)(2,1)}, u32[]{:S(2)}) copy-start(bf16[512,2048]{1,0:T(8,128)(2,1)} %copy-done.9) | copy-start | bytes 6291460
  324.8 6.0 %copy-start.12 = (bf16[512,2048]{1,0:T(8,128)(2,1)S(1)}, bf16[512,2048]{1,0:T(8,128)(2,1)}, u32[]{:S(2)}) copy-start(bf16[512,2048]{1,0:T(8,128)(2,1)} %copy-done.11) | copy-start | bytes 6291460
  324.8 6.0 %copy-start.27 = (bf16[512,1024]{1,0:T(8,128)(2,1)S(1)}, bf16[512,1024]{1,0:T(8,128)(2,1)}, u32[]{:S(2)}) copy-start(bf16[512,1024]{1,0:T(8,128)(2,1)} %convolution_convert_fusion.13) | copy-start | bytes 3145732
  324.8 77.5 %collective-permute-start.3 = (bf16[512,2048]{1,0:T(8,128)(2,1)S(1)}, bf16[512,2048]{1,0:T(8,128)(2,1)S(1)}, u32[]{:S(2)}, u32[]{:S(2)}) collective-permute-start(bf16[512,2048]{1,0:T(8,128)(2,1)S(1)} %add_convert_fusion.4), channel_id=1, source_target_pairs={{0,1},{1,0},{2,3},{3,2},{4,5},{5,4},{6,7},{7,6},{8,9},{9,8},{10,11... | collective-permute-start | bytes 6291464 | tf_op jit(solution)/shard_map/ppermute | solution.py:184
  328.9 3.4 copy-start.31
  328.9 69.6 %collective-permute-start.10 = (bf16[256,2048]{1,0:T(8,128)(2,1)S(1)}, bf16[256,2048]{1,0:T(8,128)(2,1)S(1)}, u32[]{:S(2)}, u32[]{:S(2)}) collective-permute-start(bf16[256,2048]{1,0:T(8,128)(2,1)S(1)} %slice.209), channel_id=1, source_target_pairs={{0,4},{4,0},{8,12},{12,8},{16,20},{20,16},{24,28},{28,24},{1,5},{5... | collective-permute-start | bytes 3145736 | tf_op jit(solution)/shard_map/ppermute | solution.py:188
  332.2 3.9 collective-permute-start.17
  336.1 96.7 %collective-permute-start.18 = (f32[3,1024]{1,0:T(4,128)S(1)}, f32[3,1024]{1,0:T(4,128)S(1)}, u32[]{:S(2)}, u32[]{:S(2)}) collective-permute-start(f32[3,1024]{1,0:T(4,128)S(1)} %add.274), channel_id=1, source_target_pairs={{0,16},{4,20},{8,24},{12,28},{16,0},{20,4},{24,8},{28,12},{1,17},{... | collective-permute-start | bytes 36872 | tf_op jit(solution)/shard_map/ppermute | solution.py:188
  339.9 62.4 %copy-start.14 = (bf16[512,2048]{1,0:T(8,128)(2,1)}, bf16[512,2048]{1,0:T(8,128)(2,1)S(1)}, u32[]{:S(2)}) copy-start(bf16[512,2048]{1,0:T(8,128)(2,1)S(1)} %add_convert_fusion.2) | copy-start | bytes 6291460
  341.1 103.5 %collective-permute-start.8 = (bf16[256,2048]{1,0:T(8,128)(2,1)}, bf16[256,2048]{1,0:T(8,128)(2,1)}, u32[]{:S(2)}, u32[]{:S(2)}) collective-permute-start(bf16[256,2048]{1,0:T(8,128)(2,1)} %slice.207), channel_id=1, source_target_pairs={{0,4},{4,0},{8,12},{12,8},{16,20},{20,16},{24,28},{28,24},{1,5},{5... | collective-permute-start | bytes 3145736 | tf_op jit(solution)/shard_map/ppermute | solution.py:188
  399.9 7.8 %copy-start.4 = (bf16[512,1024]{1,0:T(8,128)(2,1)S(1)}, bf16[512,1024]{1,0:T(8,128)(2,1)}, u32[]{:S(2)}) copy-start(bf16[512,1024]{1,0:T(8,128)(2,1)} %gather_fusion.1) | copy-start | bytes 3145732
  399.9 7.8 %copy-start.6 = (f32[512,1024]{1,0:T(8,128)S(1)}, f32[512,1024]{1,0:T(8,128)}, u32[]{:S(2)}) copy-start(f32[512,1024]{1,0:T(8,128)} %copy-done.5) | copy-start | bytes 6291460
  399.9 7.8 %copy-start.13 = (f32[512,1024]{1,0:T(8,128)S(1)}, f32[512,1024]{1,0:T(8,128)}, u32[]{:S(2)}) copy-start(f32[512,1024]{1,0:T(8,128)} %get-tuple-element.49) | copy-start | bytes 6291460
  399.9 7.8 %copy-start.33 = (f32[1,1024]{1,0:T(1,128)S(1)}, f32[1,1024]{1,0:T(1,128)}, u32[]{:S(2)}) copy-start(f32[1,1024]{1,0:T(1,128)} %copy-done.32) | copy-start | bytes 12292
  399.9 44.8 %collective-permute-start.11 = (bf16[256,2048]{1,0:T(8,128)(2,1)}, bf16[256,2048]{1,0:T(8,128)(2,1)}, u32[]{:S(2)}, u32[]{:S(2)}) collective-permute-start(bf16[256,2048]{1,0:T(8,128)(2,1)} %add_convert_fusion.7), channel_id=1, source_target_pairs={{0,1},{1,0},{2,3},{3,2},{4,5},{5,4},{6,7},{7,6},{8,9},{9,8},{10,11... | collective-permute-start | bytes 3145736 | tf_op jit(solution)/shard_map/ppermute | solution.py:184
  403.5 1.4 copy-start.7
  405.9 60.9 %collective-permute-start.4 = (bf16[256,2048]{1,0:T(8,128)(2,1)}, bf16[256,2048]{1,0:T(8,128)(2,1)}, u32[]{:S(2)}, u32[]{:S(2)}) collective-permute-start(bf16[256,2048]{1,0:T(8,128)(2,1)} %slice.200), channel_id=1, source_target_pairs={{0,4},{4,0},{8,12},{12,8},{16,20},{20,16},{24,28},{28,24},{1,5},{5... | collective-permute-start | bytes 3145736 | tf_op jit(solution)/shard_map/ppermute | solution.py:188
  421.4 23.3 %copy-start.15 = (bf16[512,2048]{1,0:T(8,128)(2,1)S(1)}, bf16[512,2048]{1,0:T(8,128)(2,1)}, u32[]{:S(2)}) copy-start(bf16[512,2048]{1,0:T(8,128)(2,1)} %copy-done.14) | copy-start | bytes 6291460
  432.8 34.1 %copy-start.8 = (bf16[512,2048]{1,0:T(8,128)(2,1)S(1)}, bf16[512,2048]{1,0:T(8,128)(2,1)}, u32[]{:S(2)}) copy-start(bf16[512,2048]{1,0:T(8,128)(2,1)} %copy-done.7) | copy-start | bytes 6291460
  446.8 36.6 %collective-permute-start.12 = (bf16[128,2048]{1,0:T(8,128)(2,1)S(1)}, bf16[128,2048]{1,0:T(8,128)(2,1)S(1)}, u32[]{:S(2)}, u32[]{:S(2)}) collective-permute-start(bf16[128,2048]{1,0:T(8,128)(2,1)S(1)} %slice.211), channel_id=1, source_target_pairs={{0,16},{4,20},{8,24},{12,28},{16,0},{20,4},{24,8},{28,12},{1,17},{... | collective-permute-start | bytes 1572872 | tf_op jit(solution)/shard_map/ppermute | solution.py:188
  466.8 41.5 %copy-start.1 = (s32[2,4096]{1,0:T(2,128)S(1)}, s32[2,4096]{1,0:T(2,128)}, u32[]{:S(2)}) copy-start(s32[2,4096]{1,0:T(2,128)} %param.17) | copy-start | bytes 98308
  468.5 26.1 %collective-permute-start.5 = (bf16[128,2048]{1,0:T(8,128)(2,1)S(1)}, bf16[128,2048]{1,0:T(8,128)(2,1)S(1)}, u32[]{:S(2)}, u32[]{:S(2)}) collective-permute-start(bf16[128,2048]{1,0:T(8,128)(2,1)S(1)} %slice.202), channel_id=1, source_target_pairs={{0,16},{4,20},{8,24},{12,28},{16,0},{20,4},{24,8},{28,12},{1,17},{... | collective-permute-start | bytes 1572872 | tf_op jit(solution)/shard_map/ppermute | solution.py:188
  483.5 16.7 %collective-permute-start.13 = (bf16[64,2048]{1,0:T(8,128)(2,1)S(1)}, bf16[64,2048]{1,0:T(8,128)(2,1)S(1)}, u32[]{:S(2)}, u32[]{:S(2)}) collective-permute-start(bf16[64,2048]{1,0:T(8,128)(2,1)S(1)} %slice.213), channel_id=1, source_target_pairs={{0,8},{4,12},{8,0},{12,4},{16,24},{20,28},{24,16},{28,20},{1,9},{5... | collective-permute-start | bytes 786440 | tf_op jit(solution)/shard_map/ppermute | solution.py:188
  494.8 11.0 %collective-permute-start.6 = (bf16[64,2048]{1,0:T(8,128)(2,1)S(1)}, bf16[64,2048]{1,0:T(8,128)(2,1)S(1)}, u32[]{:S(2)}, u32[]{:S(2)}) collective-permute-start(bf16[64,2048]{1,0:T(8,128)(2,1)S(1)} %slice.204), channel_id=1, source_target_pairs={{0,8},{4,12},{8,0},{12,4},{16,24},{20,28},{24,16},{28,20},{1,9},{5... | collective-permute-start | bytes 786440 | tf_op jit(solution)/shard_map/ppermute | solution.py:188
  (4 other events, 3.5 us)
Sparse Core Ops, SparseCore 0:
  12.3 81.8 all-gather.2
  97.6 113.0 all-gather.4
  307.7 128.8 reduce-scatter.1

commit v3 on v2

--- a/solution.py
+++ b/solution.py
@@ -232,11 +232,12 @@
 
 def sum_everywhere(values):
     values = values + swap_cores(values)
+    values = values + swap_chips(values, 1)
     values = values + swap_sides(values)
-    count, bit = lax.axis_size("chips"), 1
-    while bit < count:
+    bit = lax.axis_size("chips") // 2
+    while bit > 1:
         values = values + swap_chips(values, bit)
-        bit *= 2
+        bit //= 2
     return values
 
 
@@ -349,6 +350,7 @@
     ]
     sum_attn = reduce_near(grad_attn)
 
+    d_qkv, hidden_act = lax.optimization_barrier((d_qkv, hidden_act))
     branch_mlp = sum(contract_last(hidden_act[t], full_down[t]) for t in range(sides))
     branch_total = branch_attn + branch_mlp
     updated = input_float + gate[:, None] * branch_total

time: 525 us -> 521 us (level)
  transfers between devices with their start and end apart: 22 -> 22, of which waited for: 12 -> 12; matrix products, arithmetic and copies ran while one was open for 17% -> 19% of each run, Pallas kernels for 7% -> 7%
where the time goes in v3:
time: 521 us; the launch traced here: 511 us
  waiting for transfers between devices  265 us (51%)
  matrix products  107 us (21%)
  Pallas kernels  58.5 us (11%)
  local copies, waits for them, and re-layouts  29.7 us (6%)
  other arithmetic  20.4 us (4%)
  starting transfers between devices  15.1 us (3%)
  between operations  14.9 us (3%)
    ppermute x10, waiting for transfers between devices, swap_chips(): lax.ppermute(values, 'chips', [(i, i ^ bit) for i in range(lax.axis_size(...  125 us
    all_gather x1, waiting for transfers between devices, block(): far = lax.all_gather(far, ALL, axis=0, tiled=True).reshape(sides, width, -1)  77.3 us
    all_gather x1, waiting for transfers between devices, block(): lax.all_gather(near, ALL, axis=0, tiled=True).reshape(sides, width, -1)  62.3 us
    dot_general x12, matrix products, plain_dot(): return jnp.dot(left, right, preferred_element_type=jnp.float32)  43.3 us
    dot_general x8, matrix products, contract_last(): lax.dot_general(left, right, (((1,), (1,)), ((), ())), preferred_element_...  32.2 us
    dot_general x16, matrix products, contract_rows(): lax.dot_general(left, right, (((0,), (0,)), ((), ())), preferred_element_...  31.7 us
    pallas_call x2, Pallas kernels, place(): pl.pallas_call(kernel, grid=(tokens // step,), out_shape=jax.ShapeDtypeSt...  22.5 us
    pallas_call x2, Pallas kernels, attend_back(): pl.pallas_call(kernel, grid=(pairs,), out_shape=jax.ShapeDtypeStruct((row...  20.4 us
  transfers between devices with their start and end apart: 22, of which 12 were waited for; matrix products, arithmetic and copies ran while one was open for 19% of the time, Pallas kernels for 7%

profile of v3, /device:TPU:0, one launch (start us, length us, event | category | flops | bytes accessed | tf_op | source)
XLA Modules:
  0.0 511.0 jit_solution(14511279922993163960)
XLA Ops:
  12.2 1.9 pad_maximum_fusion
  16.1 7.2 %gather_fusion = bf16[512,1024]{1,0:T(8,128)(2,1)S(1)} fusion(bf16[4096,1024]{1,0:T(8,128)(2,1)} %whole_ref.2, s32[1024]{0:T(1024)S(1)} %pad_clamp_fusion), kind=kCustom, calls=%fused_computation.clone | custom fusion | bytes 2099200 | tf_op jit(solution)/shard_map/jit(_take)/gather | solution.py:281
  23.3 8.1 %gather_fusion.1 = bf16[512,1024]{1,0:T(8,128)(2,1)} fusion(bf16[4096,1024]{1,0:T(8,128)(2,1)} %whole_ref.3, s32[1024]{0:T(1024)S(1)} %pad_clamp_fusion), kind=kCustom, calls=%fused_computation.1.clone | custom fusion | bytes 2099200 | tf_op jit(solution)/shard_map/jit(_take)/gather | solution.py:282
  31.9 62.3 %all-gather.3.cloned.1.call-done = bf16[2048,2176]{1,0:T(8,128)(2,1)} async-done(((bf16[64,2176]{1,0:T(8,128)(2,1)}), bf16[2048,2176]{1,0:T(8,128)(2,1)}) %all-gather.3.cloned.1.call-update) | async-done | bytes 8912912 | tf_op jit(solution)/shard_map/all_gather | solution.py:269
  95.4 5.0 convolution_convert_fusion.9.q_ref.k_ref.v_ref
  100.4 7.5 %attend.2 = (bf16[512,512]{1,0:T(8,128)(2,1)}, f32[8,1,512]{2,1,0:T(1,128)}) custom-call(s32[1,512]{1,0:T(1,128)} %bitcast.134, s32[512,1]{1,0:T(8,128)} %copy.41.seg_column_ref, bf16[512,1536]{1,0:T(8,128)(2,1)} %convolution_convert_fusion.9.q_ref.k_ref.v_ref, bf16[512,1536]{1,0:T(8,128)(2,1)} %convolution_convert_fusion.9.q_ref.k_ref.v_ref, ...), custom_call_target="tpu_custom_call" | custom-call | tf_op jit(solution)/shard_map/attend/pallas_call | solution.py:79
  107.9 5.0 convolution_convert_fusion.8.q_ref.k_ref.v_ref
  113.0 8.0 %attend.3 = (bf16[512,512]{1,0:T(8,128)(2,1)}, f32[8,1,512]{2,1,0:T(1,128)}) custom-call(s32[1,512]{1,0:T(1,128)} %bitcast.135, s32[512,1]{1,0:T(8,128)} %copy.41.seg_column_ref, bf16[512,1536]{1,0:T(8,128)(2,1)} %convolution_convert_fusion.8.q_ref.k_ref.v_ref, bf16[512,1536]{1,0:T(8,128)(2,1)} %convolution_convert_fusion.8.q_ref.k_ref.v_ref, ...), custom_call_target="tpu_custom_call" | custom-call | tf_op jit(solution)/shard_map/attend/pallas_call | solution.py:79
  121.0 2.0 fusion.64
  123.0 2.4 multiply_reduce_fusion.2
  125.9 2.5 convolution_convert_fusion.11
  128.4 2.4 convolution_convert_fusion.13
  130.9 2.5 convolution_convert_fusion.12
  133.4 77.3 %all-gather.5.cloned.1.call-done = bf16[2048,4096]{1,0:T(8,128)(2,1)} async-done(((bf16[64,4096]{1,0:T(8,128)(2,1)}), bf16[2048,4096]{1,0:T(8,128)(2,1)}) %all-gather.5.cloned.1.call-update) | async-done | bytes 16777232 | tf_op jit(solution)/shard_map/all_gather | solution.py:271
  210.7 5.8 %multiply_convert_fusion.1 = (bf16[512,2048]{1,0:T(8,128)(2,1)S(1)}, f32[512,2048]{1,0:T(8,128)S(1)}) fusion(bf16[512,1024]{1,0:T(8,128)(2,1)} %copy-done.19, bf16[2,1024,4096]{2,1,0:T(8,128)(2,1)} %bitcast.162), kind=kOutput, calls=%fused_computation.68 | convolution fusion | flops 2156920832 | bytes 11534336 | tf_op jit(solution)/shard_map/dot_general | solution.py:27
  216.4 1.9 copy-done.35
  218.3 3.2 multiply_convert_fusion
  221.5 2.7 convolution_convert_fusion.4
  224.2 2.7 convolution_convert_fusion.5
  226.9 4.6 fusion.13
  231.6 5.1 fusion.6
  236.6 2.7 convolution_convert_fusion.6
  239.3 2.8 convolution_convert_fusion.7
  242.1 2.4 fusion.30
  244.4 2.9 multiply_reduce_fusion
  248.6 2.8 convolution_convert_fusion.18.d_ref
  251.3 2.8 convolution_convert_fusion.19.d_ref
  254.1 1.6 convolution_convert_fusion.10
  258.3 10.3 %attend_back.3 = bf16[512,1536]{1,0:T(8,128)(2,1)} custom-call(s32[1,512]{1,0:T(1,128)} %bitcast.136, s32[512,1]{1,0:T(8,128)} %copy.41.seg_column_ref, bf16[512,1536]{1,0:T(8,128)(2,1)} %convolution_convert_fusion.8.q_ref.k_ref.v_ref, bf16[512,1536]{1,0:T(8,128)(2,1)} %convolution_convert_fusion.8.q_ref.k_ref.v_ref, ...), custom_call_target="tpu_custom_call" | custom-call | tf_op jit(solution)/shard_map/attend_back/pallas_call | solution.py:134
  268.5 10.2 %attend_back.2 = bf16[512,1536]{1,0:T(8,128)(2,1)} custom-call(s32[1,512]{1,0:T(1,128)} %bitcast.137, s32[512,1]{1,0:T(8,128)} %copy.41.seg_column_ref, bf16[512,1536]{1,0:T(8,128)(2,1)} %convolution_convert_fusion.9.q_ref.k_ref.v_ref, bf16[512,1536]{1,0:T(8,128)(2,1)} %convolution_convert_fusion.9.q_ref.k_ref.v_ref, ...), custom_call_target="tpu_custom_call" | custom-call | tf_op jit(solution)/shard_map/attend_back/pallas_call | solution.py:134
  278.7 2.7 fusion.41
  284.8 4.8 fusion.28
  289.6 6.2 %fusion.49 = (f32[512]{0:T(512)S(1)}, bf16[512,1024]{1,0:T(8,128)(2,1)}) fusion(bf16[512,1024]{1,0:T(8,128)(2,1)S(1)} %copy-done.4, pred[512]{0:T(512)(128)(4,1)S(1)} %compare_and_fusion, f32[512]{0:T(512)S(1)} %get-tuple-element.58, bf16[512,1024]{1,0:T(8,128)(2,1)S(1)} %gather_fusion, f32[512,1024]{1,0:T(8,128)S(1)} %get-tuple-element.51, ...), kind=kOutput, calls=%fused_computation.108 | convolution fusion | flops 2153250304 | bytes 13636096 | tf_op jit(solution)/shard_map/dot_general | solution.py:37
  297.8 5.1 fusion.36
  303.4 2.9 add_convert_fusion
  306.4 6.5 %fusion.47 = (f32[1024]{0:T(1024)S(1)}, f32[512]{0:T(512)S(1)}, f32[1024]{0:T(1024)S(1)}, f32[512,1024]{1,0:T(8,128)}) fusion(f32[512]{0:T(512)S(1)} %fusion.96, bf16[512,1024]{1,0:T(8,128)(2,1)S(1)} %gather_fusion, pred[512]{0:T(512)(128)(4,1)S(1)} %compare_and_fusion, f32[1024]{0:T(1024)S(1)} %bitcast.155, f32[512]{0:T(512)S(1)} %fusion.95, ...), kind=kOutput, calls=%fused_computation.106 | convolution fusion | flops 1616377344 | bytes 9980416 | tf_op jit(solution)/shard_map/dot_general | solution.py:37
  314.1 1.3 collective-permute-start.15
  315.5 3.6 collective-permute-done.15
  319.1 1.4 collective-permute-start.16
  320.5 3.9 add_convert_fusion.4
  325.5 3.5 add_convert_fusion.1
  329.2 1.3 fusion.65
  330.6 1.7 collective-permute-start.17
  332.3 3.0 collective-permute-done.17
  336.1 2.9 add_convert_fusion.2
  340.3 1.7 collective-permute-start.8
  342.0 58.0 %collective-permute-done.10 = bf16[256,2048]{1,0:T(8,128)(2,1)S(1)} collective-permute-done((bf16[256,2048]{1,0:T(8,128)(2,1)S(1)}, bf16[256,2048]{1,0:T(8,128)(2,1)S(1)}, u32[]{:S(2)}, u32[]{:S(2)}) %collective-permute-start.10) | collective-permute-done | bytes 1048608 | tf_op jit(solution)/shard_map/ppermute | solution.py:188
  400.0 1.4 add_convert_fusion.7
  401.4 1.7 collective-permute-start.11
  404.3 1.4 copy-done.8
  406.8 2.5 fusion.52.rows_ref
  409.2 11.2 %place_rows.3 = bf16[4096,1024]{1,0:T(8,128)(2,1)} custom-call(s32[1,512]{1,0:T(1,128)} %copy-done.29, bf16[4096,1024]{1,0:T(8,128)(2,1)} %whole_ref.3, bf16[512,1024]{1,0:T(8,128)(2,1)} %fusion.52.rows_ref), custom_call_target="tpu_custom_call" | custom-call | tf_op jit(solution)/shard_map/place_rows/pallas_call | solution.py:219
  420.4 11.4 %place_rows.2 = bf16[4096,1024]{1,0:T(8,128)(2,1)} custom-call(s32[1,512]{1,0:T(1,128)} %copy-done.29, bf16[4096,1024]{1,0:T(8,128)(2,1)} %whole_ref.2, bf16[512,1024]{1,0:T(8,128)(2,1)} %get-tuple-element.40.rows_ref), custom_call_target="tpu_custom_call" | custom-call | tf_op jit(solution)/shard_map/place_rows/pallas_call | solution.py:219
  431.9 11.6 %collective-permute-done.8 = bf16[256,2048]{1,0:T(8,128)(2,1)} collective-permute-done((bf16[256,2048]{1,0:T(8,128)(2,1)}, bf16[256,2048]{1,0:T(8,128)(2,1)}, u32[]{:S(2)}, u32[]{:S(2)}) %collective-permute-start.8) | collective-permute-done | bytes 1048608 | tf_op jit(solution)/shard_map/ppermute | solution.py:188
  443.4 2.1 add_convert_fusion.6
  445.6 1.8 collective-permute-start.12
  447.4 18.0 %collective-permute-done.4 = bf16[256,2048]{1,0:T(8,128)(2,1)} collective-permute-done((bf16[256,2048]{1,0:T(8,128)(2,1)}, bf16[256,2048]{1,0:T(8,128)(2,1)}, u32[]{:S(2)}, u32[]{:S(2)}) %collective-permute-start.4) | collective-permute-done | bytes 1048608 | tf_op jit(solution)/shard_map/ppermute | solution.py:188
  465.4 1.6 add_convert_fusion.9
  467.1 1.9 collective-permute-start.5
  469.4 12.7 %collective-permute-done.12 = bf16[128,2048]{1,0:T(8,128)(2,1)S(1)} collective-permute-done((bf16[128,2048]{1,0:T(8,128)(2,1)S(1)}, bf16[128,2048]{1,0:T(8,128)(2,1)S(1)}, u32[]{:S(2)}, u32[]{:S(2)}) %collective-permute-start.12) | collective-permute-done | bytes 524320 | tf_op jit(solution)/shard_map/ppermute | solution.py:188
  482.4 10.8 %collective-permute-done.5 = bf16[128,2048]{1,0:T(8,128)(2,1)S(1)} collective-permute-done((bf16[128,2048]{1,0:T(8,128)(2,1)S(1)}, bf16[128,2048]{1,0:T(8,128)(2,1)S(1)}, u32[]{:S(2)}, u32[]{:S(2)}) %collective-permute-start.5) | collective-permute-done | bytes 524320 | tf_op jit(solution)/shard_map/ppermute | solution.py:188
  493.4 2.6 collective-permute-done.13
  496.9 4.6 collective-permute-done.6
  502.4 1.7 fusion.109
  (187 shorter events, 28.3 us)
Async XLA Ops:
  7.2 7.7 %copy-start = (s32[2,4096]{1,0:T(2,128)S(1)}, s32[2,4096]{1,0:T(2,128)}, u32[]{:S(2)}) copy-start(s32[2,4096]{1,0:T(2,128)} %param.17) | copy-start | bytes 98308
  7.2 87.0 %all-gather.3.cloned.1.call-start = ((), (), s32[]{:S(2)}) async-start(), calls=%async_computation.1 | async-start | bytes 9191424 | tf_op jit(solution)/shard_map/all_gather | solution.py:269
  12.2 198.5 %all-gather.5.cloned.1.call-start = ((), (), s32[]{:S(2)}) async-start(), calls=%async_computation.2 | async-start | bytes 17301504 | tf_op jit(solution)/shard_map/all_gather | solution.py:271
  14.1 488.3 %reduce-scatter.2.cloned.1.call-start = ((), (), s32[]{:S(2)}) async-start(), calls=%async_computation.3 | async-start | bytes 4456448 | tf_op jit(solution)/shard_map/reduce_scatter | solution.py:162
  14.9 16.5 %copy-start.29 = (s32[1,512]{1,0:T(1,128)}, s32[1,512]{1,0:T(1,128)S(1)}, u32[]{:S(2)}) copy-start(s32[1,512]{1,0:T(1,128)S(1)} %constant_dynamic-slice_fusion.1.index_ref) | copy-start | bytes 6148
  15.2 8.1 %copy-start.30 = (s32[512]{0:T(512)}, s32[512]{0:T(512)S(1)}, u32[]{:S(2)}) copy-start(s32[512]{0:T(512)S(1)} %convert_reduce_fusion.1) | copy-start | bytes 6148
  31.9 62.3 %copy-start.31 = (f32[512]{0:T(512)}, f32[512]{0:T(512)S(1)}, u32[]{:S(2)}) copy-start(f32[512]{0:T(512)S(1)} %fusion.54) | copy-start | bytes 6148
  95.4 27.6 %copy-start.33 = (f32[1,1024]{1,0:T(1,128)}, f32[1,1024]{1,0:T(1,128)S(1)}, u32[]{:S(2)}) copy-start(f32[1,1024]{1,0:T(1,128)S(1)} %get-tuple-element.47) | copy-start | bytes 12292
  113.0 8.0 %copy-start.21 = (bf16[512,512]{1,0:T(8,128)(2,1)S(1)}, bf16[512,512]{1,0:T(8,128)(2,1)}, u32[]{:S(2)}) copy-start(bf16[512,512]{1,0:T(8,128)(2,1)} %get-tuple-element.22) | copy-start | bytes 1572868
  125.9 2.5 copy-start.19
  128.4 2.5 copy-start.2
  210.6 5.8 %copy-start.20 = (bf16[512,1024]{1,0:T(8,128)(2,1)S(1)}, bf16[512,1024]{1,0:T(8,128)(2,1)}, u32[]{:S(2)}) copy-start(bf16[512,1024]{1,0:T(8,128)(2,1)} %copy-done.19) | copy-start | bytes 3145732
  210.7 7.7 %copy-start.35 = (bf16[2048,4096]{1,0:T(8,128)(2,1)S(1)}, bf16[2048,4096]{1,0:T(8,128)(2,1)}, u32[]{:S(2)}) copy-start(bf16[2048,4096]{1,0:T(8,128)(2,1)} %all-gather.5.cloned.1.call-done) | copy-start | bytes 50331652
  218.3 5.9 %copy-start.40 = (bf16[512,2048]{1,0:T(8,128)(2,1)}, bf16[512,2048]{1,0:T(8,128)(2,1)S(1)}, u32[]{:S(2)}) copy-start(bf16[512,2048]{1,0:T(8,128)(2,1)S(1)} %get-tuple-element.28) | copy-start | bytes 6291460
  218.3 3.2 copy-start.46
  221.5 5.4 %copy-start.43 = (bf16[512,2048]{1,0:T(8,128)(2,1)}, bf16[512,2048]{1,0:T(8,128)(2,1)S(1)}, u32[]{:S(2)}) copy-start(bf16[512,2048]{1,0:T(8,128)(2,1)S(1)} %get-tuple-element.29) | copy-start | bytes 6291460
  224.2 2.7 copy-start.3
  231.5 12.9 %copy-start.10 = (bf16[512,2048]{1,0:T(8,128)(2,1)}, bf16[512,2048]{1,0:T(8,128)(2,1)S(1)}, u32[]{:S(2)}) copy-start(bf16[512,2048]{1,0:T(8,128)(2,1)S(1)} %fusion.13) | copy-start | bytes 6291460
  231.5 5.1 copy-start.27
  236.6 5.4 %copy-start.12 = (bf16[512,2048]{1,0:T(8,128)(2,1)}, bf16[512,2048]{1,0:T(8,128)(2,1)S(1)}, u32[]{:S(2)}) copy-start(bf16[512,2048]{1,0:T(8,128)(2,1)S(1)} %fusion.6) | copy-start | bytes 6291460
  247.4 4.0 copy-start.6
  254.1 2.9 copy-start.22
  255.7 2.6 copy-start.38
  278.7 2.7 copy-start.18
  278.7 2.7 copy-start.48
  282.7 2.1 copy-start.41
  283.3 20.1 %collective-permute-start = (bf16[2,512,2048]{2,1,0:T(8,128)(2,1)S(1)}, bf16[2,512,2048]{2,1,0:T(8,128)(2,1)S(1)}, u32[]{:S(2)}, u32[]{:S(2)}) collective-permute-start(bf16[2,512,2048]{2,1,0:T(8,128)(2,1)S(1)} %maximum_maximum_fusion), channel_id=1, source_target_pairs={{0,2},{2,0},{1,3},{3,1},{4,6},{6,4},{5,7},{7,5},{8,10},{10,8},{9,1... | collective-permute-start | bytes 12582920 | tf_op jit(solution)/shard_map/ppermute | solution.py:154
  283.6 41.9 %collective-permute-start.9 = (bf16[512,2048]{1,0:T(8,128)(2,1)}, bf16[512,2048]{1,0:T(8,128)(2,1)}, u32[]{:S(2)}, u32[]{:S(2)}) collective-permute-start(bf16[512,2048]{1,0:T(8,128)(2,1)} %convolution_convert_fusion.4), channel_id=1, source_target_pairs={{0,2},{2,0},{1,3},{3,1},{4,6},{6,4},{5,7},{7,5},{8,10},{10,8},{9,1... | collective-permute-start | bytes 6291464 | tf_op jit(solution)/shard_map/ppermute | solution.py:154
  283.9 36.6 %collective-permute-start.2 = (bf16[512,2048]{1,0:T(8,128)(2,1)}, bf16[512,2048]{1,0:T(8,128)(2,1)}, u32[]{:S(2)}, u32[]{:S(2)}) collective-permute-start(bf16[512,2048]{1,0:T(8,128)(2,1)} %convolution_convert_fusion.6), channel_id=1, source_target_pairs={{0,2},{2,0},{1,3},{3,1},{4,6},{6,4},{5,7},{7,5},{8,10},{10,8},{9,1... | collective-permute-start | bytes 6291464 | tf_op jit(solution)/shard_map/ppermute | solution.py:154
  284.8 4.8 copy-start.4
  284.8 4.8 copy-start.44
  289.6 6.2 %copy-start.17 = (bf16[512,1536]{1,0:T(8,128)(2,1)S(1)}, bf16[512,1536]{1,0:T(8,128)(2,1)}, u32[]{:S(2)}) copy-start(bf16[512,1536]{1,0:T(8,128)(2,1)} %attend_back.3) | copy-start | bytes 4718596
  297.8 5.1 %copy-start.23 = (bf16[512,512]{1,0:T(8,128)(2,1)S(1)}, bf16[512,512]{1,0:T(8,128)(2,1)}, u32[]{:S(2)}) copy-start(bf16[512,512]{1,0:T(8,128)(2,1)} %get-tuple-element.22) | copy-start | bytes 1572868
  312.9 1.2 collective-permute-start.14
  313.2 22.9 %collective-permute-start.7 = (bf16[512,2048]{1,0:T(8,128)(2,1)}, bf16[512,2048]{1,0:T(8,128)(2,1)}, u32[]{:S(2)}, u32[]{:S(2)}) collective-permute-start(bf16[512,2048]{1,0:T(8,128)(2,1)} %convolution_convert_fusion.5), channel_id=1, source_target_pairs={{0,2},{2,0},{1,3},{3,1},{4,6},{6,4},{5,7},{7,5},{8,10},{10,8},{9,1... | collective-permute-start | bytes 6291464 | tf_op jit(solution)/shard_map/ppermute | solution.py:154
  314.1 4.9 collective-permute-start.15
  315.5 87.7 %collective-permute-start.1 = (bf16[512,2048]{1,0:T(8,128)(2,1)}, bf16[512,2048]{1,0:T(8,128)(2,1)S(1)}, u32[]{:S(2)}, u32[]{:S(2)}) collective-permute-start(bf16[512,2048]{1,0:T(8,128)(2,1)} %convolution_convert_fusion.7), channel_id=1, source_target_pairs={{0,2},{2,0},{1,3},{3,1},{4,6},{6,4},{5,7},{7,5},{8,10},{10,8},{9,1... | collective-permute-start | bytes 6291464 | tf_op jit(solution)/shard_map/ppermute | solution.py:154
  319.1 6.4 %copy-start.42 = (bf16[512,2048]{1,0:T(8,128)(2,1)S(1)}, bf16[512,2048]{1,0:T(8,128)(2,1)}, u32[]{:S(2)}) copy-start(bf16[512,2048]{1,0:T(8,128)(2,1)} %copy-done.40) | copy-start | bytes 6291460
  319.1 6.3 %copy-start.45 = (bf16[512,2048]{1,0:T(8,128)(2,1)S(1)}, bf16[512,2048]{1,0:T(8,128)(2,1)}, u32[]{:S(2)}) copy-start(bf16[512,2048]{1,0:T(8,128)(2,1)} %copy-done.43) | copy-start | bytes 6291460
  319.1 6.3 %copy-start.47 = (bf16[512,1024]{1,0:T(8,128)(2,1)S(1)}, bf16[512,1024]{1,0:T(8,128)(2,1)}, u32[]{:S(2)}) copy-start(bf16[512,1024]{1,0:T(8,128)(2,1)} %convolution_convert_fusion.12) | copy-start | bytes 3145732
  319.1 11.4 %collective-permute-start.16 = (f32[3,1024]{1,0:T(4,128)S(1)}, f32[3,1024]{1,0:T(4,128)S(1)}, u32[]{:S(2)}, u32[]{:S(2)}) collective-permute-start(f32[3,1024]{1,0:T(4,128)S(1)} %fusion.133), channel_id=1, source_target_pairs={{0,1},{1,0},{2,3},{3,2},{4,5},{5,4},{6,7},{7,6},{8,9},{9,8},{10,11... | collective-permute-start | bytes 36872 | tf_op jit(solution)/shard_map/ppermute | solution.py:184
  324.4 4.8 copy-start.11
  324.4 4.8 copy-start.13
  324.4 4.8 copy-start.28
  324.5 78.7 %collective-permute-start.3 = (bf16[512,2048]{1,0:T(8,128)(2,1)S(1)}, bf16[512,2048]{1,0:T(8,128)(2,1)S(1)}, u32[]{:S(2)}, u32[]{:S(2)}) collective-permute-start(bf16[512,2048]{1,0:T(8,128)(2,1)S(1)} %add_convert_fusion.4), channel_id=1, source_target_pairs={{0,1},{1,0},{2,3},{3,2},{4,5},{5,4},{6,7},{7,6},{8,9},{9,8},{10,11... | collective-permute-start | bytes 6291464 | tf_op jit(solution)/shard_map/ppermute | solution.py:184
  329.1 3.3 copy-start.32
  329.1 71.0 %collective-permute-start.10 = (bf16[256,2048]{1,0:T(8,128)(2,1)S(1)}, bf16[256,2048]{1,0:T(8,128)(2,1)S(1)}, u32[]{:S(2)}, u32[]{:S(2)}) collective-permute-start(bf16[256,2048]{1,0:T(8,128)(2,1)S(1)} %slice.209), channel_id=1, source_target_pairs={{0,4},{4,0},{8,12},{12,8},{16,20},{20,16},{24,28},{28,24},{1,5},{5... | collective-permute-start | bytes 3145736 | tf_op jit(solution)/shard_map/ppermute | solution.py:188
  330.6 4.8 collective-permute-start.17
  335.4 96.4 %collective-permute-start.18 = (f32[3,1024]{1,0:T(4,128)S(1)}, f32[3,1024]{1,0:T(4,128)S(1)}, u32[]{:S(2)}, u32[]{:S(2)}) collective-permute-start(f32[3,1024]{1,0:T(4,128)S(1)} %add.274), channel_id=1, source_target_pairs={{0,8},{4,12},{8,0},{12,4},{16,24},{20,28},{24,16},{28,20},{1,9},{5... | collective-permute-start | bytes 36872 | tf_op jit(solution)/shard_map/ppermute | solution.py:188
  339.0 64.1 %copy-start.15 = (bf16[512,2048]{1,0:T(8,128)(2,1)}, bf16[512,2048]{1,0:T(8,128)(2,1)S(1)}, u32[]{:S(2)}) copy-start(bf16[512,2048]{1,0:T(8,128)(2,1)S(1)} %add_convert_fusion.2) | copy-start | bytes 6291460
  340.3 103.2 %collective-permute-start.8 = (bf16[256,2048]{1,0:T(8,128)(2,1)}, bf16[256,2048]{1,0:T(8,128)(2,1)}, u32[]{:S(2)}, u32[]{:S(2)}) collective-permute-start(bf16[256,2048]{1,0:T(8,128)(2,1)} %slice.207), channel_id=1, source_target_pairs={{0,4},{4,0},{8,12},{12,8},{16,20},{20,16},{24,28},{28,24},{1,5},{5... | collective-permute-start | bytes 3145736 | tf_op jit(solution)/shard_map/ppermute | solution.py:188
  401.4 5.3 %copy-start.5 = (bf16[512,1024]{1,0:T(8,128)(2,1)S(1)}, bf16[512,1024]{1,0:T(8,128)(2,1)}, u32[]{:S(2)}) copy-start(bf16[512,1024]{1,0:T(8,128)(2,1)} %gather_fusion.1) | copy-start | bytes 3145732
  401.4 5.3 %copy-start.7 = (f32[512,1024]{1,0:T(8,128)S(1)}, f32[512,1024]{1,0:T(8,128)}, u32[]{:S(2)}) copy-start(f32[512,1024]{1,0:T(8,128)} %copy-done.6) | copy-start | bytes 6291460
  401.4 5.3 %copy-start.14 = (f32[512,1024]{1,0:T(8,128)S(1)}, f32[512,1024]{1,0:T(8,128)}, u32[]{:S(2)}) copy-start(f32[512,1024]{1,0:T(8,128)} %get-tuple-element.57) | copy-start | bytes 6291460
  401.4 5.3 %copy-start.34 = (f32[1,1024]{1,0:T(1,128)S(1)}, f32[1,1024]{1,0:T(1,128)}, u32[]{:S(2)}) copy-start(f32[1,1024]{1,0:T(1,128)} %copy-done.33) | copy-start | bytes 12292
  401.4 42.0 %collective-permute-start.11 = (bf16[256,2048]{1,0:T(8,128)(2,1)}, bf16[256,2048]{1,0:T(8,128)(2,1)}, u32[]{:S(2)}, u32[]{:S(2)}) collective-permute-start(bf16[256,2048]{1,0:T(8,128)(2,1)} %add_convert_fusion.7), channel_id=1, source_target_pairs={{0,1},{1,0},{2,3},{3,2},{4,5},{5,4},{6,7},{7,6},{8,9},{9,8},{10,11... | collective-permute-start | bytes 3145736 | tf_op jit(solution)/shard_map/ppermute | solution.py:184
  406.7 58.7 %collective-permute-start.4 = (bf16[256,2048]{1,0:T(8,128)(2,1)}, bf16[256,2048]{1,0:T(8,128)(2,1)}, u32[]{:S(2)}, u32[]{:S(2)}) collective-permute-start(bf16[256,2048]{1,0:T(8,128)(2,1)} %slice.200), channel_id=1, source_target_pairs={{0,4},{4,0},{8,12},{12,8},{16,20},{20,16},{24,28},{28,24},{1,5},{5... | collective-permute-start | bytes 3145736 | tf_op jit(solution)/shard_map/ppermute | solution.py:188
  420.4 23.0 %copy-start.16 = (bf16[512,2048]{1,0:T(8,128)(2,1)S(1)}, bf16[512,2048]{1,0:T(8,128)(2,1)}, u32[]{:S(2)}) copy-start(bf16[512,2048]{1,0:T(8,128)(2,1)} %copy-done.15) | copy-start | bytes 6291460
  431.8 33.6 %copy-start.9 = (bf16[512,2048]{1,0:T(8,128)(2,1)S(1)}, bf16[512,2048]{1,0:T(8,128)(2,1)}, u32[]{:S(2)}) copy-start(bf16[512,2048]{1,0:T(8,128)(2,1)} %copy-done.8) | copy-start | bytes 6291460
  445.6 36.6 %collective-permute-start.12 = (bf16[128,2048]{1,0:T(8,128)(2,1)S(1)}, bf16[128,2048]{1,0:T(8,128)(2,1)S(1)}, u32[]{:S(2)}, u32[]{:S(2)}) collective-permute-start(bf16[128,2048]{1,0:T(8,128)(2,1)S(1)} %slice.211), channel_id=1, source_target_pairs={{0,16},{4,20},{8,24},{12,28},{16,0},{20,4},{24,8},{28,12},{1,17},{... | collective-permute-start | bytes 1572872 | tf_op jit(solution)/shard_map/ppermute | solution.py:188
  465.4 38.7 %copy-start.1 = (s32[2,4096]{1,0:T(2,128)S(1)}, s32[2,4096]{1,0:T(2,128)}, u32[]{:S(2)}) copy-start(s32[2,4096]{1,0:T(2,128)} %param.17) | copy-start | bytes 98308
  467.1 26.1 %collective-permute-start.5 = (bf16[128,2048]{1,0:T(8,128)(2,1)S(1)}, bf16[128,2048]{1,0:T(8,128)(2,1)S(1)}, u32[]{:S(2)}, u32[]{:S(2)}) collective-permute-start(bf16[128,2048]{1,0:T(8,128)(2,1)S(1)} %slice.202), channel_id=1, source_target_pairs={{0,16},{4,20},{8,24},{12,28},{16,0},{20,4},{24,8},{28,12},{1,17},{... | collective-permute-start | bytes 1572872 | tf_op jit(solution)/shard_map/ppermute | solution.py:188
  482.3 13.7 %collective-permute-start.13 = (bf16[64,2048]{1,0:T(8,128)(2,1)S(1)}, bf16[64,2048]{1,0:T(8,128)(2,1)S(1)}, u32[]{:S(2)}, u32[]{:S(2)}) collective-permute-start(bf16[64,2048]{1,0:T(8,128)(2,1)S(1)} %slice.213), channel_id=1, source_target_pairs={{0,8},{4,12},{8,0},{12,4},{16,24},{20,28},{24,16},{28,20},{1,9},{5... | collective-permute-start | bytes 786440 | tf_op jit(solution)/shard_map/ppermute | solution.py:188
  493.4 8.2 %collective-permute-start.6 = (bf16[64,2048]{1,0:T(8,128)(2,1)S(1)}, bf16[64,2048]{1,0:T(8,128)(2,1)S(1)}, u32[]{:S(2)}, u32[]{:S(2)}) collective-permute-start(bf16[64,2048]{1,0:T(8,128)(2,1)S(1)} %slice.204), channel_id=1, source_target_pairs={{0,8},{4,12},{8,0},{12,4},{16,24},{20,28},{24,16},{28,20},{1,9},{5... | collective-permute-start | bytes 786440 | tf_op jit(solution)/shard_map/ppermute | solution.py:188
  (7 other events, 8.8 us)
Sparse Core Ops, SparseCore 0:
  12.3 81.8 all-gather.2
  97.6 113.0 all-gather.4
  306.5 127.7 reduce-scatter.1

commit v4 on v3

--- a/solution.py
+++ b/solution.py
@@ -202,6 +202,27 @@
         if bit > 1:
             values = values.astype(jnp.bfloat16)
     return values
+
+
+def halve_grads(left, right):
+    half, columns = left.shape[1] // 2, right[0].shape[1]
+    quarter = half // 2
+    colors = (slice(0, columns // 2), slice(columns // 2, columns))
+    sent = [contract_rows(left[:, half:], right[t]).astype(jnp.bfloat16) for t in (0, 1)]
+    got = [swap_cores(sent[t]) for t in (0, 1)]
+    part_a, part_b = [
+        [add_low(contract_rows(left[:, :half], right[t][:, color]), got[t][:, color]) for t in (0, 1)]
+        for color in colors
+    ]
+    got_a = swap_sides(part_a[1])
+    got_b = [swap_chips(part_b[t][quarter:], 1) for t in (0, 1)]
+    part_a = add_low(part_a[0], got_a)
+    part_b = [add_low(part_b[t][:quarter], got_b[t]) for t in (0, 1)]
+    got_a = swap_chips(part_a[quarter:], 1)
+    got_b = swap_sides(part_b[1])
+    part_a = add_low(part_a[:quarter], got_a)
+    part_b = add_low(part_b[0], got_b)
+    return halve_line(jnp.concatenate([part_a, part_b], axis=1)), sent
 
 
 def place(whole, rows, index):
@@ -265,15 +286,14 @@
 
     vectors = jnp.stack([attn_gain, mlp_gain, router_w], axis=1)
     vectors = jnp.pad(vectors, ((0, 0), (0, 128 - 3)))
-    near = jnp.concatenate([w_query, w_key, w_value, w_output, vectors], axis=1)
+    near = jnp.concatenate([w_query, w_key, w_value, w_output, w_up, vectors], axis=1)
     near = lax.all_gather(near, ALL, axis=0, tiled=True).reshape(sides, width, -1)
-    far = jnp.concatenate([w_up, w_down], axis=1)
-    far = lax.all_gather(far, ALL, axis=0, tiled=True).reshape(sides, width, -1)
+    far = lax.all_gather(w_down, ALL, axis=0, tiled=True).reshape(sides, width, -1)
     full_qkv = [near[t, :, : 3 * heads] for t in range(sides)]
     full_output = [near[t, :, 3 * heads : 4 * heads] for t in range(sides)]
-    full_up = [far[t, :, :hidden] for t in range(sides)]
-    full_down = [far[t, :, hidden:] for t in range(sides)]
-    small = near[0, :, 4 * heads : 4 * heads + 3].astype(jnp.float32).T
+    full_up = [near[t, :, 4 * heads : 4 * heads + hidden] for t in range(sides)]
+    full_down = [far[t] for t in range(sides)]
+    small = near[0, :, 4 * heads + hidden : 4 * heads + hidden + 3].astype(jnp.float32).T
     attn_gain_f, mlp_gain_f, router_f = small[0], small[1], small[2]
 
     own_index = lax.dynamic_index_in_dim(routed_index, side, 0, keepdims=False)
@@ -299,31 +319,18 @@
 
     hidden_pre = [plain_dot(normed_mlp, full_up[t]) for t in range(sides)]
     hidden_act = [jax.nn.gelu(hidden_pre[t], approximate=True).astype(jnp.bfloat16) for t in range(sides)]
+    own_act = [jnp.where(side == 0, hidden_act[t], hidden_act[1 - t]) for t in range(sides)]
+    left_down = relative_order(d_mlp_low, False)
+    sum_down, _ = halve_grads(left_down, own_act)
     d_pre = []
     for t in range(sides):
         _, gelu_back = jax.vjp(partial(jax.nn.gelu, approximate=True), hidden_pre[t])
-        d_pre.append(gelu_back(plain_dot(d_mlp_low, full_down[t]))[0].astype(jnp.bfloat16))
+        d_act = plain_dot(d_mlp_low, full_down[t])
+        d_pre.append(gelu_back(d_act)[0].astype(jnp.bfloat16))
     own_pre = [jnp.where(side == 0, d_pre[t], d_pre[1 - t]) for t in range(sides)]
-    own_act = [jnp.where(side == 0, hidden_act[t], hidden_act[1 - t]) for t in range(sides)]
     left_up = relative_order(normed_mlp, False)
-    left_down = relative_order(d_mlp_low, False)
-    half = width // 2
-    sent_up = [contract_rows(left_up[:, half:], own_pre[t]).astype(jnp.bfloat16) for t in (1, 0)][::-1]
-    sent_down = [contract_rows(left_down[:, half:], own_act[t]).astype(jnp.bfloat16) for t in (1, 0)][::-1]
-    got_up = [swap_cores(sent_up[t]) for t in (1, 0)][::-1]
-    got_down = [swap_cores(sent_down[t]) for t in (1, 0)][::-1]
-    d_pre, sent_up, sent_down = lax.optimization_barrier((d_pre, sent_up, sent_down))
-    part_up = [add_low(contract_rows(left_up[:, :half], own_pre[t]), got_up[t]) for t in (0, 1)]
-    part_down = [add_low(contract_rows(left_down[:, :half], own_act[t]), got_down[t]) for t in (0, 1)]
-    quarter = half // 2
-    got_up = swap_sides(part_up[1])
-    got_down = [swap_chips(part_down[t][quarter:], 1) for t in (0, 1)]
-    one_up = add_low(part_up[0], got_up)
-    one_down = [add_low(part_down[t][:quarter], got_down[t]) for t in (0, 1)]
-    got_up = swap_chips(one_up[quarter:], 1)
-    got_down = swap_sides(one_down[1])
-    sum_up = halve_line(add_low(one_up[:quarter], got_up))
-    sum_down = halve_line(add_low(one_down[0], got_down))
+    sum_up, sent_up = halve_grads(left_up, own_pre)
+    d_pre, sent_up = lax.optimization_barrier((d_pre, sent_up))
 
     d_normed_mlp = sum(contract_last(d_pre[t], full_up[t]) for t in range(sides))
     _, norm_back_mlp = jax.vjp(rms_norm, middle, mlp_gain_f)
@@ -333,6 +340,7 @@
     for t in range(sides):
         d_attended = plain_dot(d_attn_low, full_output[t]).astype(jnp.bfloat16)
         d_qkv.append(attend_back(qkv[t], d_attended, lse[t], seg_row, seg_column))
+    half = width // 2
     left_qkv = relative_order(normed_attn, True)
     left_output = relative_order(d_attn_low, True)
     grad_attn = [

time: 521 us -> 538 us (1.033)
  starting transfers between devices: 15.1 us -> 25.3 us
  matrix products: 107 us -> 115 us
    all_gather x1, waiting for transfers between devices: 77.3 us -> 29.2 us  [block(): lax.all_gather(w_down, ALL, axis=0, tiled=True).reshape(sides, width, -1)]
    all_gather x1, waiting for transfers between devices: 62.3 us -> 100 us  [block(): lax.all_gather(near, ALL, axis=0, tiled=True).reshape(sides, width, -1)]
    ppermute x3 -> x5, waiting for transfers between devices: 0.01 us -> 16.2 us  [swap_sides(): return lax.ppermute(values, 'tensor', [(0, 1), (1, 0)])]
    dot_general x12, matrix products: 43.3 us -> 52.2 us  [plain_dot(): return jnp.dot(left, right, preferred_element_type=jnp.float32)]
    ppermute x10 -> x13, starting transfers between devices: 9.49 us -> 18 us  [swap_chips(): lax.ppermute(values, 'chips', [(i, i ^ bit) for i in range(lax.axis_size(...]
    dot_general x16 -> x20, matrix products: 31.7 us -> 34.9 us  [contract_rows(): lax.dot_general(left, right, (((0,), (0,)), ((), ())), preferred_element_...]
    ppermute x10 -> x13, waiting for transfers between devices: 125 us -> 122 us  [swap_chips(): lax.ppermute(values, 'chips', [(i, i ^ bit) for i in range(lax.axis_size(...]
  transfers between devices with their start and end apart: 22 -> 27, of which waited for: 12 -> 12; matrix products, arithmetic and copies ran while one was open for 19% -> 23% of each run, Pallas kernels for 7% -> 11%
where the time goes in v4:
time: 538 us; the launch traced here: 528 us
  waiting for transfers between devices  268 us (50%)
  matrix products  115 us (21%)
  Pallas kernels  58.5 us (11%)
  local copies, waits for them, and re-layouts  27.2 us (5%)
  starting transfers between devices  25.3 us (5%)
  other arithmetic  19.2 us (4%)
  between operations  15.2 us (3%)
    ppermute x13, waiting for transfers between devices, swap_chips(): lax.ppermute(values, 'chips', [(i, i ^ bit) for i in range(lax.axis_size(...  122 us
    all_gather x1, waiting for transfers between devices, block(): lax.all_gather(near, ALL, axis=0, tiled=True).reshape(sides, width, -1)  100 us
    dot_general x12, matrix products, plain_dot(): return jnp.dot(left, right, preferred_element_type=jnp.float32)  52.2 us
    dot_general x20, matrix products, contract_rows(): lax.dot_general(left, right, (((0,), (0,)), ((), ())), preferred_element_...  34.9 us
    all_gather x1, waiting for transfers between devices, block(): lax.all_gather(w_down, ALL, axis=0, tiled=True).reshape(sides, width, -1)  29.2 us
    dot_general x8, matrix products, contract_last(): lax.dot_general(left, right, (((1,), (1,)), ((), ())), preferred_element_...  27.7 us
    pallas_call x2, Pallas kernels, place(): pl.pallas_call(kernel, grid=(tokens // step,), out_shape=jax.ShapeDtypeSt...  22.8 us
    pallas_call x2, Pallas kernels, attend_back(): pl.pallas_call(kernel, grid=(pairs,), out_shape=jax.ShapeDtypeStruct((row...  20.4 us
  transfers between devices with their start and end apart: 27, of which 12 were waited for; matrix products, arithmetic and copies ran while one was open for 23% of the time, Pallas kernels for 11%

profile of v4, /device:TPU:0, one launch (start us, length us, event | category | flops | bytes accessed | tf_op | source)
XLA Modules:
  0.0 528.4 jit_solution(3740350415252454263)
XLA Ops:
  16.0 7.2 %gather_fusion = bf16[512,1024]{1,0:T(8,128)(2,1)S(1)} fusion(bf16[4096,1024]{1,0:T(8,128)(2,1)} %whole_ref.2, s32[1024]{0:T(1024)S(1)} %pad_clamp_fusion), kind=kCustom, calls=%fused_computation.clone | custom fusion | bytes 2099200 | tf_op jit(solution)/shard_map/jit(_take)/gather | solution.py:301
  23.2 8.4 %gather_fusion.1 = bf16[512,1024]{1,0:T(8,128)(2,1)} fusion(bf16[4096,1024]{1,0:T(8,128)(2,1)} %whole_ref.3, s32[1024]{0:T(1024)S(1)} %pad_clamp_fusion), kind=kCustom, calls=%fused_computation.1.clone | custom fusion | bytes 2099200 | tf_op jit(solution)/shard_map/jit(_take)/gather | solution.py:302
  32.7 100.3 %all-gather.3.cloned.1.call-done = bf16[2048,4224]{1,0:T(8,128)(2,1)} async-done(((bf16[64,4224]{1,0:T(8,128)(2,1)}), bf16[2048,4224]{1,0:T(8,128)(2,1)}) %all-gather.3.cloned.1.call-update) | async-done | bytes 17301520 | tf_op jit(solution)/shard_map/all_gather | solution.py:290
  134.2 5.0 convolution_convert_fusion.9.q_ref.k_ref.v_ref
  139.2 7.5 %attend.2 = (bf16[512,512]{1,0:T(8,128)(2,1)}, f32[8,1,512]{2,1,0:T(1,128)}) custom-call(s32[1,512]{1,0:T(1,128)} %bitcast.125, s32[512,1]{1,0:T(8,128)} %copy.41.seg_column_ref, bf16[512,1536]{1,0:T(8,128)(2,1)} %convolution_convert_fusion.9.q_ref.k_ref.v_ref, bf16[512,1536]{1,0:T(8,128)(2,1)} %convolution_convert_fusion.9.q_ref.k_ref.v_ref, ...), custom_call_target="tpu_custom_call" | custom-call | tf_op jit(solution)/shard_map/attend/pallas_call | solution.py:79
  146.7 5.0 convolution_convert_fusion.8.q_ref.k_ref.v_ref
  151.7 7.8 %attend.3 = (bf16[512,512]{1,0:T(8,128)(2,1)}, f32[8,1,512]{2,1,0:T(1,128)}) custom-call(s32[1,512]{1,0:T(1,128)} %bitcast.126, s32[512,1]{1,0:T(8,128)} %copy.41.seg_column_ref, bf16[512,1536]{1,0:T(8,128)(2,1)} %convolution_convert_fusion.8.q_ref.k_ref.v_ref, bf16[512,1536]{1,0:T(8,128)(2,1)} %convolution_convert_fusion.8.q_ref.k_ref.v_ref, ...), custom_call_target="tpu_custom_call" | custom-call | tf_op jit(solution)/shard_map/attend/pallas_call | solution.py:79
  159.5 2.1 fusion.102
  161.6 2.4 multiply_reduce_fusion.2
  164.5 4.5 fusion.29
  169.1 10.4 %broadcast_select_fusion.1 = (bf16[512,2048]{1,0:T(8,128)(2,1)}, bf16[512,2048]{1,0:T(8,128)(2,1)}, bf16[512,2048]{1,0:T(8,128)(2,1)}, f32[512,2048]{1,0:T(8,128)}) fusion(pred[]{:T(512)S(6)} %eq.26, f32[512,2048]{1,0:T(8,128)S(1)} %fusion.29, bf16[512,1024]{1,0:T(8,128)(2,1)S(1)} %multiply_convert_fusion.2, bf16[2,1024,4224]{2,1,0:T(8,128)(2,1)} %bitcast.112), kind=kOutput, calls=%fused_computation.130 | convolution fusion | flops 2167406592 | bytes 19922944 | tf_op jit(solution)/shard_map/dot_general | solution.py:27
  179.5 2.4 convolution_convert_fusion.13
  182.0 29.2 %all-gather.5.cloned.1.call-done = bf16[2048,2048]{1,0:T(8,128)(2,1)} async-done(((bf16[64,2048]{1,0:T(8,128)(2,1)}), bf16[2048,2048]{1,0:T(8,128)(2,1)}) %all-gather.5.cloned.1.call-update) | async-done | bytes 8388624 | tf_op jit(solution)/shard_map/all_gather | solution.py:291
  211.2 7.8 %fusion.6 = bf16[512,2048]{1,0:T(8,128)(2,1)S(1)} fusion(f32[512,2048]{1,0:T(8,128)} %copy-done.41, bf16[2048,2048]{1,0:T(8,128)(2,1)} %all-gather.5.cloned.1.call-done, f32[512]{0:T(512)S(1)} %add_divide_fusion, bf16[512,1024]{1,0:T(8,128)(2,1)} %gather_fusion.1, pred[512]{0:T(512)(128)(4,1)S(1)} %compare_and_fusion), kind=kOutput, calls=%fused_computation.35 | convolution fusion | flops 2170552320 | bytes 11536896 | tf_op jit(solution)/shard_map/dot_general | solution.py:27
  219.0 8.2 %broadcast_select_fusion.2 = (bf16[512,2048]{1,0:T(8,128)(2,1)S(1)}, bf16[512,2048]{1,0:T(8,128)(2,1)S(1)}, bf16[512,2048]{1,0:T(8,128)(2,1)S(1)}) fusion(bf16[512,2048]{1,0:T(8,128)(2,1)S(1)} %fusion.6, pred[]{:T(512)S(6)} %eq.26, f32[512,2048]{1,0:T(8,128)} %get-tuple-element.59, bf16[2048,2048]{1,0:T(8,128)(2,1)} %all-gather.5.cloned.1.call-done, ...), kind=kOutput, calls=%fused_computation.131 | convolution fusion | flops 2172649472 | bytes 17828352 | tf_op jit(solution)/shard_map/dot_general | solution.py:27
  227.3 2.6 convolution_convert_fusion.6
  229.9 2.6 convolution_convert_fusion.7
  232.5 2.4 fusion.28
  234.9 2.8 multiply_reduce_fusion
  239.0 1.5 convolution_convert_fusion.18.d_ref
  240.5 1.5 convolution_convert_fusion.19.d_ref
  242.5 1.6 convolution_convert_fusion.11
  244.2 2.6 convolution_convert_fusion.12
  248.0 1.3 fusion.72
  249.3 10.3 %attend_back.3 = bf16[512,1536]{1,0:T(8,128)(2,1)} custom-call(s32[1,512]{1,0:T(1,128)} %bitcast.127, s32[512,1]{1,0:T(8,128)} %copy.41.seg_column_ref, bf16[512,1536]{1,0:T(8,128)(2,1)} %convolution_convert_fusion.8.q_ref.k_ref.v_ref, bf16[512,1536]{1,0:T(8,128)(2,1)} %convolution_convert_fusion.8.q_ref.k_ref.v_ref, ...), custom_call_target="tpu_custom_call" | custom-call | tf_op jit(solution)/shard_map/attend_back/pallas_call | solution.py:134
  259.6 10.1 %attend_back.2 = bf16[512,1536]{1,0:T(8,128)(2,1)} custom-call(s32[1,512]{1,0:T(1,128)} %bitcast.128, s32[512,1]{1,0:T(8,128)} %copy.41.seg_column_ref, bf16[512,1536]{1,0:T(8,128)(2,1)} %convolution_convert_fusion.9.q_ref.k_ref.v_ref, bf16[512,1536]{1,0:T(8,128)(2,1)} %convolution_convert_fusion.9.q_ref.k_ref.v_ref, ...), custom_call_target="tpu_custom_call" | custom-call | tf_op jit(solution)/shard_map/attend_back/pallas_call | solution.py:134
  269.7 2.7 fusion.45
  274.1 4.9 fusion.32
  279.0 3.9 fusion.57
  282.9 3.8 fusion.40
  288.2 5.4 %fusion.55 = (f32[1024]{0:T(1024)S(1)}, f32[512]{0:T(512)S(1)}, f32[1024]{0:T(1024)S(1)}, f32[512,1024]{1,0:T(8,128)}) fusion(f32[512]{0:T(512)S(1)} %fusion.136, bf16[512,1024]{1,0:T(8,128)(2,1)S(1)} %gather_fusion, pred[512]{0:T(512)(128)(4,1)S(1)} %compare_and_fusion, f32[1024]{0:T(1024)S(1)} %bitcast.146, f32[512]{0:T(512)S(1)} %fusion.135, ...), kind=kOutput, calls=%fused_computation.103 | convolution fusion | flops 1616377344 | bytes 9980416 | tf_op jit(solution)/shard_map/dot_general | solution.py:37
  294.2 1.5 convolution_convert_fusion.10
  295.7 2.6 convolution_convert_fusion.4
  301.8 2.6 convolution_convert_fusion.5
  305.2 1.5 collective-permute-start.20
  306.7 2.7 add_convert_fusion
  310.6 4.2 fusion.60.rows_ref
  314.8 2.0 collective-permute-start.22
  316.8 2.2 fusion.86
  320.0 1.5 collective-permute-start.23
  322.2 11.2 %place_rows.3 = bf16[4096,1024]{1,0:T(8,128)(2,1)} custom-call(s32[1,512]{1,0:T(1,128)} %copy-done.31, bf16[4096,1024]{1,0:T(8,128)(2,1)} %whole_ref.3, bf16[512,1024]{1,0:T(8,128)(2,1)} %fusion.60.rows_ref), custom_call_target="tpu_custom_call" | custom-call | tf_op jit(solution)/shard_map/place_rows/pallas_call | solution.py:240
  333.5 11.5 %place_rows.2 = bf16[4096,1024]{1,0:T(8,128)(2,1)} custom-call(s32[1,512]{1,0:T(1,128)} %copy-done.31, bf16[4096,1024]{1,0:T(8,128)(2,1)} %whole_ref.2, bf16[512,1024]{1,0:T(8,128)(2,1)} %get-tuple-element.45.rows_ref), custom_call_target="tpu_custom_call" | custom-call | tf_op jit(solution)/shard_map/place_rows/pallas_call | solution.py:240
  345.1 2.4 add_convert_fusion.4
  348.6 2.0 add_convert_fusion.1
  350.7 1.8 collective-permute-start.15
  352.5 2.0 add_convert_fusion.2
  355.1 2.0 add_convert_fusion.9
  358.2 2.0 add_convert_fusion.6
  361.5 2.0 add_convert_fusion.7
  363.5 23.9 %collective-permute-done.15 = bf16[256,1024]{1,0:T(8,128)(2,1)S(1)} collective-permute-done((bf16[256,1024]{1,0:T(8,128)(2,1)S(1)}, bf16[256,1024]{1,0:T(8,128)(2,1)S(1)}, u32[]{:S(2)}, u32[]{:S(2)}) %collective-permute-start.15) | collective-permute-done | bytes 524320 | tf_op jit(solution)/shard_map/ppermute | solution.py:188
  387.4 2.2 collective-permute-start.5
  389.8 46.3 %collective-permute-done.6 = bf16[256,1024]{1,0:T(8,128)(2,1)S(1)} collective-permute-done((bf16[256,1024]{1,0:T(8,128)(2,1)S(1)}, bf16[256,1024]{1,0:T(8,128)(2,1)S(1)}, u32[]{:S(2)}, u32[]{:S(2)}) %collective-permute-start.6) | collective-permute-done | bytes 524320 | tf_op jit(solution)/shard_map/ppermute | solution.py:188
  438.4 1.8 add_convert_fusion.3
  441.2 1.8 add_convert_fusion.8
  444.3 6.6 %collective-permute-done.16 = bf16[256,1024]{1,0:T(8,128)(2,1)S(1)} collective-permute-done((bf16[256,1024]{1,0:T(8,128)(2,1)S(1)}, bf16[256,1024]{1,0:T(8,128)(2,1)S(1)}, u32[]{:S(2)}, u32[]{:S(2)}) %collective-permute-start.16) | collective-permute-done | bytes 524320 | tf_op jit(solution)/shard_map/ppermute | solution.py:184
  451.2 9.6 %collective-permute-done.7 = bf16[256,1024]{1,0:T(8,128)(2,1)S(1)} collective-permute-done((bf16[256,1024]{1,0:T(8,128)(2,1)S(1)}, bf16[256,1024]{1,0:T(8,128)(2,1)S(1)}, u32[]{:S(2)}, u32[]{:S(2)}) %collective-permute-start.7) | collective-permute-done | bytes 524320 | tf_op jit(solution)/shard_map/ppermute | solution.py:184
  461.3 2.0 collective-permute-start.17
  463.3 6.3 %collective-permute-done.4 = bf16[256,1024]{1,0:T(8,128)(2,1)S(1)} collective-permute-done((bf16[256,1024]{1,0:T(8,128)(2,1)S(1)}, bf16[256,1024]{1,0:T(8,128)(2,1)S(1)}, u32[]{:S(2)}, u32[]{:S(2)}) %collective-permute-start.4) | collective-permute-done | bytes 524320 | tf_op jit(solution)/shard_map/ppermute | solution.py:188
  469.8 1.9 collective-permute-start.8
  472.2 24.3 %collective-permute-done.17 = bf16[128,2048]{1,0:T(8,128)(2,1)S(1)} collective-permute-done((bf16[128,2048]{1,0:T(8,128)(2,1)S(1)}, bf16[128,2048]{1,0:T(8,128)(2,1)S(1)}, u32[]{:S(2)}, u32[]{:S(2)}) %collective-permute-start.17) | collective-permute-done | bytes 524320 | tf_op jit(solution)/shard_map/ppermute | solution.py:188
  497.8 10.0 %collective-permute-done.8 = bf16[128,2048]{1,0:T(8,128)(2,1)S(1)} collective-permute-done((bf16[128,2048]{1,0:T(8,128)(2,1)S(1)}, bf16[128,2048]{1,0:T(8,128)(2,1)S(1)}, u32[]{:S(2)}, u32[]{:S(2)}) %collective-permute-start.8) | collective-permute-done | bytes 524320 | tf_op jit(solution)/shard_map/ppermute | solution.py:188
  508.0 5.4 %collective-permute-done.18 = bf16[64,2048]{1,0:T(8,128)(2,1)S(1)} collective-permute-done((bf16[64,2048]{1,0:T(8,128)(2,1)S(1)}, bf16[64,2048]{1,0:T(8,128)(2,1)S(1)}, u32[]{:S(2)}, u32[]{:S(2)}) %collective-permute-start.18) | collective-permute-done | bytes 262176 | tf_op jit(solution)/shard_map/ppermute | solution.py:188
  514.2 4.7 collective-permute-done.9
  519.7 1.7 fusion.149
  (214 shorter events, 38.8 us)
Async XLA Ops:
  7.2 7.6 %copy-start = (s32[2,4096]{1,0:T(2,128)S(1)}, s32[2,4096]{1,0:T(2,128)}, u32[]{:S(2)}) copy-start(s32[2,4096]{1,0:T(2,128)} %param.17) | copy-start | bytes 98308
  7.2 125.8 %all-gather.3.cloned.1.call-start = ((), (), s32[]{:S(2)}) async-start(), calls=%async_computation.1 | async-start | bytes 17842176 | tf_op jit(solution)/shard_map/all_gather | solution.py:290
  13.2 197.9 %all-gather.5.cloned.1.call-start = ((), (), s32[]{:S(2)}) async-start(), calls=%async_computation.2 | async-start | bytes 8650752 | tf_op jit(solution)/shard_map/all_gather | solution.py:291
  14.0 505.7 %reduce-scatter.2.cloned.1.call-start = ((), (), s32[]{:S(2)}) async-start(), calls=%async_computation.3 | async-start | bytes 4456448 | tf_op jit(solution)/shard_map/reduce_scatter | solution.py:162
  14.8 16.9 %copy-start.31 = (s32[1,512]{1,0:T(1,128)}, s32[1,512]{1,0:T(1,128)S(1)}, u32[]{:S(2)}) copy-start(s32[1,512]{1,0:T(1,128)S(1)} %constant_dynamic-slice_fusion.1.index_ref) | copy-start | bytes 6148
  15.1 8.1 %copy-start.32 = (s32[512]{0:T(512)}, s32[512]{0:T(512)S(1)}, u32[]{:S(2)}) copy-start(s32[512]{0:T(512)S(1)} %convert_reduce_fusion.1) | copy-start | bytes 6148
  151.7 7.8 %copy-start.19 = (bf16[512,512]{1,0:T(8,128)(2,1)S(1)}, bf16[512,512]{1,0:T(8,128)(2,1)}, u32[]{:S(2)}) copy-start(bf16[512,512]{1,0:T(8,128)(2,1)} %get-tuple-element.22) | copy-start | bytes 1572868
  169.1 10.5 %copy-start.41 = (f32[512,2048]{1,0:T(8,128)}, f32[512,2048]{1,0:T(8,128)S(1)}, u32[]{:S(2)}) copy-start(f32[512,2048]{1,0:T(8,128)S(1)} %fusion.29) | copy-start | bytes 12582916
  211.1 7.8 %copy-start.2 = (bf16[512,1024]{1,0:T(8,128)(2,1)S(1)}, bf16[512,1024]{1,0:T(8,128)(2,1)}, u32[]{:S(2)}) copy-start(bf16[512,1024]{1,0:T(8,128)(2,1)} %gather_fusion.1) | copy-start | bytes 3145732
  211.1 21.4 %slice-start = ((s8[17301504]{0:T(1024)(128)(4,1)}), s8[4194304]{0:T(1024)(128)(4,1)S(1)}, s32[]{:S(2)}) async-start(s8[17301504]{0:T(1024)(128)(4,1)} %bitcast.115), calls=%async_computation.4 | async-start | bytes 8388608
  211.1 21.4 %slice-start.1 = ((s8[17301504]{0:T(1024)(128)(4,1)}), s8[4194304]{0:T(1024)(128)(4,1)S(1)}, s32[]{:S(2)}) async-start(s8[17301504]{0:T(1024)(128)(4,1)} %bitcast.115), calls=%async_computation.5 | async-start | bytes 8388608
  219.0 8.3 %copy-start.24 = (bf16[512,1024]{1,0:T(8,128)(2,1)S(1)}, bf16[512,1024]{1,0:T(8,128)(2,1)}, u32[]{:S(2)}) copy-start(bf16[512,1024]{1,0:T(8,128)(2,1)} %convolution_convert_fusion.13) | copy-start | bytes 3145732
  219.0 13.5 %slice-start.2 = ((s8[17301504]{0:T(1024)(128)(4,1)}), s8[4194304]{0:T(1024)(128)(4,1)S(1)}, s32[]{:S(2)}) async-start(s8[17301504]{0:T(1024)(128)(4,1)} %bitcast.115), calls=%async_computation.6 | async-start | bytes 8388608
  219.0 13.5 %slice-start.3 = ((s8[17301504]{0:T(1024)(128)(4,1)}), s8[4194304]{0:T(1024)(128)(4,1)S(1)}, s32[]{:S(2)}) async-start(s8[17301504]{0:T(1024)(128)(4,1)} %bitcast.115), calls=%async_computation.7 | async-start | bytes 8388608
  219.0 13.5 %slice-start.4 = ((s8[17301504]{0:T(1024)(128)(4,1)}), s8[524288]{0:T(1024)(128)(4,1)S(1)}, s32[]{:S(2)}) async-start(s8[17301504]{0:T(1024)(128)(4,1)} %bitcast.115), calls=%async_computation.8 | async-start | bytes 1048576
  227.3 5.2 copy-start.13
  227.3 5.2 copy-start.39
  242.0 113.1 %collective-permute-start.2 = (bf16[512,2048]{1,0:T(8,128)(2,1)}, bf16[512,2048]{1,0:T(8,128)(2,1)}, u32[]{:S(2)}, u32[]{:S(2)}) collective-permute-start(bf16[512,2048]{1,0:T(8,128)(2,1)} %convolution_convert_fusion.6), channel_id=1, source_target_pairs={{0,2},{2,0},{1,3},{3,1},{4,6},{6,4},{5,7},{7,5},{8,10},{10,8},{9,1... | collective-permute-start | bytes 6291464 | tf_op jit(solution)/shard_map/ppermute | solution.py:154
  242.3 118.0 %collective-permute-start.1 = (bf16[512,2048]{1,0:T(8,128)(2,1)}, bf16[512,2048]{1,0:T(8,128)(2,1)}, u32[]{:S(2)}, u32[]{:S(2)}) collective-permute-start(bf16[512,2048]{1,0:T(8,128)(2,1)} %convolution_convert_fusion.7), channel_id=1, source_target_pairs={{0,2},{2,0},{1,3},{3,1},{4,6},{6,4},{5,7},{7,5},{8,10},{10,8},{9,1... | collective-permute-start | bytes 6291464 | tf_op jit(solution)/shard_map/ppermute | solution.py:154
  244.1 3.9 copy-start.37
  244.2 3.9 copy-start.20
  272.5 6.5 %slice-start.5 = ((s8[8388608]{0:T(1024)(128)(4,1)}), s8[4194304]{0:T(1024)(128)(4,1)S(1)}, s32[]{:S(2)}) async-start(s8[8388608]{0:T(1024)(128)(4,1)} %bitcast.153), calls=%async_computation.9 | async-start | bytes 8388608
  274.1 4.9 copy-start.3
  274.1 4.9 copy-start.9
  274.1 4.9 slice-start.6
  282.9 3.8 copy-start.22
  282.9 3.8 copy-start.23
  287.6 17.6 %collective-permute-start = (bf16[2,512,2048]{2,1,0:T(8,128)(2,1)S(1)}, bf16[2,512,2048]{2,1,0:T(8,128)(2,1)S(1)}, u32[]{:S(2)}, u32[]{:S(2)}) collective-permute-start(bf16[2,512,2048]{2,1,0:T(8,128)(2,1)S(1)} %maximum_maximum_fusion), channel_id=1, source_target_pairs={{0,2},{2,0},{1,3},{3,1},{4,6},{6,4},{5,7},{7,5},{8,10},{10,8},{9,1... | collective-permute-start | bytes 12582920 | tf_op jit(solution)/shard_map/ppermute | solution.py:154
  293.6 11.2 %collective-permute-start.19 = (f32[3,1024]{1,0:T(4,128)S(1)}, f32[3,1024]{1,0:T(4,128)S(1)}, u32[]{:S(2)}, u32[]{:S(2)}) collective-permute-start(f32[3,1024]{1,0:T(4,128)S(1)} %pad_maximum_fusion.2), channel_id=1, source_target_pairs={{0,2},{2,0},{1,3},{3,1},{4,6},{6,4},{5,7},{7,5},{8,10},{10,8},{9,1... | collective-permute-start | bytes 36872 | tf_op jit(solution)/shard_map/ppermute | solution.py:154
  295.7 5.5 %copy-start.27 = (bf16[512,1024]{1,0:T(8,128)(2,1)}, bf16[512,1024]{1,0:T(8,128)(2,1)S(1)}, u32[]{:S(2)}) copy-start(bf16[512,1024]{1,0:T(8,128)(2,1)S(1)} %convolution_convert_fusion.10) | copy-start | bytes 3145732
  295.7 3.4 copy-start.34
  298.4 46.7 %collective-permute-start.11 = (bf16[512,2048]{1,0:T(8,128)(2,1)}, bf16[512,2048]{1,0:T(8,128)(2,1)}, u32[]{:S(2)}, u32[]{:S(2)}) collective-permute-start(bf16[512,2048]{1,0:T(8,128)(2,1)} %convolution_convert_fusion.4), channel_id=1, source_target_pairs={{0,2},{2,0},{1,3},{3,1},{4,6},{6,4},{5,7},{7,5},{8,10},{10,8},{9,1... | collective-permute-start | bytes 6291464 | tf_op jit(solution)/shard_map/ppermute | solution.py:154
  304.8 47.6 %collective-permute-start.10 = (bf16[512,2048]{1,0:T(8,128)(2,1)}, bf16[512,2048]{1,0:T(8,128)(2,1)}, u32[]{:S(2)}, u32[]{:S(2)}) collective-permute-start(bf16[512,2048]{1,0:T(8,128)(2,1)} %convolution_convert_fusion.5), channel_id=1, source_target_pairs={{0,2},{2,0},{1,3},{3,1},{4,6},{6,4},{5,7},{7,5},{8,10},{10,8},{9,1... | collective-permute-start | bytes 6291464 | tf_op jit(solution)/shard_map/ppermute | solution.py:154
  305.2 4.2 collective-permute-start.20
  309.5 5.3 %collective-permute-start.21 = (f32[3,1024]{1,0:T(4,128)S(1)}, f32[3,1024]{1,0:T(4,128)S(1)}, u32[]{:S(2)}, u32[]{:S(2)}) collective-permute-start(f32[3,1024]{1,0:T(4,128)S(1)} %fusion.177), channel_id=1, source_target_pairs={{0,1},{1,0},{2,3},{3,2},{4,5},{5,4},{6,7},{7,6},{8,9},{9,8},{10,11... | collective-permute-start | bytes 36872 | tf_op jit(solution)/shard_map/ppermute | solution.py:184
  310.6 6.3 %copy-start.17 = (bf16[512,2048]{1,0:T(8,128)(2,1)S(1)}, bf16[512,2048]{1,0:T(8,128)(2,1)}, u32[]{:S(2)}) copy-start(bf16[512,2048]{1,0:T(8,128)(2,1)} %get-tuple-element.39) | copy-start | bytes 6291460
  310.6 6.3 %copy-start.28 = (bf16[512,1024]{1,0:T(8,128)(2,1)S(1)}, bf16[512,1024]{1,0:T(8,128)(2,1)}, u32[]{:S(2)}) copy-start(bf16[512,1024]{1,0:T(8,128)(2,1)} %copy-done.27) | copy-start | bytes 3145732
  310.6 10.9 %copy-start.14 = (bf16[512,2048]{1,0:T(8,128)(2,1)S(1)}, bf16[512,2048]{1,0:T(8,128)(2,1)}, u32[]{:S(2)}) copy-start(bf16[512,2048]{1,0:T(8,128)(2,1)} %copy-done.13) | copy-start | bytes 6291460
  310.6 10.9 %copy-start.25 = (bf16[512,1024]{1,0:T(8,128)(2,1)S(1)}, bf16[512,1024]{1,0:T(8,128)(2,1)}, u32[]{:S(2)}) copy-start(bf16[512,1024]{1,0:T(8,128)(2,1)} %convolution_convert_fusion.13) | copy-start | bytes 3145732
  314.8 5.2 collective-permute-start.22
  320.0 25.0 %collective-permute-start.23 = (f32[3,1024]{1,0:T(4,128)S(1)}, f32[3,1024]{1,0:T(4,128)S(1)}, u32[]{:S(2)}, u32[]{:S(2)}) collective-permute-start(f32[3,1024]{1,0:T(4,128)S(1)} %add.310), channel_id=1, source_target_pairs={{0,8},{4,12},{8,0},{12,4},{16,24},{20,28},{24,16},{28,20},{1,9},{5... | collective-permute-start | bytes 36872 | tf_op jit(solution)/shard_map/ppermute | solution.py:188
  333.5 11.6 %copy-start.29 = (bf16[512,1024]{1,0:T(8,128)(2,1)S(1)}, bf16[512,1024]{1,0:T(8,128)(2,1)}, u32[]{:S(2)}) copy-start(bf16[512,1024]{1,0:T(8,128)(2,1)} %copy-done.27) | copy-start | bytes 3145732
  345.0 3.6 copy-start.7
  345.0 3.6 copy-start.30
  347.5 4.9 copy-start.18
  347.5 90.0 %collective-permute-start.12 = (bf16[512,1024]{1,0:T(8,128)(2,1)S(1)}, bf16[512,1024]{1,0:T(8,128)(2,1)S(1)}, u32[]{:S(2)}, u32[]{:S(2)}) collective-permute-start(bf16[512,1024]{1,0:T(8,128)(2,1)S(1)} %add_convert_fusion.4), channel_id=1, source_target_pairs={{0,1},{1,0},{2,3},{3,2},{4,5},{5,4},{6,7},{7,6},{8,9},{9,8},{10,11... | collective-permute-start | bytes 3145736 | tf_op jit(solution)/shard_map/ppermute | solution.py:184
  350.6 4.5 copy-start.26
  350.6 4.5 copy-start.40
  350.7 36.7 %collective-permute-start.15 = (bf16[256,1024]{1,0:T(8,128)(2,1)S(1)}, bf16[256,1024]{1,0:T(8,128)(2,1)S(1)}, u32[]{:S(2)}, u32[]{:S(2)}) collective-permute-start(bf16[256,1024]{1,0:T(8,128)(2,1)S(1)} %slice.325), channel_id=1, source_target_pairs={{0,4},{4,0},{8,12},{12,8},{16,20},{20,16},{24,28},{28,24},{1,5},{5... | collective-permute-start | bytes 1572872 | tf_op jit(solution)/shard_map/ppermute | solution.py:188
  354.5 88.6 %collective-permute-start.14 = (bf16[256,1024]{1,0:T(8,128)(2,1)S(1)}, bf16[256,1024]{1,0:T(8,128)(2,1)S(1)}, u32[]{:S(2)}, u32[]{:S(2)}) collective-permute-start(bf16[256,1024]{1,0:T(8,128)(2,1)S(1)} %slice.321), channel_id=1, source_target_pairs={{0,4},{4,0},{8,12},{12,8},{16,20},{20,16},{24,28},{28,24},{1,5},{5... | collective-permute-start | bytes 1572872 | tf_op jit(solution)/shard_map/ppermute | solution.py:188
  357.1 4.4 copy-start.15
  357.1 83.2 %collective-permute-start.3 = (bf16[512,1024]{1,0:T(8,128)(2,1)S(1)}, bf16[512,1024]{1,0:T(8,128)(2,1)S(1)}, u32[]{:S(2)}, u32[]{:S(2)}) collective-permute-start(bf16[512,1024]{1,0:T(8,128)(2,1)S(1)} %add_convert_fusion.9), channel_id=1, source_target_pairs={{0,1},{1,0},{2,3},{3,2},{4,5},{5,4},{6,7},{7,6},{8,9},{9,8},{10,11... | collective-permute-start | bytes 3145736 | tf_op jit(solution)/shard_map/ppermute | solution.py:184
  360.2 78.2 %copy-start.5 = (f32[512,1024]{1,0:T(8,128)S(1)}, f32[512,1024]{1,0:T(8,128)}, u32[]{:S(2)}) copy-start(f32[512,1024]{1,0:T(8,128)} %fusion.86) | copy-start | bytes 6291460
  360.2 75.9 %collective-permute-start.6 = (bf16[256,1024]{1,0:T(8,128)(2,1)S(1)}, bf16[256,1024]{1,0:T(8,128)(2,1)S(1)}, u32[]{:S(2)}, u32[]{:S(2)}) collective-permute-start(bf16[256,1024]{1,0:T(8,128)(2,1)S(1)} %slice.305), channel_id=1, source_target_pairs={{0,4},{4,0},{8,12},{12,8},{16,20},{20,16},{24,28},{28,24},{1,5},{5... | collective-permute-start | bytes 1572872 | tf_op jit(solution)/shard_map/ppermute | solution.py:188
  387.4 63.8 %collective-permute-start.5 = (bf16[256,1024]{1,0:T(8,128)(2,1)S(1)}, bf16[256,1024]{1,0:T(8,128)(2,1)S(1)}, u32[]{:S(2)}, u32[]{:S(2)}) collective-permute-start(bf16[256,1024]{1,0:T(8,128)(2,1)S(1)} %slice.301), channel_id=1, source_target_pairs={{0,4},{4,0},{8,12},{12,8},{16,20},{20,16},{24,28},{28,24},{1,5},{5... | collective-permute-start | bytes 1572872 | tf_op jit(solution)/shard_map/ppermute | solution.py:188
  436.1 14.8 %collective-permute-start.16 = (bf16[256,1024]{1,0:T(8,128)(2,1)S(1)}, bf16[256,1024]{1,0:T(8,128)(2,1)S(1)}, u32[]{:S(2)}, u32[]{:S(2)}) collective-permute-start(bf16[256,1024]{1,0:T(8,128)(2,1)S(1)} %add_convert_fusion.13), channel_id=1, source_target_pairs={{0,1},{1,0},{2,3},{3,2},{4,5},{5,4},{6,7},{7,6},{8,9},{9,8},{10,11... | collective-permute-start | bytes 1572872 | tf_op jit(solution)/shard_map/ppermute | solution.py:184
  437.5 23.2 %collective-permute-start.7 = (bf16[256,1024]{1,0:T(8,128)(2,1)S(1)}, bf16[256,1024]{1,0:T(8,128)(2,1)S(1)}, u32[]{:S(2)}, u32[]{:S(2)}) collective-permute-start(bf16[256,1024]{1,0:T(8,128)(2,1)S(1)} %add_convert_fusion.18), channel_id=1, source_target_pairs={{0,1},{1,0},{2,3},{3,2},{4,5},{5,4},{6,7},{7,6},{8,9},{9,8},{10,11... | collective-permute-start | bytes 1572872 | tf_op jit(solution)/shard_map/ppermute | solution.py:184
  440.3 20.8 %collective-permute-start.13 = (bf16[256,1024]{1,0:T(8,128)(2,1)S(1)}, bf16[256,1024]{1,0:T(8,128)(2,1)S(1)}, u32[]{:S(2)}, u32[]{:S(2)}) collective-permute-start(bf16[256,1024]{1,0:T(8,128)(2,1)S(1)} %slice.317), channel_id=1, source_target_pairs={{0,4},{4,0},{8,12},{12,8},{16,20},{20,16},{24,28},{28,24},{1,5},{5... | collective-permute-start | bytes 1572872 | tf_op jit(solution)/shard_map/ppermute | solution.py:188
  443.1 26.5 %collective-permute-start.4 = (bf16[256,1024]{1,0:T(8,128)(2,1)S(1)}, bf16[256,1024]{1,0:T(8,128)(2,1)S(1)}, u32[]{:S(2)}, u32[]{:S(2)}) collective-permute-start(bf16[256,1024]{1,0:T(8,128)(2,1)S(1)} %slice.297), channel_id=1, source_target_pairs={{0,4},{4,0},{8,12},{12,8},{16,20},{20,16},{24,28},{28,24},{1,5},{5... | collective-permute-start | bytes 1572872 | tf_op jit(solution)/shard_map/ppermute | solution.py:188
  461.3 35.2 %collective-permute-start.17 = (bf16[128,2048]{1,0:T(8,128)(2,1)S(1)}, bf16[128,2048]{1,0:T(8,128)(2,1)S(1)}, u32[]{:S(2)}, u32[]{:S(2)}) collective-permute-start(bf16[128,2048]{1,0:T(8,128)(2,1)S(1)} %pad_maximum_fusion), channel_id=1, source_target_pairs={{0,16},{4,20},{8,24},{12,28},{16,0},{20,4},{24,8},{28,12},{1,17},{... | collective-permute-start | bytes 1572872 | tf_op jit(solution)/shard_map/ppermute | solution.py:188
  469.8 37.9 %collective-permute-start.8 = (bf16[128,2048]{1,0:T(8,128)(2,1)S(1)}, bf16[128,2048]{1,0:T(8,128)(2,1)S(1)}, u32[]{:S(2)}, u32[]{:S(2)}) collective-permute-start(bf16[128,2048]{1,0:T(8,128)(2,1)S(1)} %pad_maximum_fusion.1), channel_id=1, source_target_pairs={{0,16},{4,20},{8,24},{12,28},{16,0},{20,4},{24,8},{28,12},{1,17},{... | collective-permute-start | bytes 1572872 | tf_op jit(solution)/shard_map/ppermute | solution.py:188
  471.7 49.7 %copy-start.1 = (s32[2,4096]{1,0:T(2,128)S(1)}, s32[2,4096]{1,0:T(2,128)}, u32[]{:S(2)}) copy-start(s32[2,4096]{1,0:T(2,128)} %param.17) | copy-start | bytes 98308
  496.6 16.7 %collective-permute-start.18 = (bf16[64,2048]{1,0:T(8,128)(2,1)S(1)}, bf16[64,2048]{1,0:T(8,128)(2,1)S(1)}, u32[]{:S(2)}, u32[]{:S(2)}) collective-permute-start(bf16[64,2048]{1,0:T(8,128)(2,1)S(1)} %slice.329), channel_id=1, source_target_pairs={{0,8},{4,12},{8,0},{12,4},{16,24},{20,28},{24,16},{28,20},{1,9},{5... | collective-permute-start | bytes 786440 | tf_op jit(solution)/shard_map/ppermute | solution.py:188
  507.9 11.0 %collective-permute-start.9 = (bf16[64,2048]{1,0:T(8,128)(2,1)S(1)}, bf16[64,2048]{1,0:T(8,128)(2,1)S(1)}, u32[]{:S(2)}, u32[]{:S(2)}) collective-permute-start(bf16[64,2048]{1,0:T(8,128)(2,1)S(1)} %slice.309), channel_id=1, source_target_pairs={{0,8},{4,12},{8,0},{12,4},{16,24},{20,28},{24,16},{28,20},{1,9},{5... | collective-permute-start | bytes 786440 | tf_op jit(solution)/shard_map/ppermute | solution.py:188
  (13 other events, 27.2 us)
Sparse Core Ops, SparseCore 0:
  13.4 119.5 all-gather.2
  135.8 75.3 all-gather.4
  309.6 119.7 reduce-scatter.1

commit v5 on v4

--- a/solution.py
+++ b/solution.py
@@ -55,6 +55,7 @@
 def attend(qkv, seg_row, seg_column):
     rows, width = qkv.shape[0], qkv.shape[1] // 3
     pairs = width // PAIR
+    block = rows // 2
     scale = HEAD_DIM ** (-0.5)
 
     def kernel(seg_row_ref, seg_column_ref, q_ref, k_ref, v_ref, out_ref, lse_ref, bias_ref):
@@ -63,18 +64,20 @@
             fill_bias(seg_row_ref, seg_column_ref, bias_ref)
 
         query, keyed, valued = q_ref[...], k_ref[...], v_ref[...]
-        found = []
-        for head in (0, 1):
-            chosen = query * (lanes_of(head) * scale).astype(jnp.bfloat16)
-            scores = contract_last(keyed, chosen) + bias_ref[...]
-            top = jnp.max(scores, axis=0, keepdims=True)
-            expanded = jnp.exp(scores - top)
-            total = jnp.sum(expanded, axis=0, keepdims=True)
-            lse_ref[head, :, :] = top + jnp.log(total)
-            probs = (expanded * (1.0 / total)).astype(jnp.bfloat16)
-            found.append(contract_rows(probs, valued))
         lane = lax.broadcasted_iota(jnp.int32, (1, PAIR), 1)
-        out_ref[...] = jnp.where(lane < HEAD_DIM, found[0], found[1]).astype(jnp.bfloat16)
+        for low in range(0, rows, block):
+            high = low + block
+            found = []
+            for head in (0, 1):
+                chosen = query[low:high] * (lanes_of(head) * scale).astype(jnp.bfloat16)
+                scores = contract_last(keyed[:high], chosen) + bias_ref[:high, low:high]
+                top = jnp.max(scores, axis=0, keepdims=True)
+                expanded = jnp.exp(scores - top)
+                total = jnp.sum(expanded, axis=0, keepdims=True)
+                lse_ref[head, :, low:high] = top + jnp.log(total)
+                probs = (expanded * (1.0 / total)).astype(jnp.bfloat16)
+                found.append(contract_rows(probs, valued[:high]))
+            out_ref[low:high, :] = jnp.where(lane < HEAD_DIM, found[0], found[1]).astype(jnp.bfloat16)
 
     return pl.pallas_call(
         kernel,
@@ -102,6 +105,7 @@
 def attend_back(qkv, d_attended, lse, seg_row, seg_column):
     rows, width = qkv.shape[0], qkv.shape[1] // 3
     pairs = width // PAIR
+    block = rows // 2
     scale = HEAD_DIM ** (-0.5)
 
     def kernel(seg_row_ref, seg_column_ref, q_ref, k_ref, v_ref, d_ref, lse_ref, out_ref, bias_ref):
@@ -113,23 +117,34 @@
 
         query, keyed, valued, d_out = q_ref[...], k_ref[...], v_ref[...], d_ref[...]
         scaled = query * jnp.bfloat16(scale)
-        d_query, d_key, d_value = [], [], []
-        for head in (0, 1):
-            lanes = lanes_of(head)
-            scores = contract_last(keyed, scaled * lanes) + bias_ref[...]
-            probs = jnp.exp(scores - lse_ref[head, :, :])
-            d_probs = contract_last(valued, d_out * lanes)
-            inner = jnp.sum(probs * d_probs, axis=0, keepdims=True)
-            d_scores = (probs * (d_probs - inner)).astype(jnp.bfloat16)
-            d_value.append(plain_dot(probs.astype(jnp.bfloat16), d_out))
-            d_key.append(plain_dot(d_scores, scaled))
-            d_query.append(contract_rows(d_scores, keyed) * scale)
         lane = lax.broadcasted_iota(jnp.int32, (1, PAIR), 1)
-        for at, pair in enumerate((d_query, d_key, d_value)):
+        first = lane < HEAD_DIM
+
+        def store(at, low, high, pair):
             column = pl.multiple_of(at * width + step * PAIR, PAIR)
-            out_ref[:, pl.ds(column, PAIR)] = jnp.where(lane < HEAD_DIM, pair[0], pair[1]).astype(
-                jnp.bfloat16
-            )
+            out_ref[low:high, pl.ds(column, PAIR)] = jnp.where(first, pair[0], pair[1]).astype(jnp.bfloat16)
+
+        d_key, d_value = [None, None], [None, None]
+        for low in reversed(range(0, rows, block)):
+            high = low + block
+            d_query = []
+            for head in (0, 1):
+                lanes = lanes_of(head)
+                scores = contract_last(keyed[:high], scaled[low:high] * lanes) + bias_ref[:high, low:high]
+                probs = jnp.exp(scores - lse_ref[head, :, low:high])
+                d_probs = contract_last(valued[:high], d_out[low:high] * lanes)
+                inner = jnp.sum(probs * d_probs, axis=0, keepdims=True)
+                d_scores = (probs * (d_probs - inner)).astype(jnp.bfloat16)
+                more_value = plain_dot(probs.astype(jnp.bfloat16), d_out[low:high])
+                more_key = plain_dot(d_scores, scaled[low:high])
+                d_query.append(contract_rows(d_scores, keyed[:high]) * scale)
+                if d_key[head] is not None:
+                    more_value = more_value + d_value[head][:high]
+                    more_key = more_key + d_key[head][:high]
+                d_value[head], d_key[head] = more_value, more_key
+            store(0, low, high, d_query)
+            store(1, low, high, [part[low:] for part in d_key])
+            store(2, low, high, [part[low:] for part in d_value])
 
     return pl.pallas_call(
         kernel,
@@ -148,6 +163,19 @@
         scratch_shapes=[pltpu.VMEM((rows, rows), jnp.float32)],
         name="attend_back",
     )(seg_row, seg_column, qkv, qkv, qkv, d_attended, lse)
+
+
+def side_by_side(parts):
+    columns = [part.shape[1] for part in parts]
+
+    def kernel(*refs):
+        at = 0
+        for ref, count in zip(refs[:-1], columns):
+            refs[-1][:, at : at + count] = ref[...]
+            at += count
+
+    shape = jax.ShapeDtypeStruct((parts[0].shape[0], sum(columns)), parts[0].dtype)
+    return pl.pallas_call(kernel, out_shape=shape, name="side_by_side")(*parts)
 
 
 def swap_cores(values):
@@ -286,7 +314,7 @@
 
     vectors = jnp.stack([attn_gain, mlp_gain, router_w], axis=1)
     vectors = jnp.pad(vectors, ((0, 0), (0, 128 - 3)))
-    near = jnp.concatenate([w_query, w_key, w_value, w_output, w_up, vectors], axis=1)
+    near = side_by_side([w_query, w_key, w_value, w_output, w_up, vectors])
     near = lax.all_gather(near, ALL, axis=0, tiled=True).reshape(sides, width, -1)
     far = lax.all_gather(w_down, ALL, axis=0, tiled=True).reshape(sides, width, -1)
     full_qkv = [near[t, :, : 3 * heads] for t in range(sides)]
@@ -321,12 +349,16 @@
     hidden_act = [jax.nn.gelu(hidden_pre[t], approximate=True).astype(jnp.bfloat16) for t in range(sides)]
     own_act = [jnp.where(side == 0, hidden_act[t], hidden_act[1 - t]) for t in range(sides)]
     left_down = relative_order(d_mlp_low, False)
+    slope = []
+    for t in range(sides):
+        _, gelu_back = jax.vjp(partial(jax.nn.gelu, approximate=True), hidden_pre[t])
+        slope.append(gelu_back(jnp.ones_like(hidden_pre[t]))[0])
+    slope, own_act = lax.optimization_barrier((slope, own_act))
     sum_down, _ = halve_grads(left_down, own_act)
     d_pre = []
     for t in range(sides):
-        _, gelu_back = jax.vjp(partial(jax.nn.gelu, approximate=True), hidden_pre[t])
         d_act = plain_dot(d_mlp_low, full_down[t])
-        d_pre.append(gelu_back(d_act)[0].astype(jnp.bfloat16))
+        d_pre.append((d_act * slope[t]).astype(jnp.bfloat16))
     own_pre = [jnp.where(side == 0, d_pre[t], d_pre[1 - t]) for t in range(sides)]
     left_up = relative_order(normed_mlp, False)
     sum_up, sent_up = halve_grads(left_up, own_pre)

time: 538 us -> 533 us (level)
  waiting for transfers between devices: 268 us -> 261 us
  other arithmetic: 19.2 us -> 24.6 us
    all_gather x1, waiting for transfers between devices: 29.2 us -> 19.7 us  [block(): lax.all_gather(w_down, ALL, axis=0, tiled=True).reshape(sides, width, -1)]
  transfers between devices with their start and end apart: 27 -> 27, of which waited for: 12 -> 12; matrix products, arithmetic and copies ran while one was open for 23% -> 24% of each run, Pallas kernels for 11% -> 11%
where the time goes in v5:
time: 533 us; the launch traced here: 524 us
  waiting for transfers between devices  261 us (49%)
  matrix products  112 us (21%)
  Pallas kernels  61.5 us (12%)
  local copies, waits for them, and re-layouts  25.3 us (5%)
  other arithmetic  24.6 us (5%)
  starting transfers between devices  24.3 us (5%)
  between operations  15.1 us (3%)
    ppermute x13, waiting for transfers between devices, swap_chips(): lax.ppermute(values, 'chips', [(i, i ^ bit) for i in range(lax.axis_size(...  123 us
    all_gather x1, waiting for transfers between devices, block(): lax.all_gather(near, ALL, axis=0, tiled=True).reshape(sides, width, -1)  101 us
    dot_general x12, matrix products, plain_dot(): return jnp.dot(left, right, preferred_element_type=jnp.float32)  53.7 us
    dot_general x20, matrix products, contract_rows(): lax.dot_general(left, right, (((0,), (0,)), ((), ())), preferred_element_...  33.3 us
    dot_general x8, matrix products, contract_last(): lax.dot_general(left, right, (((1,), (1,)), ((), ())), preferred_element_...  25.2 us
    pallas_call x2, Pallas kernels, place(): pl.pallas_call(kernel, grid=(tokens // step,), out_shape=jax.ShapeDtypeSt...  22.8 us
    pallas_call x2, Pallas kernels, attend_back(): pl.pallas_call(kernel, grid=(pairs,), out_shape=jax.ShapeDtypeStruct((row...  21.5 us
    all_gather x1, waiting for transfers between devices, block(): lax.all_gather(w_down, ALL, axis=0, tiled=True).reshape(sides, width, -1)  19.7 us
  transfers between devices with their start and end apart: 27, of which 12 were waited for; matrix products, arithmetic and copies ran while one was open for 24% of the time, Pallas kernels for 11%

profile of v5, /device:TPU:0, one launch (start us, length us, event | category | flops | bytes accessed | tf_op | source)
XLA Modules:
  0.0 524.1 jit_solution(1621581588249487790)
XLA Ops:
  8.7 1.9 side_by_side.1
  13.4 7.2 %gather_fusion = bf16[512,1024]{1,0:T(8,128)(2,1)S(1)} fusion(bf16[4096,1024]{1,0:T(8,128)(2,1)} %whole_ref.2, s32[1024]{0:T(1024)S(1)} %pad_clamp_fusion), kind=kCustom, calls=%fused_computation.clone | custom fusion | bytes 2099200 | tf_op jit(solution)/shard_map/jit(_take)/gather | solution.py:329
  20.6 8.4 %gather_fusion.1 = bf16[512,1024]{1,0:T(8,128)(2,1)} fusion(bf16[4096,1024]{1,0:T(8,128)(2,1)} %whole_ref.3, s32[1024]{0:T(1024)S(1)} %pad_clamp_fusion), kind=kCustom, calls=%fused_computation.1.clone | custom fusion | bytes 2099200 | tf_op jit(solution)/shard_map/jit(_take)/gather | solution.py:330
  29.5 101.5 %all-gather.3.cloned.1.call-done = bf16[2048,4224]{1,0:T(8,128)(2,1)} async-done(((bf16[64,4224]{1,0:T(8,128)(2,1)}), bf16[2048,4224]{1,0:T(8,128)(2,1)}) %all-gather.3.cloned.1.call-update) | async-done | bytes 17301520 | tf_op jit(solution)/shard_map/all_gather | solution.py:318
  132.3 5.0 convolution_convert_fusion.9.q_ref.k_ref.v_ref
  137.3 7.5 %attend.2 = (bf16[512,512]{1,0:T(8,128)(2,1)}, f32[8,1,512]{2,1,0:T(1,128)}) custom-call(s32[1,512]{1,0:T(1,128)} %bitcast.127, s32[512,1]{1,0:T(8,128)} %copy.55.seg_column_ref, bf16[512,1536]{1,0:T(8,128)(2,1)} %convolution_convert_fusion.9.q_ref.k_ref.v_ref, bf16[512,1536]{1,0:T(8,128)(2,1)} %convolution_convert_fusion.9.q_ref.k_ref.v_ref, ...), custom_call_target="tpu_custom_call" | custom-call | tf_op jit(solution)/shard_map/attend/pallas_call | solution.py:82
  144.8 5.1 convolution_convert_fusion.8.q_ref.k_ref.v_ref
  149.8 7.8 %attend.3 = (bf16[512,512]{1,0:T(8,128)(2,1)}, f32[8,1,512]{2,1,0:T(1,128)}) custom-call(s32[1,512]{1,0:T(1,128)} %bitcast.128, s32[512,1]{1,0:T(8,128)} %copy.55.seg_column_ref, bf16[512,1536]{1,0:T(8,128)(2,1)} %convolution_convert_fusion.8.q_ref.k_ref.v_ref, bf16[512,1536]{1,0:T(8,128)(2,1)} %convolution_convert_fusion.8.q_ref.k_ref.v_ref, ...), custom_call_target="tpu_custom_call" | custom-call | tf_op jit(solution)/shard_map/attend/pallas_call | solution.py:82
  157.7 2.2 fusion.100
  159.8 2.4 multiply_reduce_fusion.2
  162.7 8.6 %fusion.11 = (f32[512,2048]{1,0:T(8,128)}, f32[512,2048]{1,0:T(8,128)S(1)}) fusion(bf16[512,1024]{1,0:T(8,128)(2,1)S(1)} %multiply_convert_fusion.4, bf16[2,1024,4224]{2,1,0:T(8,128)(2,1)} %bitcast.113), kind=kOutput, calls=%fused_computation.40 | convolution fusion | flops 2165309440 | bytes 13631488 | tf_op jit(solution)/shard_map/dot_general | solution.py:27
  171.3 8.6 %fusion.5 = (f32[512,2048]{1,0:T(8,128)}, f32[512,2048]{1,0:T(8,128)S(1)}) fusion(bf16[512,1024]{1,0:T(8,128)(2,1)S(1)} %multiply_convert_fusion.4, bf16[2,1024,4224]{2,1,0:T(8,128)(2,1)} %bitcast.114), kind=kOutput, calls=%fused_computation.34 | convolution fusion | flops 2165309440 | bytes 13631488 | tf_op jit(solution)/shard_map/dot_general | solution.py:27
  179.9 3.8 broadcast_select_fusion.2
  185.0 1.6 broadcast_select_fusion.3
  186.6 2.9 convolution_convert_fusion.13
  189.5 19.7 %all-gather.5.cloned.1.call-done = bf16[2048,2048]{1,0:T(8,128)(2,1)} async-done(((bf16[64,2048]{1,0:T(8,128)(2,1)}), bf16[2048,2048]{1,0:T(8,128)(2,1)}) %all-gather.5.cloned.1.call-update) | async-done | bytes 8388624 | tf_op jit(solution)/shard_map/all_gather | solution.py:319
  209.2 7.6 %multiply_convert_fusion.1 = bf16[512,2048]{1,0:T(8,128)(2,1)} fusion(f32[512,2048]{1,0:T(8,128)} %get-tuple-element.28, bf16[2048,2048]{1,0:T(8,128)(2,1)} %all-gather.5.cloned.1.call-done, f32[512]{0:T(512)S(1)} %add_divide_fusion, bf16[512,1024]{1,0:T(8,128)(2,1)} %gather_fusion.1, pred[512]{0:T(512)(128)(4,1)S(1)} %compare_and_fusion), kind=kOutput, calls=%fused_computation.60 | convolution fusion | flops 2151677952 | bytes 11536896 | tf_op jit(solution)/shard_map/dot_general | solution.py:27
  216.9 7.2 %broadcast_select_fusion = (bf16[512,2048]{1,0:T(8,128)(2,1)S(1)}, bf16[512,2048]{1,0:T(8,128)(2,1)S(1)}, bf16[512,2048]{1,0:T(8,128)(2,1)}) fusion(bf16[512,2048]{1,0:T(8,128)(2,1)} %multiply_convert_fusion.1, pred[]{:T(512)S(6)} %eq.25, f32[512,2048]{1,0:T(8,128)} %get-tuple-element.29, bf16[2048,2048]{1,0:T(8,128)(2,1)} %all-gather.5.cloned.1.call-done, ...), kind=kOutput, calls=%fused_computation.129 | convolution fusion | flops 2153775104 | bytes 17828352 | tf_op jit(solution)/shard_map/dot_general | solution.py:27
  224.1 2.6 convolution_convert_fusion.6
  226.7 2.6 convolution_convert_fusion.7
  230.5 2.4 fusion.26
  232.9 2.9 multiply_reduce_fusion
  237.2 1.5 convolution_convert_fusion.18.d_ref
  238.8 1.5 convolution_convert_fusion.19.d_ref
  240.8 2.5 convolution_convert_fusion.12
  243.3 10.8 %attend_back.3 = bf16[512,1536]{1,0:T(8,128)(2,1)} custom-call(s32[1,512]{1,0:T(1,128)} %bitcast.129, s32[512,1]{1,0:T(8,128)} %copy.55.seg_column_ref, bf16[512,1536]{1,0:T(8,128)(2,1)} %convolution_convert_fusion.8.q_ref.k_ref.v_ref, bf16[512,1536]{1,0:T(8,128)(2,1)} %convolution_convert_fusion.8.q_ref.k_ref.v_ref, ...), custom_call_target="tpu_custom_call" | custom-call | tf_op jit(solution)/shard_map/attend_back/pallas_call | solution.py:149
  254.1 10.7 %attend_back.2 = bf16[512,1536]{1,0:T(8,128)(2,1)} custom-call(s32[1,512]{1,0:T(1,128)} %bitcast.130, s32[512,1]{1,0:T(8,128)} %copy.55.seg_column_ref, bf16[512,1536]{1,0:T(8,128)(2,1)} %convolution_convert_fusion.9.q_ref.k_ref.v_ref, bf16[512,1536]{1,0:T(8,128)(2,1)} %convolution_convert_fusion.9.q_ref.k_ref.v_ref, ...), custom_call_target="tpu_custom_call" | custom-call | tf_op jit(solution)/shard_map/attend_back/pallas_call | solution.py:149
  264.8 2.7 fusion.47
  268.8 1.6 convolution_convert_fusion.11
  272.5 2.4 fusion.30
  274.9 3.9 fusion.55
  278.7 3.7 fusion.42
  283.9 5.4 %fusion.53 = (f32[1024]{0:T(1024)S(1)}, f32[512]{0:T(512)S(1)}, f32[1024]{0:T(1024)S(1)}, f32[512,1024]{1,0:T(8,128)}) fusion(f32[512]{0:T(512)S(1)} %fusion.134, bf16[512,1024]{1,0:T(8,128)(2,1)S(1)} %gather_fusion, pred[512]{0:T(512)(128)(4,1)S(1)} %compare_and_fusion, f32[1024]{0:T(1024)S(1)} %bitcast.148, f32[512]{0:T(512)S(1)} %fusion.133, ...), kind=kOutput, calls=%fused_computation.103 | convolution fusion | flops 1616377344 | bytes 9980416 | tf_op jit(solution)/shard_map/dot_general | solution.py:37
  289.7 1.5 convolution_convert_fusion.10
  291.2 2.6 convolution_convert_fusion.4
  297.2 2.7 convolution_convert_fusion.5
  302.3 2.7 add_convert_fusion
  306.1 4.3 fusion.58.rows_ref
  310.4 2.0 collective-permute-start.22
  312.4 2.1 fusion.98
  317.8 11.3 %place_rows.3 = bf16[4096,1024]{1,0:T(8,128)(2,1)} custom-call(s32[1,512]{1,0:T(1,128)} %copy-done.31, bf16[4096,1024]{1,0:T(8,128)(2,1)} %whole_ref.3, bf16[512,1024]{1,0:T(8,128)(2,1)} %fusion.58.rows_ref), custom_call_target="tpu_custom_call" | custom-call | tf_op jit(solution)/shard_map/place_rows/pallas_call | solution.py:268
  329.0 11.5 %place_rows.2 = bf16[4096,1024]{1,0:T(8,128)(2,1)} custom-call(s32[1,512]{1,0:T(1,128)} %copy-done.31, bf16[4096,1024]{1,0:T(8,128)(2,1)} %whole_ref.2, bf16[512,1024]{1,0:T(8,128)(2,1)} %get-tuple-element.53.rows_ref), custom_call_target="tpu_custom_call" | custom-call | tf_op jit(solution)/shard_map/place_rows/pallas_call | solution.py:268
  340.7 2.4 add_convert_fusion.4
  344.2 2.0 add_convert_fusion.1
  346.2 1.8 collective-permute-start.15
  348.0 2.0 add_convert_fusion.2
  350.7 2.0 add_convert_fusion.9
  353.8 2.0 add_convert_fusion.6
  357.1 2.0 add_convert_fusion.7
  359.1 23.8 %collective-permute-done.15 = bf16[256,1024]{1,0:T(8,128)(2,1)S(1)} collective-permute-done((bf16[256,1024]{1,0:T(8,128)(2,1)S(1)}, bf16[256,1024]{1,0:T(8,128)(2,1)S(1)}, u32[]{:S(2)}, u32[]{:S(2)}) %collective-permute-start.15) | collective-permute-done | bytes 524320 | tf_op jit(solution)/shard_map/ppermute | solution.py:216
  382.9 2.2 collective-permute-start.5
  385.3 46.3 %collective-permute-done.6 = bf16[256,1024]{1,0:T(8,128)(2,1)S(1)} collective-permute-done((bf16[256,1024]{1,0:T(8,128)(2,1)S(1)}, bf16[256,1024]{1,0:T(8,128)(2,1)S(1)}, u32[]{:S(2)}, u32[]{:S(2)}) %collective-permute-start.6) | collective-permute-done | bytes 524320 | tf_op jit(solution)/shard_map/ppermute | solution.py:216
  433.9 1.8 add_convert_fusion.3
  436.8 1.8 add_convert_fusion.8
  439.8 6.6 %collective-permute-done.16 = bf16[256,1024]{1,0:T(8,128)(2,1)S(1)} collective-permute-done((bf16[256,1024]{1,0:T(8,128)(2,1)S(1)}, bf16[256,1024]{1,0:T(8,128)(2,1)S(1)}, u32[]{:S(2)}, u32[]{:S(2)}) %collective-permute-start.16) | collective-permute-done | bytes 524320 | tf_op jit(solution)/shard_map/ppermute | solution.py:212
  446.7 9.6 %collective-permute-done.7 = bf16[256,1024]{1,0:T(8,128)(2,1)S(1)} collective-permute-done((bf16[256,1024]{1,0:T(8,128)(2,1)S(1)}, bf16[256,1024]{1,0:T(8,128)(2,1)S(1)}, u32[]{:S(2)}, u32[]{:S(2)}) %collective-permute-start.7) | collective-permute-done | bytes 524320 | tf_op jit(solution)/shard_map/ppermute | solution.py:212
  456.8 1.7 collective-permute-start.17
  458.5 6.6 %collective-permute-done.4 = bf16[256,1024]{1,0:T(8,128)(2,1)S(1)} collective-permute-done((bf16[256,1024]{1,0:T(8,128)(2,1)S(1)}, bf16[256,1024]{1,0:T(8,128)(2,1)S(1)}, u32[]{:S(2)}, u32[]{:S(2)}) %collective-permute-start.4) | collective-permute-done | bytes 524320 | tf_op jit(solution)/shard_map/ppermute | solution.py:216
  465.3 1.6 collective-permute-start.8
  467.5 24.7 %collective-permute-done.17 = bf16[128,2048]{1,0:T(8,128)(2,1)S(1)} collective-permute-done((bf16[128,2048]{1,0:T(8,128)(2,1)S(1)}, bf16[128,2048]{1,0:T(8,128)(2,1)S(1)}, u32[]{:S(2)}, u32[]{:S(2)}) %collective-permute-start.17) | collective-permute-done | bytes 524320 | tf_op jit(solution)/shard_map/ppermute | solution.py:216
  493.0 10.4 %collective-permute-done.8 = bf16[128,2048]{1,0:T(8,128)(2,1)S(1)} collective-permute-done((bf16[128,2048]{1,0:T(8,128)(2,1)S(1)}, bf16[128,2048]{1,0:T(8,128)(2,1)S(1)}, u32[]{:S(2)}, u32[]{:S(2)}) %collective-permute-start.8) | collective-permute-done | bytes 524320 | tf_op jit(solution)/shard_map/ppermute | solution.py:216
  503.6 5.4 %collective-permute-done.18 = bf16[64,2048]{1,0:T(8,128)(2,1)S(1)} collective-permute-done((bf16[64,2048]{1,0:T(8,128)(2,1)S(1)}, bf16[64,2048]{1,0:T(8,128)(2,1)S(1)}, u32[]{:S(2)}, u32[]{:S(2)}) %collective-permute-start.18) | collective-permute-done | bytes 262176 | tf_op jit(solution)/shard_map/ppermute | solution.py:216
  509.8 4.7 collective-permute-done.9
  515.4 1.7 fusion.147
  (203 shorter events, 39.1 us)
Async XLA Ops:
  7.2 5.0 copy-start
  7.2 123.9 %all-gather.3.cloned.1.call-start = ((), (), s32[]{:S(2)}) async-start(), calls=%async_computation.1 | async-start | bytes 17842176 | tf_op jit(solution)/shard_map/all_gather | solution.py:318
  10.6 198.6 %all-gather.5.cloned.1.call-start = ((), (), s32[]{:S(2)}) async-start(), calls=%async_computation.2 | async-start | bytes 8650752 | tf_op jit(solution)/shard_map/all_gather | solution.py:319
  11.4 504.0 %reduce-scatter.2.cloned.1.call-start = ((), (), s32[]{:S(2)}) async-start(), calls=%async_computation.3 | async-start | bytes 4456448 | tf_op jit(solution)/shard_map/reduce_scatter | solution.py:190
  12.1 16.9 %copy-start.31 = (s32[1,512]{1,0:T(1,128)}, s32[1,512]{1,0:T(1,128)S(1)}, u32[]{:S(2)}) copy-start(s32[1,512]{1,0:T(1,128)S(1)} %constant_dynamic-slice_fusion.1.index_ref) | copy-start | bytes 6148
  12.5 8.1 %copy-start.32 = (s32[512]{0:T(512)}, s32[512]{0:T(512)S(1)}, u32[]{:S(2)}) copy-start(s32[512]{0:T(512)S(1)} %convert_reduce_fusion.1) | copy-start | bytes 6148
  149.8 7.8 %copy-start.22 = (bf16[512,512]{1,0:T(8,128)(2,1)S(1)}, bf16[512,512]{1,0:T(8,128)(2,1)}, u32[]{:S(2)}) copy-start(bf16[512,512]{1,0:T(8,128)(2,1)} %get-tuple-element.26) | copy-start | bytes 1572868
  183.7 2.9 copy-start.8
  209.2 7.6 %copy-start.2 = (bf16[512,1024]{1,0:T(8,128)(2,1)S(1)}, bf16[512,1024]{1,0:T(8,128)(2,1)}, u32[]{:S(2)}) copy-start(bf16[512,1024]{1,0:T(8,128)(2,1)} %gather_fusion.1) | copy-start | bytes 3145732
  216.9 7.2 %copy-start.24 = (bf16[512,1024]{1,0:T(8,128)(2,1)S(1)}, bf16[512,1024]{1,0:T(8,128)(2,1)}, u32[]{:S(2)}) copy-start(bf16[512,1024]{1,0:T(8,128)(2,1)} %convolution_convert_fusion.13) | copy-start | bytes 3145732
  216.9 12.4 %slice-start = ((s8[17301504]{0:T(1024)(128)(4,1)}), s8[4194304]{0:T(1024)(128)(4,1)S(1)}, s32[]{:S(2)}) async-start(s8[17301504]{0:T(1024)(128)(4,1)} %bitcast.117), calls=%async_computation.4 | async-start | bytes 8388608
  216.9 12.4 %slice-start.1 = ((s8[17301504]{0:T(1024)(128)(4,1)}), s8[4194304]{0:T(1024)(128)(4,1)S(1)}, s32[]{:S(2)}) async-start(s8[17301504]{0:T(1024)(128)(4,1)} %bitcast.117), calls=%async_computation.5 | async-start | bytes 8388608
  216.9 12.4 %slice-start.2 = ((s8[17301504]{0:T(1024)(128)(4,1)}), s8[4194304]{0:T(1024)(128)(4,1)S(1)}, s32[]{:S(2)}) async-start(s8[17301504]{0:T(1024)(128)(4,1)} %bitcast.117), calls=%async_computation.6 | async-start | bytes 8388608
  216.9 12.4 %slice-start.3 = ((s8[17301504]{0:T(1024)(128)(4,1)}), s8[4194304]{0:T(1024)(128)(4,1)S(1)}, s32[]{:S(2)}) async-start(s8[17301504]{0:T(1024)(128)(4,1)} %bitcast.117), calls=%async_computation.7 | async-start | bytes 8388608
  224.1 5.2 copy-start.19
  224.1 5.2 copy-start.34
  224.1 5.2 slice-start.4
  226.7 3.8 copy-start.37
  230.5 2.4 copy-start.36
  235.8 2.9 copy-start.4
  237.2 6.1 %copy-start.17 = (bf16[512,1024]{1,0:T(8,128)(2,1)}, bf16[512,1024]{1,0:T(8,128)(2,1)S(1)}, u32[]{:S(2)}) copy-start(bf16[512,1024]{1,0:T(8,128)(2,1)S(1)} %fusion.54) | copy-start | bytes 3145732
  240.3 110.3 %collective-permute-start.2 = (bf16[512,2048]{1,0:T(8,128)(2,1)}, bf16[512,2048]{1,0:T(8,128)(2,1)}, u32[]{:S(2)}, u32[]{:S(2)}) collective-permute-start(bf16[512,2048]{1,0:T(8,128)(2,1)} %convolution_convert_fusion.6), channel_id=1, source_target_pairs={{0,2},{2,0},{1,3},{3,1},{4,6},{6,4},{5,7},{7,5},{8,10},{10,8},{9,1... | collective-permute-start | bytes 6291464 | tf_op jit(solution)/shard_map/ppermute | solution.py:182
  240.6 115.2 %collective-permute-start.1 = (bf16[512,2048]{1,0:T(8,128)(2,1)}, bf16[512,2048]{1,0:T(8,128)(2,1)}, u32[]{:S(2)}, u32[]{:S(2)}) collective-permute-start(bf16[512,2048]{1,0:T(8,128)(2,1)} %convolution_convert_fusion.7), channel_id=1, source_target_pairs={{0,2},{2,0},{1,3},{3,1},{4,6},{6,4},{5,7},{7,5},{8,10},{10,8},{9,1... | collective-permute-start | bytes 6291464 | tf_op jit(solution)/shard_map/ppermute | solution.py:182
  264.8 2.7 copy-start.16
  264.8 2.7 copy-start.38
  267.6 3.8 slice-start.5
  268.8 2.6 copy-start.9
  268.8 3.7 slice-start.6
  283.3 17.4 %collective-permute-start = (bf16[2,512,2048]{2,1,0:T(8,128)(2,1)S(1)}, bf16[2,512,2048]{2,1,0:T(8,128)(2,1)S(1)}, u32[]{:S(2)}, u32[]{:S(2)}) collective-permute-start(bf16[2,512,2048]{2,1,0:T(8,128)(2,1)S(1)} %maximum_maximum_fusion), channel_id=1, source_target_pairs={{0,2},{2,0},{1,3},{3,1},{4,6},{6,4},{5,7},{7,5},{8,10},{10,8},{9,1... | collective-permute-start | bytes 12582920 | tf_op jit(solution)/shard_map/ppermute | solution.py:182
  289.3 11.1 %collective-permute-start.19 = (f32[3,1024]{1,0:T(4,128)S(1)}, f32[3,1024]{1,0:T(4,128)S(1)}, u32[]{:S(2)}, u32[]{:S(2)}) collective-permute-start(f32[3,1024]{1,0:T(4,128)S(1)} %pad_maximum_fusion.2), channel_id=1, source_target_pairs={{0,2},{2,0},{1,3},{3,1},{4,6},{6,4},{5,7},{7,5},{8,10},{10,8},{9,1... | collective-permute-start | bytes 36872 | tf_op jit(solution)/shard_map/ppermute | solution.py:182
  291.2 5.4 %copy-start.27 = (bf16[512,1024]{1,0:T(8,128)(2,1)}, bf16[512,1024]{1,0:T(8,128)(2,1)S(1)}, u32[]{:S(2)}) copy-start(bf16[512,1024]{1,0:T(8,128)(2,1)S(1)} %convolution_convert_fusion.10) | copy-start | bytes 3145732
  293.8 46.9 %collective-permute-start.11 = (bf16[512,2048]{1,0:T(8,128)(2,1)}, bf16[512,2048]{1,0:T(8,128)(2,1)}, u32[]{:S(2)}, u32[]{:S(2)}) collective-permute-start(bf16[512,2048]{1,0:T(8,128)(2,1)} %convolution_convert_fusion.4), channel_id=1, source_target_pairs={{0,2},{2,0},{1,3},{3,1},{4,6},{6,4},{5,7},{7,5},{8,10},{10,8},{9,1... | collective-permute-start | bytes 6291464 | tf_op jit(solution)/shard_map/ppermute | solution.py:182
  300.4 47.6 %collective-permute-start.10 = (bf16[512,2048]{1,0:T(8,128)(2,1)}, bf16[512,2048]{1,0:T(8,128)(2,1)}, u32[]{:S(2)}, u32[]{:S(2)}) collective-permute-start(bf16[512,2048]{1,0:T(8,128)(2,1)} %convolution_convert_fusion.5), channel_id=1, source_target_pairs={{0,2},{2,0},{1,3},{3,1},{4,6},{6,4},{5,7},{7,5},{8,10},{10,8},{9,1... | collective-permute-start | bytes 6291464 | tf_op jit(solution)/shard_map/ppermute | solution.py:182
  300.8 4.2 collective-permute-start.20
  305.0 5.4 %collective-permute-start.21 = (f32[3,1024]{1,0:T(4,128)S(1)}, f32[3,1024]{1,0:T(4,128)S(1)}, u32[]{:S(2)}, u32[]{:S(2)}) collective-permute-start(f32[3,1024]{1,0:T(4,128)S(1)} %fusion.175), channel_id=1, source_target_pairs={{0,1},{1,0},{2,3},{3,2},{4,5},{5,4},{6,7},{7,6},{8,9},{9,8},{10,11... | collective-permute-start | bytes 36872 | tf_op jit(solution)/shard_map/ppermute | solution.py:212
  306.1 6.3 %copy-start.11 = (bf16[512,2048]{1,0:T(8,128)(2,1)S(1)}, bf16[512,2048]{1,0:T(8,128)(2,1)}, u32[]{:S(2)}) copy-start(bf16[512,2048]{1,0:T(8,128)(2,1)} %broadcast_select_fusion.3) | copy-start | bytes 6291460
  306.1 6.3 %copy-start.28 = (bf16[512,1024]{1,0:T(8,128)(2,1)S(1)}, bf16[512,1024]{1,0:T(8,128)(2,1)}, u32[]{:S(2)}) copy-start(bf16[512,1024]{1,0:T(8,128)(2,1)} %copy-done.27) | copy-start | bytes 3145732
  306.1 10.9 %copy-start.20 = (bf16[512,2048]{1,0:T(8,128)(2,1)S(1)}, bf16[512,2048]{1,0:T(8,128)(2,1)}, u32[]{:S(2)}) copy-start(bf16[512,2048]{1,0:T(8,128)(2,1)} %copy-done.19) | copy-start | bytes 6291460
  306.1 10.9 %copy-start.25 = (bf16[512,1024]{1,0:T(8,128)(2,1)S(1)}, bf16[512,1024]{1,0:T(8,128)(2,1)}, u32[]{:S(2)}) copy-start(bf16[512,1024]{1,0:T(8,128)(2,1)} %convolution_convert_fusion.13) | copy-start | bytes 3145732
  310.4 5.2 collective-permute-start.22
  315.6 25.0 %collective-permute-start.23 = (f32[3,1024]{1,0:T(4,128)S(1)}, f32[3,1024]{1,0:T(4,128)S(1)}, u32[]{:S(2)}, u32[]{:S(2)}) collective-permute-start(f32[3,1024]{1,0:T(4,128)S(1)} %add.310), channel_id=1, source_target_pairs={{0,8},{4,12},{8,0},{12,4},{16,24},{20,28},{24,16},{28,20},{1,9},{5... | collective-permute-start | bytes 36872 | tf_op jit(solution)/shard_map/ppermute | solution.py:216
  329.0 11.6 %copy-start.29 = (bf16[512,1024]{1,0:T(8,128)(2,1)S(1)}, bf16[512,1024]{1,0:T(8,128)(2,1)}, u32[]{:S(2)}) copy-start(bf16[512,1024]{1,0:T(8,128)(2,1)} %copy-done.27) | copy-start | bytes 3145732
  340.6 3.6 copy-start.14
  340.6 3.6 copy-start.30
  343.1 4.9 copy-start.12
  343.1 89.8 %collective-permute-start.12 = (bf16[512,1024]{1,0:T(8,128)(2,1)S(1)}, bf16[512,1024]{1,0:T(8,128)(2,1)S(1)}, u32[]{:S(2)}, u32[]{:S(2)}) collective-permute-start(bf16[512,1024]{1,0:T(8,128)(2,1)S(1)} %add_convert_fusion.4), channel_id=1, source_target_pairs={{0,1},{1,0},{2,3},{3,2},{4,5},{5,4},{6,7},{7,6},{8,9},{9,8},{10,11... | collective-permute-start | bytes 3145736 | tf_op jit(solution)/shard_map/ppermute | solution.py:212
  346.2 4.5 copy-start.26
  346.2 4.5 copy-start.35
  346.2 36.7 %collective-permute-start.15 = (bf16[256,1024]{1,0:T(8,128)(2,1)S(1)}, bf16[256,1024]{1,0:T(8,128)(2,1)S(1)}, u32[]{:S(2)}, u32[]{:S(2)}) collective-permute-start(bf16[256,1024]{1,0:T(8,128)(2,1)S(1)} %slice.321), channel_id=1, source_target_pairs={{0,4},{4,0},{8,12},{12,8},{16,20},{20,16},{24,28},{28,24},{1,5},{5... | collective-permute-start | bytes 1572872 | tf_op jit(solution)/shard_map/ppermute | solution.py:216
  350.0 88.6 %collective-permute-start.14 = (bf16[256,1024]{1,0:T(8,128)(2,1)S(1)}, bf16[256,1024]{1,0:T(8,128)(2,1)S(1)}, u32[]{:S(2)}, u32[]{:S(2)}) collective-permute-start(bf16[256,1024]{1,0:T(8,128)(2,1)S(1)} %slice.318), channel_id=1, source_target_pairs={{0,4},{4,0},{8,12},{12,8},{16,20},{20,16},{24,28},{28,24},{1,5},{5... | collective-permute-start | bytes 1572872 | tf_op jit(solution)/shard_map/ppermute | solution.py:216
  352.6 4.4 copy-start.21
  352.7 83.1 %collective-permute-start.3 = (bf16[512,1024]{1,0:T(8,128)(2,1)S(1)}, bf16[512,1024]{1,0:T(8,128)(2,1)S(1)}, u32[]{:S(2)}, u32[]{:S(2)}) collective-permute-start(bf16[512,1024]{1,0:T(8,128)(2,1)S(1)} %add_convert_fusion.9), channel_id=1, source_target_pairs={{0,1},{1,0},{2,3},{3,2},{4,5},{5,4},{6,7},{7,6},{8,9},{9,8},{10,11... | collective-permute-start | bytes 3145736 | tf_op jit(solution)/shard_map/ppermute | solution.py:212
  355.8 78.2 %copy-start.5 = (f32[512,1024]{1,0:T(8,128)S(1)}, f32[512,1024]{1,0:T(8,128)}, u32[]{:S(2)}) copy-start(f32[512,1024]{1,0:T(8,128)} %fusion.98) | copy-start | bytes 6291460
  355.8 75.8 %collective-permute-start.6 = (bf16[256,1024]{1,0:T(8,128)(2,1)S(1)}, bf16[256,1024]{1,0:T(8,128)(2,1)S(1)}, u32[]{:S(2)}, u32[]{:S(2)}) collective-permute-start(bf16[256,1024]{1,0:T(8,128)(2,1)S(1)} %slice.305), channel_id=1, source_target_pairs={{0,4},{4,0},{8,12},{12,8},{16,20},{20,16},{24,28},{28,24},{1,5},{5... | collective-permute-start | bytes 1572872 | tf_op jit(solution)/shard_map/ppermute | solution.py:216
  382.9 63.8 %collective-permute-start.5 = (bf16[256,1024]{1,0:T(8,128)(2,1)S(1)}, bf16[256,1024]{1,0:T(8,128)(2,1)S(1)}, u32[]{:S(2)}, u32[]{:S(2)}) collective-permute-start(bf16[256,1024]{1,0:T(8,128)(2,1)S(1)} %slice.301), channel_id=1, source_target_pairs={{0,4},{4,0},{8,12},{12,8},{16,20},{20,16},{24,28},{28,24},{1,5},{5... | collective-permute-start | bytes 1572872 | tf_op jit(solution)/shard_map/ppermute | solution.py:216
  431.6 14.8 %collective-permute-start.16 = (bf16[256,1024]{1,0:T(8,128)(2,1)S(1)}, bf16[256,1024]{1,0:T(8,128)(2,1)S(1)}, u32[]{:S(2)}, u32[]{:S(2)}) collective-permute-start(bf16[256,1024]{1,0:T(8,128)(2,1)S(1)} %add_convert_fusion.13), channel_id=1, source_target_pairs={{0,1},{1,0},{2,3},{3,2},{4,5},{5,4},{6,7},{7,6},{8,9},{9,8},{10,11... | collective-permute-start | bytes 1572872 | tf_op jit(solution)/shard_map/ppermute | solution.py:212
  432.9 23.4 %collective-permute-start.7 = (bf16[256,1024]{1,0:T(8,128)(2,1)S(1)}, bf16[256,1024]{1,0:T(8,128)(2,1)S(1)}, u32[]{:S(2)}, u32[]{:S(2)}) collective-permute-start(bf16[256,1024]{1,0:T(8,128)(2,1)S(1)} %add_convert_fusion.18), channel_id=1, source_target_pairs={{0,1},{1,0},{2,3},{3,2},{4,5},{5,4},{6,7},{7,6},{8,9},{9,8},{10,11... | collective-permute-start | bytes 1572872 | tf_op jit(solution)/shard_map/ppermute | solution.py:212
  435.8 20.8 %collective-permute-start.13 = (bf16[256,1024]{1,0:T(8,128)(2,1)S(1)}, bf16[256,1024]{1,0:T(8,128)(2,1)S(1)}, u32[]{:S(2)}, u32[]{:S(2)}) collective-permute-start(bf16[256,1024]{1,0:T(8,128)(2,1)S(1)} %slice.315), channel_id=1, source_target_pairs={{0,4},{4,0},{8,12},{12,8},{16,20},{20,16},{24,28},{28,24},{1,5},{5... | collective-permute-start | bytes 1572872 | tf_op jit(solution)/shard_map/ppermute | solution.py:216
  438.6 26.4 %collective-permute-start.4 = (bf16[256,1024]{1,0:T(8,128)(2,1)S(1)}, bf16[256,1024]{1,0:T(8,128)(2,1)S(1)}, u32[]{:S(2)}, u32[]{:S(2)}) collective-permute-start(bf16[256,1024]{1,0:T(8,128)(2,1)S(1)} %slice.297), channel_id=1, source_target_pairs={{0,4},{4,0},{8,12},{12,8},{16,20},{20,16},{24,28},{28,24},{1,5},{5... | collective-permute-start | bytes 1572872 | tf_op jit(solution)/shard_map/ppermute | solution.py:216
  456.8 35.3 %collective-permute-start.17 = (bf16[128,2048]{1,0:T(8,128)(2,1)S(1)}, bf16[128,2048]{1,0:T(8,128)(2,1)S(1)}, u32[]{:S(2)}, u32[]{:S(2)}) collective-permute-start(bf16[128,2048]{1,0:T(8,128)(2,1)S(1)} %pad_maximum_fusion), channel_id=1, source_target_pairs={{0,16},{4,20},{8,24},{12,28},{16,0},{20,4},{24,8},{28,12},{1,17},{... | collective-permute-start | bytes 1572872 | tf_op jit(solution)/shard_map/ppermute | solution.py:216
  465.3 38.1 %collective-permute-start.8 = (bf16[128,2048]{1,0:T(8,128)(2,1)S(1)}, bf16[128,2048]{1,0:T(8,128)(2,1)S(1)}, u32[]{:S(2)}, u32[]{:S(2)}) collective-permute-start(bf16[128,2048]{1,0:T(8,128)(2,1)S(1)} %pad_maximum_fusion.1), channel_id=1, source_target_pairs={{0,16},{4,20},{8,24},{12,28},{16,0},{20,4},{24,8},{28,12},{1,17},{... | collective-permute-start | bytes 1572872 | tf_op jit(solution)/shard_map/ppermute | solution.py:216
  466.9 50.2 %copy-start.1 = (s32[2,4096]{1,0:T(2,128)S(1)}, s32[2,4096]{1,0:T(2,128)}, u32[]{:S(2)}) copy-start(s32[2,4096]{1,0:T(2,128)} %param.17) | copy-start | bytes 98308
  492.3 16.7 %collective-permute-start.18 = (bf16[64,2048]{1,0:T(8,128)(2,1)S(1)}, bf16[64,2048]{1,0:T(8,128)(2,1)S(1)}, u32[]{:S(2)}, u32[]{:S(2)}) collective-permute-start(bf16[64,2048]{1,0:T(8,128)(2,1)S(1)} %slice.325), channel_id=1, source_target_pairs={{0,8},{4,12},{8,0},{12,4},{16,24},{20,28},{24,16},{28,20},{1,9},{5... | collective-permute-start | bytes 786440 | tf_op jit(solution)/shard_map/ppermute | solution.py:216
  503.5 11.0 %collective-permute-start.9 = (bf16[64,2048]{1,0:T(8,128)(2,1)S(1)}, bf16[64,2048]{1,0:T(8,128)(2,1)S(1)}, u32[]{:S(2)}, u32[]{:S(2)}) collective-permute-start(bf16[64,2048]{1,0:T(8,128)(2,1)S(1)} %slice.309), channel_id=1, source_target_pairs={{0,8},{4,12},{8,0},{12,4},{16,24},{20,28},{24,16},{28,20},{1,9},{5... | collective-permute-start | bytes 786440 | tf_op jit(solution)/shard_map/ppermute | solution.py:216
  (9 other events, 15.9 us)
Sparse Core Ops, SparseCore 0:
  11.5 119.5 all-gather.2
  133.9 75.2 all-gather.4
  305.1 119.7 reduce-scatter.1

commit v6 on v4

--- a/solution.py
+++ b/solution.py
@@ -150,6 +150,19 @@
     )(seg_row, seg_column, qkv, qkv, qkv, d_attended, lse)
 
 
+def side_by_side(parts):
+    columns = [part.shape[1] for part in parts]
+
+    def kernel(*refs):
+        at = 0
+        for ref, count in zip(refs[:-1], columns):
+            refs[-1][:, at : at + count] = ref[...]
+            at += count
+
+    shape = jax.ShapeDtypeStruct((parts[0].shape[0], sum(columns)), parts[0].dtype)
+    return pl.pallas_call(kernel, out_shape=shape, name="side_by_side")(*parts)
+
+
 def swap_cores(values):
     return lax.ppermute(values, "core", [(0, 1), (1, 0)])
 
@@ -220,9 +233,12 @@
     part_b = [add_low(part_b[t][:quarter], got_b[t]) for t in (0, 1)]
     got_a = swap_chips(part_a[quarter:], 1)
     got_b = swap_sides(part_b[1])
-    part_a = add_low(part_a[:quarter], got_a)
-    part_b = add_low(part_b[0], got_b)
-    return halve_line(jnp.concatenate([part_a, part_b], axis=1)), sent
+    return (part_a[:quarter], got_a, part_b[0], got_b), sent
+
+
+def finish_grads(state):
+    part_a, got_a, part_b, got_b = state
+    return halve_line(jnp.concatenate([add_low(part_a, got_a), add_low(part_b, got_b)], axis=1))
 
 
 def place(whole, rows, index):
@@ -286,7 +302,7 @@
 
     vectors = jnp.stack([attn_gain, mlp_gain, router_w], axis=1)
     vectors = jnp.pad(vectors, ((0, 0), (0, 128 - 3)))
-    near = jnp.concatenate([w_query, w_key, w_value, w_output, w_up, vectors], axis=1)
+    near = side_by_side([w_query, w_key, w_value, w_output, w_up, vectors])
     near = lax.all_gather(near, ALL, axis=0, tiled=True).reshape(sides, width, -1)
     far = lax.all_gather(w_down, ALL, axis=0, tiled=True).reshape(sides, width, -1)
     full_qkv = [near[t, :, : 3 * heads] for t in range(sides)]
@@ -321,25 +337,32 @@
     hidden_act = [jax.nn.gelu(hidden_pre[t], approximate=True).astype(jnp.bfloat16) for t in range(sides)]
     own_act = [jnp.where(side == 0, hidden_act[t], hidden_act[1 - t]) for t in range(sides)]
     left_down = relative_order(d_mlp_low, False)
-    sum_down, _ = halve_grads(left_down, own_act)
+    slope = []
+    for t in range(sides):
+        _, gelu_back = jax.vjp(partial(jax.nn.gelu, approximate=True), hidden_pre[t])
+        slope.append(gelu_back(jnp.ones_like(hidden_pre[t]))[0])
+    slope, own_act = lax.optimization_barrier((slope, own_act))
+    state_down, _ = halve_grads(left_down, own_act)
     d_pre = []
     for t in range(sides):
-        _, gelu_back = jax.vjp(partial(jax.nn.gelu, approximate=True), hidden_pre[t])
         d_act = plain_dot(d_mlp_low, full_down[t])
-        d_pre.append(gelu_back(d_act)[0].astype(jnp.bfloat16))
+        d_pre.append((d_act * slope[t]).astype(jnp.bfloat16))
     own_pre = [jnp.where(side == 0, d_pre[t], d_pre[1 - t]) for t in range(sides)]
     left_up = relative_order(normed_mlp, False)
-    sum_up, sent_up = halve_grads(left_up, own_pre)
+    state_up, sent_up = halve_grads(left_up, own_pre)
     d_pre, sent_up = lax.optimization_barrier((d_pre, sent_up))
 
     d_normed_mlp = sum(contract_last(d_pre[t], full_up[t]) for t in range(sides))
     _, norm_back_mlp = jax.vjp(rms_norm, middle, mlp_gain_f)
     d_middle, d_mlp_gain = norm_back_mlp(d_normed_mlp)
     d_attn_low = (d_branch + d_middle).astype(jnp.bfloat16)
-    d_qkv = []
-    for t in range(sides):
+    d_qkv = [None] * sides
+    for t in reversed(range(sides)):
         d_attended = plain_dot(d_attn_low, full_output[t]).astype(jnp.bfloat16)
-        d_qkv.append(attend_back(qkv[t], d_attended, lse[t], seg_row, seg_column))
+        d_qkv[t] = attend_back(qkv[t], d_attended, lse[t], seg_row, seg_column)
+    state_down, _ = lax.optimization_barrier((state_down, d_qkv[-1]))
+    sum_down = finish_grads(state_down)
+    sum_up = finish_grads(state_up)
     half = width // 2
     left_qkv = relative_order(normed_attn, True)
     left_output = relative_order(d_attn_low, True)

time: 538 us -> 536 us (level)
  other arithmetic: 19.2 us -> 24.6 us
    ppermute x13, waiting for transfers between devices: 122 us -> 134 us  [swap_chips(): lax.ppermute(values, 'chips', [(i, i ^ bit) for i in range(lax.axis_size(...]
    all_gather x1, waiting for transfers between devices: 29.2 us -> 19.8 us  [block(): lax.all_gather(w_down, ALL, axis=0, tiled=True).reshape(sides, width, -1)]
  transfers between devices with their start and end apart: 27 -> 27, of which waited for: 12 -> 13; matrix products, arithmetic and copies ran while one was open for 23% -> 24% of each run, Pallas kernels for 11% -> 11%
where the time goes in v6:
time: 536 us; the launch traced here: 527 us
  waiting for transfers between devices  269 us (50%)
  matrix products  112 us (21%)
  Pallas kernels  60.2 us (11%)
  local copies, waits for them, and re-layouts  25.2 us (5%)
  other arithmetic  24.6 us (5%)
  starting transfers between devices  20.4 us (4%)
  between operations  15.1 us (3%)
    ppermute x13, waiting for transfers between devices, swap_chips(): lax.ppermute(values, 'chips', [(i, i ^ bit) for i in range(lax.axis_size(...  134 us
    all_gather x1, waiting for transfers between devices, block(): lax.all_gather(near, ALL, axis=0, tiled=True).reshape(sides, width, -1)  102 us
    dot_general x12, matrix products, plain_dot(): return jnp.dot(left, right, preferred_element_type=jnp.float32)  53.7 us
    dot_general x20, matrix products, contract_rows(): lax.dot_general(left, right, (((0,), (0,)), ((), ())), preferred_element_...  33.2 us
    dot_general x8, matrix products, contract_last(): lax.dot_general(left, right, (((1,), (1,)), ((), ())), preferred_element_...  25.2 us
    pallas_call x2, Pallas kernels, place(): pl.pallas_call(kernel, grid=(tokens // step,), out_shape=jax.ShapeDtypeSt...  22.8 us
    pallas_call x2, Pallas kernels, attend_back(): pl.pallas_call(kernel, grid=(pairs,), out_shape=jax.ShapeDtypeStruct((row...  20.2 us
    all_gather x1, waiting for transfers between devices, block(): lax.all_gather(w_down, ALL, axis=0, tiled=True).reshape(sides, width, -1)  19.8 us
  transfers between devices with their start and end apart: 27, of which 13 were waited for; matrix products, arithmetic and copies ran while one was open for 24% of the time, Pallas kernels for 11%

profile of v6, /device:TPU:0, one launch (start us, length us, event | category | flops | bytes accessed | tf_op | source)
XLA Modules:
  0.0 527.0 jit_solution(6935792285460062284)
XLA Ops:
  8.7 1.9 side_by_side.1
  13.4 7.2 %gather_fusion = bf16[512,1024]{1,0:T(8,128)(2,1)S(1)} fusion(bf16[4096,1024]{1,0:T(8,128)(2,1)} %whole_ref.2, s32[1024]{0:T(1024)S(1)} %pad_clamp_fusion), kind=kCustom, calls=%fused_computation.clone | custom fusion | bytes 2099200 | tf_op jit(solution)/shard_map/jit(_take)/gather | solution.py:317
  20.6 8.4 %gather_fusion.1 = bf16[512,1024]{1,0:T(8,128)(2,1)} fusion(bf16[4096,1024]{1,0:T(8,128)(2,1)} %whole_ref.3, s32[1024]{0:T(1024)S(1)} %pad_clamp_fusion), kind=kCustom, calls=%fused_computation.1.clone | custom fusion | bytes 2099200 | tf_op jit(solution)/shard_map/jit(_take)/gather | solution.py:318
  29.5 101.5 %all-gather.3.cloned.1.call-done = bf16[2048,4224]{1,0:T(8,128)(2,1)} async-done(((bf16[64,4224]{1,0:T(8,128)(2,1)}), bf16[2048,4224]{1,0:T(8,128)(2,1)}) %all-gather.3.cloned.1.call-update) | async-done | bytes 17301520 | tf_op jit(solution)/shard_map/all_gather | solution.py:306
  132.3 5.0 convolution_convert_fusion.9.q_ref.k_ref.v_ref
  137.3 7.5 %attend.2 = (bf16[512,512]{1,0:T(8,128)(2,1)}, f32[8,1,512]{2,1,0:T(1,128)}) custom-call(s32[1,512]{1,0:T(1,128)} %bitcast.127, s32[512,1]{1,0:T(8,128)} %copy.55.seg_column_ref, bf16[512,1536]{1,0:T(8,128)(2,1)} %convolution_convert_fusion.9.q_ref.k_ref.v_ref, bf16[512,1536]{1,0:T(8,128)(2,1)} %convolution_convert_fusion.9.q_ref.k_ref.v_ref, ...), custom_call_target="tpu_custom_call" | custom-call | tf_op jit(solution)/shard_map/attend/pallas_call | solution.py:79
  144.8 5.1 convolution_convert_fusion.8.q_ref.k_ref.v_ref
  149.8 7.8 %attend.3 = (bf16[512,512]{1,0:T(8,128)(2,1)}, f32[8,1,512]{2,1,0:T(1,128)}) custom-call(s32[1,512]{1,0:T(1,128)} %bitcast.128, s32[512,1]{1,0:T(8,128)} %copy.55.seg_column_ref, bf16[512,1536]{1,0:T(8,128)(2,1)} %convolution_convert_fusion.8.q_ref.k_ref.v_ref, bf16[512,1536]{1,0:T(8,128)(2,1)} %convolution_convert_fusion.8.q_ref.k_ref.v_ref, ...), custom_call_target="tpu_custom_call" | custom-call | tf_op jit(solution)/shard_map/attend/pallas_call | solution.py:79
  157.7 2.2 fusion.100
  159.8 2.4 multiply_reduce_fusion.2
  162.7 8.6 %fusion.11 = (f32[512,2048]{1,0:T(8,128)}, f32[512,2048]{1,0:T(8,128)S(1)}) fusion(bf16[512,1024]{1,0:T(8,128)(2,1)S(1)} %multiply_convert_fusion.4, bf16[2,1024,4224]{2,1,0:T(8,128)(2,1)} %bitcast.113), kind=kOutput, calls=%fused_computation.40 | convolution fusion | flops 2165309440 | bytes 13631488 | tf_op jit(solution)/shard_map/dot_general | solution.py:27
  171.3 8.6 %fusion.5 = (f32[512,2048]{1,0:T(8,128)}, f32[512,2048]{1,0:T(8,128)S(1)}) fusion(bf16[512,1024]{1,0:T(8,128)(2,1)S(1)} %multiply_convert_fusion.4, bf16[2,1024,4224]{2,1,0:T(8,128)(2,1)} %bitcast.114), kind=kOutput, calls=%fused_computation.34 | convolution fusion | flops 2165309440 | bytes 13631488 | tf_op jit(solution)/shard_map/dot_general | solution.py:27
  179.9 3.8 broadcast_select_fusion.2
  186.5 2.9 convolution_convert_fusion.13
  189.4 19.8 %all-gather.5.cloned.1.call-done = bf16[2048,2048]{1,0:T(8,128)(2,1)} async-done(((bf16[64,2048]{1,0:T(8,128)(2,1)}), bf16[2048,2048]{1,0:T(8,128)(2,1)}) %all-gather.5.cloned.1.call-update) | async-done | bytes 8388624 | tf_op jit(solution)/shard_map/all_gather | solution.py:307
  209.2 7.6 %multiply_convert_fusion.1 = bf16[512,2048]{1,0:T(8,128)(2,1)} fusion(f32[512,2048]{1,0:T(8,128)} %get-tuple-element.32, bf16[2048,2048]{1,0:T(8,128)(2,1)} %all-gather.5.cloned.1.call-done, f32[512]{0:T(512)S(1)} %add_divide_fusion, bf16[512,1024]{1,0:T(8,128)(2,1)} %gather_fusion.1, pred[512]{0:T(512)(128)(4,1)S(1)} %compare_and_fusion), kind=kOutput, calls=%fused_computation.60 | convolution fusion | flops 2151677952 | bytes 11536896 | tf_op jit(solution)/shard_map/dot_general | solution.py:27
  216.9 7.2 %broadcast_select_fusion = (bf16[512,2048]{1,0:T(8,128)(2,1)S(1)}, bf16[512,2048]{1,0:T(8,128)(2,1)S(1)}, bf16[512,2048]{1,0:T(8,128)(2,1)}) fusion(bf16[512,2048]{1,0:T(8,128)(2,1)} %multiply_convert_fusion.1, pred[]{:T(512)S(6)} %eq.25, f32[512,2048]{1,0:T(8,128)} %get-tuple-element.33, bf16[2048,2048]{1,0:T(8,128)(2,1)} %all-gather.5.cloned.1.call-done, ...), kind=kOutput, calls=%fused_computation.129 | convolution fusion | flops 2153775104 | bytes 17828352 | tf_op jit(solution)/shard_map/dot_general | solution.py:27
  224.1 2.6 convolution_convert_fusion.6
  226.8 2.6 convolution_convert_fusion.7
  230.5 2.4 fusion.26
  233.0 2.9 multiply_reduce_fusion
  237.2 1.5 convolution_convert_fusion.18.d_ref
  238.8 1.5 convolution_convert_fusion.19.d_ref
  240.8 2.5 convolution_convert_fusion.12
  243.3 10.1 %attend_back.3 = bf16[512,1536]{1,0:T(8,128)(2,1)} custom-call(s32[1,512]{1,0:T(1,128)} %bitcast.129, s32[512,1]{1,0:T(8,128)} %copy.55.seg_column_ref, bf16[512,1536]{1,0:T(8,128)(2,1)} %convolution_convert_fusion.8.q_ref.k_ref.v_ref, bf16[512,1536]{1,0:T(8,128)(2,1)} %convolution_convert_fusion.8.q_ref.k_ref.v_ref, ...), custom_call_target="tpu_custom_call" | custom-call | tf_op jit(solution)/shard_map/attend_back/pallas_call | solution.py:134
  253.4 10.1 %attend_back.2 = bf16[512,1536]{1,0:T(8,128)(2,1)} custom-call(s32[1,512]{1,0:T(1,128)} %bitcast.130, s32[512,1]{1,0:T(8,128)} %copy.55.seg_column_ref, bf16[512,1536]{1,0:T(8,128)(2,1)} %convolution_convert_fusion.9.q_ref.k_ref.v_ref, bf16[512,1536]{1,0:T(8,128)(2,1)} %convolution_convert_fusion.9.q_ref.k_ref.v_ref, ...), custom_call_target="tpu_custom_call" | custom-call | tf_op jit(solution)/shard_map/attend_back/pallas_call | solution.py:134
  263.5 2.7 fusion.47
  267.5 1.6 convolution_convert_fusion.11
  271.2 2.4 fusion.30
  273.6 3.8 fusion.55
  277.4 3.7 fusion.42
  282.5 5.4 %fusion.53 = (f32[1024]{0:T(1024)S(1)}, f32[512]{0:T(512)S(1)}, f32[1024]{0:T(1024)S(1)}, f32[512,1024]{1,0:T(8,128)}) fusion(f32[512]{0:T(512)S(1)} %fusion.134, bf16[512,1024]{1,0:T(8,128)(2,1)S(1)} %gather_fusion, pred[512]{0:T(512)(128)(4,1)S(1)} %compare_and_fusion, f32[1024]{0:T(1024)S(1)} %bitcast.148, f32[512]{0:T(512)S(1)} %fusion.133, ...), kind=kOutput, calls=%fused_computation.103 | convolution fusion | flops 1616377344 | bytes 9980416 | tf_op jit(solution)/shard_map/dot_general | solution.py:37
  289.9 2.7 convolution_convert_fusion.4
  295.4 2.6 convolution_convert_fusion.5
  300.6 1.8 collective-permute-done.20
  302.4 1.6 collective-permute-start.21
  304.0 2.7 add_convert_fusion
  306.8 4.2 fusion.58.rows_ref
  311.1 2.0 collective-permute-start.22
  313.1 2.0 fusion.98
  318.4 11.2 %place_rows.3 = bf16[4096,1024]{1,0:T(8,128)(2,1)} custom-call(s32[1,512]{1,0:T(1,128)} %copy-done.31, bf16[4096,1024]{1,0:T(8,128)(2,1)} %whole_ref.3, bf16[512,1024]{1,0:T(8,128)(2,1)} %fusion.58.rows_ref), custom_call_target="tpu_custom_call" | custom-call | tf_op jit(solution)/shard_map/place_rows/pallas_call | solution.py:256
  329.6 11.5 %place_rows.2 = bf16[4096,1024]{1,0:T(8,128)(2,1)} custom-call(s32[1,512]{1,0:T(1,128)} %copy-done.31, bf16[4096,1024]{1,0:T(8,128)(2,1)} %whole_ref.2, bf16[512,1024]{1,0:T(8,128)(2,1)} %get-tuple-element.61.rows_ref), custom_call_target="tpu_custom_call" | custom-call | tf_op jit(solution)/shard_map/place_rows/pallas_call | solution.py:256
  341.2 2.4 add_convert_fusion.1
  344.3 2.0 add_convert_fusion.2
  346.4 1.5 collective-permute-start.14
  347.9 2.0 add_convert_fusion.4
  350.6 2.0 add_convert_fusion.9
  354.0 2.0 add_convert_fusion.6
  357.0 2.0 add_convert_fusion.7
  359.0 22.4 %collective-permute-done.15 = bf16[256,1024]{1,0:T(8,128)(2,1)S(1)} collective-permute-done((bf16[256,1024]{1,0:T(8,128)(2,1)S(1)}, bf16[256,1024]{1,0:T(8,128)(2,1)S(1)}, u32[]{:S(2)}, u32[]{:S(2)}) %collective-permute-start.15) | collective-permute-done | bytes 524320 | tf_op jit(solution)/shard_map/ppermute | solution.py:201
  381.6 52.2 %collective-permute-done.6 = bf16[256,1024]{1,0:T(8,128)(2,1)S(1)} collective-permute-done((bf16[256,1024]{1,0:T(8,128)(2,1)S(1)}, bf16[256,1024]{1,0:T(8,128)(2,1)S(1)}, u32[]{:S(2)}, u32[]{:S(2)}) %collective-permute-start.6) | collective-permute-done | bytes 524320 | tf_op jit(solution)/shard_map/ppermute | solution.py:201
  434.5 1.6 collective-permute-start.7
  436.4 1.8 add_convert_fusion.3
  438.3 1.8 add_convert_fusion.8
  440.1 2.1 collective-permute-start.4
  442.2 2.9 collective-permute-done.5
  445.1 13.3 %collective-permute-done.7 = bf16[256,1024]{1,0:T(8,128)(2,1)S(1)} collective-permute-done((bf16[256,1024]{1,0:T(8,128)(2,1)S(1)}, bf16[256,1024]{1,0:T(8,128)(2,1)S(1)}, u32[]{:S(2)}, u32[]{:S(2)}) %collective-permute-start.7) | collective-permute-done | bytes 524320 | tf_op jit(solution)/shard_map/ppermute | solution.py:197
  459.1 1.5 collective-permute-start.17
  460.6 6.6 %collective-permute-done.4 = bf16[256,1024]{1,0:T(8,128)(2,1)S(1)} collective-permute-done((bf16[256,1024]{1,0:T(8,128)(2,1)S(1)}, bf16[256,1024]{1,0:T(8,128)(2,1)S(1)}, u32[]{:S(2)}, u32[]{:S(2)}) %collective-permute-start.4) | collective-permute-done | bytes 524320 | tf_op jit(solution)/shard_map/ppermute | solution.py:201
  469.3 26.2 %collective-permute-done.17 = bf16[128,2048]{1,0:T(8,128)(2,1)S(1)} collective-permute-done((bf16[128,2048]{1,0:T(8,128)(2,1)S(1)}, bf16[128,2048]{1,0:T(8,128)(2,1)S(1)}, u32[]{:S(2)}, u32[]{:S(2)}) %collective-permute-start.17) | collective-permute-done | bytes 524320 | tf_op jit(solution)/shard_map/ppermute | solution.py:201
  495.7 10.6 %collective-permute-done.8 = bf16[128,2048]{1,0:T(8,128)(2,1)S(1)} collective-permute-done((bf16[128,2048]{1,0:T(8,128)(2,1)S(1)}, bf16[128,2048]{1,0:T(8,128)(2,1)S(1)}, u32[]{:S(2)}, u32[]{:S(2)}) %collective-permute-start.8) | collective-permute-done | bytes 524320 | tf_op jit(solution)/shard_map/ppermute | solution.py:201
  506.5 5.4 %collective-permute-done.18 = bf16[64,2048]{1,0:T(8,128)(2,1)S(1)} collective-permute-done((bf16[64,2048]{1,0:T(8,128)(2,1)S(1)}, bf16[64,2048]{1,0:T(8,128)(2,1)S(1)}, u32[]{:S(2)}, u32[]{:S(2)}) %collective-permute-start.18) | collective-permute-done | bytes 262176 | tf_op jit(solution)/shard_map/ppermute | solution.py:201
  512.7 4.7 collective-permute-done.9
  518.3 1.7 fusion.148
  (204 shorter events, 37.4 us)
Async XLA Ops:
  7.2 5.0 copy-start
  7.2 123.9 %all-gather.3.cloned.1.call-start = ((), (), s32[]{:S(2)}) async-start(), calls=%async_computation.1 | async-start | bytes 17842176 | tf_op jit(solution)/shard_map/all_gather | solution.py:306
  10.6 198.6 %all-gather.5.cloned.1.call-start = ((), (), s32[]{:S(2)}) async-start(), calls=%async_computation.2 | async-start | bytes 8650752 | tf_op jit(solution)/shard_map/all_gather | solution.py:307
  11.4 506.9 %reduce-scatter.2.cloned.1.call-start = ((), (), s32[]{:S(2)}) async-start(), calls=%async_computation.3 | async-start | bytes 4456448 | tf_op jit(solution)/shard_map/reduce_scatter | solution.py:175
  12.1 16.9 %copy-start.31 = (s32[1,512]{1,0:T(1,128)}, s32[1,512]{1,0:T(1,128)S(1)}, u32[]{:S(2)}) copy-start(s32[1,512]{1,0:T(1,128)S(1)} %constant_dynamic-slice_fusion.1.index_ref) | copy-start | bytes 6148
  12.5 8.1 %copy-start.32 = (s32[512]{0:T(512)}, s32[512]{0:T(512)S(1)}, u32[]{:S(2)}) copy-start(s32[512]{0:T(512)S(1)} %convert_reduce_fusion.1) | copy-start | bytes 6148
  149.8 7.8 %copy-start.22 = (bf16[512,512]{1,0:T(8,128)(2,1)S(1)}, bf16[512,512]{1,0:T(8,128)(2,1)}, u32[]{:S(2)}) copy-start(bf16[512,512]{1,0:T(8,128)(2,1)} %get-tuple-element.30) | copy-start | bytes 1572868
  183.7 2.8 copy-start.8
  209.2 7.7 %copy-start.2 = (bf16[512,1024]{1,0:T(8,128)(2,1)S(1)}, bf16[512,1024]{1,0:T(8,128)(2,1)}, u32[]{:S(2)}) copy-start(bf16[512,1024]{1,0:T(8,128)(2,1)} %gather_fusion.1) | copy-start | bytes 3145732
  216.9 7.3 %copy-start.24 = (bf16[512,1024]{1,0:T(8,128)(2,1)S(1)}, bf16[512,1024]{1,0:T(8,128)(2,1)}, u32[]{:S(2)}) copy-start(bf16[512,1024]{1,0:T(8,128)(2,1)} %convolution_convert_fusion.13) | copy-start | bytes 3145732
  216.9 12.5 %slice-start = ((s8[17301504]{0:T(1024)(128)(4,1)}), s8[4194304]{0:T(1024)(128)(4,1)S(1)}, s32[]{:S(2)}) async-start(s8[17301504]{0:T(1024)(128)(4,1)} %bitcast.117), calls=%async_computation.4 | async-start | bytes 8388608
  216.9 12.5 %slice-start.1 = ((s8[17301504]{0:T(1024)(128)(4,1)}), s8[4194304]{0:T(1024)(128)(4,1)S(1)}, s32[]{:S(2)}) async-start(s8[17301504]{0:T(1024)(128)(4,1)} %bitcast.117), calls=%async_computation.5 | async-start | bytes 8388608
  216.9 12.5 %slice-start.2 = ((s8[17301504]{0:T(1024)(128)(4,1)}), s8[4194304]{0:T(1024)(128)(4,1)S(1)}, s32[]{:S(2)}) async-start(s8[17301504]{0:T(1024)(128)(4,1)} %bitcast.117), calls=%async_computation.6 | async-start | bytes 8388608
  216.9 12.5 %slice-start.3 = ((s8[17301504]{0:T(1024)(128)(4,1)}), s8[4194304]{0:T(1024)(128)(4,1)S(1)}, s32[]{:S(2)}) async-start(s8[17301504]{0:T(1024)(128)(4,1)} %bitcast.117), calls=%async_computation.7 | async-start | bytes 8388608
  224.1 5.2 copy-start.19
  224.1 5.2 copy-start.34
  224.1 5.2 slice-start.4
  226.7 3.8 copy-start.37
  230.5 2.4 copy-start.36
  235.8 2.9 copy-start.4
  237.2 6.1 %copy-start.17 = (bf16[512,1024]{1,0:T(8,128)(2,1)}, bf16[512,1024]{1,0:T(8,128)(2,1)S(1)}, u32[]{:S(2)}) copy-start(bf16[512,1024]{1,0:T(8,128)(2,1)S(1)} %fusion.54) | copy-start | bytes 3145732
  240.3 110.3 %collective-permute-start.2 = (bf16[512,2048]{1,0:T(8,128)(2,1)}, bf16[512,2048]{1,0:T(8,128)(2,1)}, u32[]{:S(2)}, u32[]{:S(2)}) collective-permute-start(bf16[512,2048]{1,0:T(8,128)(2,1)} %convolution_convert_fusion.6), channel_id=1, source_target_pairs={{0,2},{2,0},{1,3},{3,1},{4,6},{6,4},{5,7},{7,5},{8,10},{10,8},{9,1... | collective-permute-start | bytes 6291464 | tf_op jit(solution)/shard_map/ppermute | solution.py:167
  240.6 115.5 %collective-permute-start.1 = (bf16[512,2048]{1,0:T(8,128)(2,1)}, bf16[512,2048]{1,0:T(8,128)(2,1)}, u32[]{:S(2)}, u32[]{:S(2)}) collective-permute-start(bf16[512,2048]{1,0:T(8,128)(2,1)} %convolution_convert_fusion.7), channel_id=1, source_target_pairs={{0,2},{2,0},{1,3},{3,1},{4,6},{6,4},{5,7},{7,5},{8,10},{10,8},{9,1... | collective-permute-start | bytes 6291464 | tf_op jit(solution)/shard_map/ppermute | solution.py:167
  263.5 2.7 copy-start.16
  263.5 2.7 copy-start.38
  266.3 3.8 slice-start.5
  267.5 2.6 copy-start.9
  267.5 3.7 slice-start.6
  282.0 20.4 %collective-permute-start = (bf16[2,512,2048]{2,1,0:T(8,128)(2,1)S(1)}, bf16[2,512,2048]{2,1,0:T(8,128)(2,1)S(1)}, u32[]{:S(2)}, u32[]{:S(2)}) collective-permute-start(bf16[2,512,2048]{2,1,0:T(8,128)(2,1)S(1)} %maximum_maximum_fusion), channel_id=1, source_target_pairs={{0,2},{2,0},{1,3},{3,1},{4,6},{6,4},{5,7},{7,5},{8,10},{10,8},{9,1... | collective-permute-start | bytes 12582920 | tf_op jit(solution)/shard_map/ppermute | solution.py:167
  288.0 10.6 %collective-permute-start.19 = (f32[3,1024]{1,0:T(4,128)S(1)}, f32[3,1024]{1,0:T(4,128)S(1)}, u32[]{:S(2)}, u32[]{:S(2)}) collective-permute-start(f32[3,1024]{1,0:T(4,128)S(1)} %pad_maximum_fusion.2), channel_id=1, source_target_pairs={{0,2},{2,0},{1,3},{3,1},{4,6},{6,4},{5,7},{7,5},{8,10},{10,8},{9,1... | collective-permute-start | bytes 36872 | tf_op jit(solution)/shard_map/ppermute | solution.py:167
  289.9 5.0 copy-start.27
  292.6 48.6 %collective-permute-start.11 = (bf16[512,2048]{1,0:T(8,128)(2,1)}, bf16[512,2048]{1,0:T(8,128)(2,1)}, u32[]{:S(2)}, u32[]{:S(2)}) collective-permute-start(bf16[512,2048]{1,0:T(8,128)(2,1)} %convolution_convert_fusion.4), channel_id=1, source_target_pairs={{0,2},{2,0},{1,3},{3,1},{4,6},{6,4},{5,7},{7,5},{8,10},{10,8},{9,1... | collective-permute-start | bytes 6291464 | tf_op jit(solution)/shard_map/ppermute | solution.py:167
  298.6 3.8 collective-permute-start.20
  302.4 41.9 %collective-permute-start.10 = (bf16[512,2048]{1,0:T(8,128)(2,1)}, bf16[512,2048]{1,0:T(8,128)(2,1)}, u32[]{:S(2)}, u32[]{:S(2)}) collective-permute-start(bf16[512,2048]{1,0:T(8,128)(2,1)} %convolution_convert_fusion.5), channel_id=1, source_target_pairs={{0,2},{2,0},{1,3},{3,1},{4,6},{6,4},{5,7},{7,5},{8,10},{10,8},{9,1... | collective-permute-start | bytes 6291464 | tf_op jit(solution)/shard_map/ppermute | solution.py:167
  302.4 8.6 %collective-permute-start.21 = (f32[3,1024]{1,0:T(4,128)S(1)}, f32[3,1024]{1,0:T(4,128)S(1)}, u32[]{:S(2)}, u32[]{:S(2)}) collective-permute-start(f32[3,1024]{1,0:T(4,128)S(1)} %fusion.176), channel_id=1, source_target_pairs={{0,1},{1,0},{2,3},{3,2},{4,5},{5,4},{6,7},{7,6},{8,9},{9,8},{10,11... | collective-permute-start | bytes 36872 | tf_op jit(solution)/shard_map/ppermute | solution.py:197
  306.8 6.3 %copy-start.11 = (bf16[512,2048]{1,0:T(8,128)(2,1)S(1)}, bf16[512,2048]{1,0:T(8,128)(2,1)}, u32[]{:S(2)}) copy-start(bf16[512,2048]{1,0:T(8,128)(2,1)} %broadcast_select_fusion.3) | copy-start | bytes 6291460
  306.8 6.3 %copy-start.28 = (bf16[512,1024]{1,0:T(8,128)(2,1)S(1)}, bf16[512,1024]{1,0:T(8,128)(2,1)}, u32[]{:S(2)}) copy-start(bf16[512,1024]{1,0:T(8,128)(2,1)} %copy-done.27) | copy-start | bytes 3145732
  306.8 10.8 %copy-start.20 = (bf16[512,2048]{1,0:T(8,128)(2,1)S(1)}, bf16[512,2048]{1,0:T(8,128)(2,1)}, u32[]{:S(2)}) copy-start(bf16[512,2048]{1,0:T(8,128)(2,1)} %copy-done.19) | copy-start | bytes 6291460
  306.8 10.8 %copy-start.25 = (bf16[512,1024]{1,0:T(8,128)(2,1)S(1)}, bf16[512,1024]{1,0:T(8,128)(2,1)}, u32[]{:S(2)}) copy-start(bf16[512,1024]{1,0:T(8,128)(2,1)} %convolution_convert_fusion.13) | copy-start | bytes 3145732
  311.1 5.2 collective-permute-start.22
  316.3 24.9 %collective-permute-start.23 = (f32[3,1024]{1,0:T(4,128)S(1)}, f32[3,1024]{1,0:T(4,128)S(1)}, u32[]{:S(2)}, u32[]{:S(2)}) collective-permute-start(f32[3,1024]{1,0:T(4,128)S(1)} %add.310), channel_id=1, source_target_pairs={{0,8},{4,12},{8,0},{12,4},{16,24},{20,28},{24,16},{28,20},{1,9},{5... | collective-permute-start | bytes 36872 | tf_op jit(solution)/shard_map/ppermute | solution.py:201
  329.6 11.6 %copy-start.29 = (bf16[512,1024]{1,0:T(8,128)(2,1)S(1)}, bf16[512,1024]{1,0:T(8,128)(2,1)}, u32[]{:S(2)}) copy-start(bf16[512,1024]{1,0:T(8,128)(2,1)} %copy-done.27) | copy-start | bytes 3145732
  341.1 3.2 copy-start.12
  341.1 3.2 copy-start.30
  343.7 4.3 copy-start.14
  343.7 37.7 %collective-permute-start.15 = (bf16[256,1024]{1,0:T(8,128)(2,1)S(1)}, bf16[256,1024]{1,0:T(8,128)(2,1)S(1)}, u32[]{:S(2)}, u32[]{:S(2)}) collective-permute-start(bf16[256,1024]{1,0:T(8,128)(2,1)S(1)} %slice.321), channel_id=1, source_target_pairs={{0,4},{4,0},{8,12},{12,8},{16,20},{20,16},{24,28},{28,24},{1,5},{5... | collective-permute-start | bytes 1572872 | tf_op jit(solution)/shard_map/ppermute | solution.py:201
  346.3 4.3 copy-start.26
  346.3 4.3 copy-start.35
  346.4 88.1 %collective-permute-start.14 = (bf16[256,1024]{1,0:T(8,128)(2,1)S(1)}, bf16[256,1024]{1,0:T(8,128)(2,1)S(1)}, u32[]{:S(2)}, u32[]{:S(2)}) collective-permute-start(bf16[256,1024]{1,0:T(8,128)(2,1)S(1)} %slice.318), channel_id=1, source_target_pairs={{0,4},{4,0},{8,12},{12,8},{16,20},{20,16},{24,28},{28,24},{1,5},{5... | collective-permute-start | bytes 1572872 | tf_op jit(solution)/shard_map/ppermute | solution.py:201
  349.9 86.4 %collective-permute-start.12 = (bf16[512,1024]{1,0:T(8,128)(2,1)S(1)}, bf16[512,1024]{1,0:T(8,128)(2,1)S(1)}, u32[]{:S(2)}, u32[]{:S(2)}) collective-permute-start(bf16[512,1024]{1,0:T(8,128)(2,1)S(1)} %add_convert_fusion.4), channel_id=1, source_target_pairs={{0,1},{1,0},{2,3},{3,2},{4,5},{5,4},{6,7},{7,6},{8,9},{9,8},{10,11... | collective-permute-start | bytes 3145736 | tf_op jit(solution)/shard_map/ppermute | solution.py:197
  352.6 4.4 copy-start.21
  352.6 85.7 %collective-permute-start.3 = (bf16[512,1024]{1,0:T(8,128)(2,1)S(1)}, bf16[512,1024]{1,0:T(8,128)(2,1)S(1)}, u32[]{:S(2)}, u32[]{:S(2)}) collective-permute-start(bf16[512,1024]{1,0:T(8,128)(2,1)S(1)} %add_convert_fusion.9), channel_id=1, source_target_pairs={{0,1},{1,0},{2,3},{3,2},{4,5},{5,4},{6,7},{7,6},{8,9},{9,8},{10,11... | collective-permute-start | bytes 3145736 | tf_op jit(solution)/shard_map/ppermute | solution.py:197
  356.1 80.3 %copy-start.5 = (f32[512,1024]{1,0:T(8,128)S(1)}, f32[512,1024]{1,0:T(8,128)}, u32[]{:S(2)}) copy-start(f32[512,1024]{1,0:T(8,128)} %fusion.98) | copy-start | bytes 6291460
  356.1 77.8 %collective-permute-start.6 = (bf16[256,1024]{1,0:T(8,128)(2,1)S(1)}, bf16[256,1024]{1,0:T(8,128)(2,1)S(1)}, u32[]{:S(2)}, u32[]{:S(2)}) collective-permute-start(bf16[256,1024]{1,0:T(8,128)(2,1)S(1)} %slice.305), channel_id=1, source_target_pairs={{0,4},{4,0},{8,12},{12,8},{16,20},{20,16},{24,28},{28,24},{1,5},{5... | collective-permute-start | bytes 1572872 | tf_op jit(solution)/shard_map/ppermute | solution.py:201
  381.4 63.7 %collective-permute-start.5 = (bf16[256,1024]{1,0:T(8,128)(2,1)S(1)}, bf16[256,1024]{1,0:T(8,128)(2,1)S(1)}, u32[]{:S(2)}, u32[]{:S(2)}) collective-permute-start(bf16[256,1024]{1,0:T(8,128)(2,1)S(1)} %slice.301), channel_id=1, source_target_pairs={{0,4},{4,0},{8,12},{12,8},{16,20},{20,16},{24,28},{28,24},{1,5},{5... | collective-permute-start | bytes 1572872 | tf_op jit(solution)/shard_map/ppermute | solution.py:201
  433.8 24.8 %collective-permute-start.16 = (bf16[256,1024]{1,0:T(8,128)(2,1)S(1)}, bf16[256,1024]{1,0:T(8,128)(2,1)S(1)}, u32[]{:S(2)}, u32[]{:S(2)}) collective-permute-start(bf16[256,1024]{1,0:T(8,128)(2,1)S(1)} %add_convert_fusion.14), channel_id=1, source_target_pairs={{0,1},{1,0},{2,3},{3,2},{4,5},{5,4},{6,7},{7,6},{8,9},{9,8},{10,11... | collective-permute-start | bytes 1572872 | tf_op jit(solution)/shard_map/ppermute | solution.py:197
  434.5 23.8 %collective-permute-start.7 = (bf16[256,1024]{1,0:T(8,128)(2,1)S(1)}, bf16[256,1024]{1,0:T(8,128)(2,1)S(1)}, u32[]{:S(2)}, u32[]{:S(2)}) collective-permute-start(bf16[256,1024]{1,0:T(8,128)(2,1)S(1)} %add_convert_fusion.18), channel_id=1, source_target_pairs={{0,1},{1,0},{2,3},{3,2},{4,5},{5,4},{6,7},{7,6},{8,9},{9,8},{10,11... | collective-permute-start | bytes 1572872 | tf_op jit(solution)/shard_map/ppermute | solution.py:197
  438.2 20.4 %collective-permute-start.13 = (bf16[256,1024]{1,0:T(8,128)(2,1)S(1)}, bf16[256,1024]{1,0:T(8,128)(2,1)S(1)}, u32[]{:S(2)}, u32[]{:S(2)}) collective-permute-start(bf16[256,1024]{1,0:T(8,128)(2,1)S(1)} %get-tuple-element.62), channel_id=1, source_target_pairs={{0,4},{4,0},{8,12},{12,8},{16,20},{20,16},{24,28},{28,24},{1,5},{5... | collective-permute-start | bytes 1572872 | tf_op jit(solution)/shard_map/ppermute | solution.py:201
  440.1 27.1 %collective-permute-start.4 = (bf16[256,1024]{1,0:T(8,128)(2,1)S(1)}, bf16[256,1024]{1,0:T(8,128)(2,1)S(1)}, u32[]{:S(2)}, u32[]{:S(2)}) collective-permute-start(bf16[256,1024]{1,0:T(8,128)(2,1)S(1)} %slice.297), channel_id=1, source_target_pairs={{0,4},{4,0},{8,12},{12,8},{16,20},{20,16},{24,28},{28,24},{1,5},{5... | collective-permute-start | bytes 1572872 | tf_op jit(solution)/shard_map/ppermute | solution.py:201
  459.1 36.4 %collective-permute-start.17 = (bf16[128,2048]{1,0:T(8,128)(2,1)S(1)}, bf16[128,2048]{1,0:T(8,128)(2,1)S(1)}, u32[]{:S(2)}, u32[]{:S(2)}) collective-permute-start(bf16[128,2048]{1,0:T(8,128)(2,1)S(1)} %pad_maximum_fusion), channel_id=1, source_target_pairs={{0,16},{4,20},{8,24},{12,28},{16,0},{20,4},{24,8},{28,12},{1,17},{... | collective-permute-start | bytes 1572872 | tf_op jit(solution)/shard_map/ppermute | solution.py:201
  467.4 38.8 %collective-permute-start.8 = (bf16[128,2048]{1,0:T(8,128)(2,1)S(1)}, bf16[128,2048]{1,0:T(8,128)(2,1)S(1)}, u32[]{:S(2)}, u32[]{:S(2)}) collective-permute-start(bf16[128,2048]{1,0:T(8,128)(2,1)S(1)} %pad_maximum_fusion.1), channel_id=1, source_target_pairs={{0,16},{4,20},{8,24},{12,28},{16,0},{20,4},{24,8},{28,12},{1,17},{... | collective-permute-start | bytes 1572872 | tf_op jit(solution)/shard_map/ppermute | solution.py:201
  468.8 51.2 %copy-start.1 = (s32[2,4096]{1,0:T(2,128)S(1)}, s32[2,4096]{1,0:T(2,128)}, u32[]{:S(2)}) copy-start(s32[2,4096]{1,0:T(2,128)} %param.17) | copy-start | bytes 98308
  495.6 16.3 %collective-permute-start.18 = (bf16[64,2048]{1,0:T(8,128)(2,1)S(1)}, bf16[64,2048]{1,0:T(8,128)(2,1)S(1)}, u32[]{:S(2)}, u32[]{:S(2)}) collective-permute-start(bf16[64,2048]{1,0:T(8,128)(2,1)S(1)} %slice.325), channel_id=1, source_target_pairs={{0,8},{4,12},{8,0},{12,4},{16,24},{20,28},{24,16},{28,20},{1,9},{5... | collective-permute-start | bytes 786440 | tf_op jit(solution)/shard_map/ppermute | solution.py:201
  506.4 11.0 %collective-permute-start.9 = (bf16[64,2048]{1,0:T(8,128)(2,1)S(1)}, bf16[64,2048]{1,0:T(8,128)(2,1)S(1)}, u32[]{:S(2)}, u32[]{:S(2)}) collective-permute-start(bf16[64,2048]{1,0:T(8,128)(2,1)S(1)} %slice.309), channel_id=1, source_target_pairs={{0,8},{4,12},{8,0},{12,4},{16,24},{20,28},{24,16},{28,20},{1,9},{5... | collective-permute-start | bytes 786440 | tf_op jit(solution)/shard_map/ppermute | solution.py:201
  (9 other events, 15.9 us)
Sparse Core Ops, SparseCore 0:
  11.5 119.5 all-gather.2
  133.9 75.2 all-gather.4
  306.9 120.7 reduce-scatter.1
